TPU v7x, 32 devices: a whole 2x2x4 slice. The times are simulated.
32 devices in a mesh: dp: 2 (over y), expert: 16 (over z, x, core).
Axes of the slice: x: 2, y: 2, z: 4, core: 2. Of those that a mesh axis runs over, the one named last changes fastest.
Arguments:
- tokens: bfloat16 [2048, 2048], P('expert', 'dp'), may hold values from -6 to 6
- cotangent: bfloat16 [2048, 2048], P('expert', 'dp'), may hold values from -6 to 6
- routes: int32 [2048, 8], P('expert'), may hold values from 0 to 15, all different within a row; in each aligned block of 128 rows (0 to 127, 128 to 255, ...) at most 72 rows name the same one
- gate_probs: float32 [2048, 8], P('expert'), may hold values from 0.02 to 1
- matching: int32 [16], replicated, may hold values from 0 to 15, as said below
- gate_weight: bfloat16 [16, 2048, 768], P('expert', None, 'dp'), may hold values from -0.125 to 0.125
- up_weight: bfloat16 [16, 2048, 768], P('expert', None, 'dp'), may hold values from -0.125 to 0.125
- down_weight: bfloat16 [16, 768, 2048], P('expert', 'dp'), may hold values from -0.21875 to 0.21875
Outputs:
- layer_out: bfloat16 [2048, 2048], P('expert', 'dp')
- gate_grad: bfloat16 [16, 2048, 768], P('expert', None, 'dp')
- up_grad: bfloat16 [16, 2048, 768], P('expert', None, 'dp')
- down_grad: bfloat16 [16, 768, 2048], P('expert', 'dp')
Inputs may be any that keep to these rules, and one draw needn't show every extreme that they name: `routes`: each row names 8 different experts. Within each aligned block of 128 rows no expert is named by more than 72 rows, and in some block some expert is named by exactly 72 rows. The weights of expert e sit in slot matching[e]; matching pairs the slots: matching[matching[e]] = e and matching[e] != e.
All inputs are finite; a program needn't handle non-finite values.
Results may differ from a plain program's by a relative error of at most 0.0065.
Values may be sent and summed in bfloat16 or wider, within the bound.
No kernel may reach another device: no remote copies, remote signals or barrier semaphores. Data moves between devices by JAX's collectives and lax.ppermute only.
A program may use at most 128 MiB of HBM per device.

v0:
```python
import jax
import jax.numpy as jnp
from jax import lax
from jax.sharding import PartitionSpec as P


def on_device(tokens, cotangent, routes, gate_probs, matching, gate_weight, up_weight, down_weight):
    expert_count = lax.axis_size("expert")
    token_count, fan_out = routes.shape
    capacity = max(2, token_count * fan_out * 9 // (8 * expert_count))
    route_count = token_count * fan_out
    mix_weights = gate_probs / jnp.sum(gate_probs, axis=1, keepdims=True)
    flat_routes = routes.reshape(-1)
    expert_hit = flat_routes[:, None] == jnp.arange(matching.shape[0], dtype=jnp.int32)[None, :]
    host_of = jnp.sum(jnp.where(expert_hit, matching[None, :], 0), axis=1)
    host_hit = (host_of[:, None] == jnp.arange(expert_count, dtype=jnp.int32)[None, :]).astype(
        jnp.int32
    )
    running = jnp.cumsum(host_hit, axis=0)
    slot_rank = jnp.sum((running - 1) * host_hit, axis=1)
    position = host_of * capacity + slot_rank
    slot_table = (
        jnp.full((expert_count * capacity,), route_count, jnp.int32)
        .at[position]
        .set(jnp.arange(route_count, dtype=jnp.int32))
    )
    filled = slot_table < route_count
    route_ids = jnp.minimum(slot_table, route_count - 1)
    token_ids = jnp.where(filled, route_ids // fan_out, token_count)
    clamped_ids = route_ids // fan_out
    slot_mix = jnp.where(filled, jnp.take(mix_weights.reshape(-1), route_ids), 0.0)
    recv_rows = lax.all_to_all(
        jnp.take(tokens, token_ids, axis=0, mode="fill", fill_value=0),
        "expert",
        split_axis=0,
        concat_axis=0,
        tiled=True,
    )
    gathered = jnp.take(cotangent, clamped_ids, axis=0)
    recv_cot = lax.all_to_all(
        (slot_mix[:, None] * gathered.astype(jnp.float32)).astype(jnp.bfloat16),
        "expert",
        split_axis=0,
        concat_axis=0,
        tiled=True,
    )
    inputs, out_cot = (
        lax.all_gather(recv_rows, "dp", axis=1, tiled=True),
        lax.all_gather(recv_cot, "dp", axis=1, tiled=True),
    )
    gate_pre = jnp.dot(inputs, gate_weight[0], preferred_element_type=jnp.float32)
    up_pre = jnp.dot(inputs, up_weight[0], preferred_element_type=jnp.float32)
    sigma_gate = jax.nn.sigmoid(gate_pre)
    silu_gate = gate_pre * sigma_gate
    hidden = (silu_gate * up_pre).astype(jnp.bfloat16)
    partial_out = jnp.dot(hidden, down_weight[0], preferred_element_type=jnp.float32)
    contract_rows = (((0,), (0,)), ((), ()))
    down_grad = lax.dot_general(
        hidden, out_cot, contract_rows, preferred_element_type=jnp.float32
    ).astype(jnp.bfloat16)
    hidden_cot = lax.dot_general(
        out_cot, down_weight[0], (((1,), (1,)), ((), ())), preferred_element_type=jnp.float32
    )
    slope = sigma_gate * (1.0 + gate_pre * (1.0 - sigma_gate))
    gate_cot = (hidden_cot * up_pre * slope).astype(jnp.bfloat16)
    up_cot = (hidden_cot * silu_gate).astype(jnp.bfloat16)
    gate_grad = lax.dot_general(
        inputs, gate_cot, contract_rows, preferred_element_type=jnp.float32
    ).astype(jnp.bfloat16)
    up_grad = lax.dot_general(
        inputs, up_cot, contract_rows, preferred_element_type=jnp.float32
    ).astype(jnp.bfloat16)
    summed = lax.psum_scatter(
        partial_out.astype(jnp.bfloat16), "dp", scatter_dimension=1, tiled=True
    )
    merged = lax.all_to_all(summed, "expert", split_axis=0, concat_axis=0, tiled=True)
    half_width = merged.shape[1]
    expert_out = jnp.take(merged, position, axis=0).reshape(token_count, fan_out, half_width)
    layer_out = jnp.sum(mix_weights[:, :, None] * expert_out.astype(jnp.float32), axis=1).astype(
        jnp.bfloat16
    )
    return (layer_out, gate_grad[None], up_grad[None], down_grad[None])


def solution(mesh):
    placed = (
        P("expert", "dp"),
        P("expert", "dp"),
        P("expert", None),
        P("expert", None),
        P(),
        P("expert", None, "dp"),
        P("expert", None, "dp"),
        P("expert", "dp", None),
    )
    return jax.shard_map(
        on_device,
        mesh=mesh,
        in_specs=placed,
        out_specs=(
            P("expert", "dp"),
            P("expert", None, "dp"),
            P("expert", None, "dp"),
            P("expert", "dp", None),
        ),
        check_vma=False,
    )
```

profile of v0, /device:TPU:0, one launch (start us, length us, event | category | flops | bytes accessed | tf_op | source)
XLA Modules:
  0.0 332.1 jit_solution(8756342723979164747)
XLA Ops:
  7.2 0.0 copy-start
  7.2 0.0 all-gather.3.cloned.1.call-start
  7.2 0.9 copy.16
  8.1 0.1 eq.38
  8.2 0.7 select_reduce_fusion
  9.0 4.5 %reduce-window.6 = s32[16,8,128]{2,1,0:T(8,128)S(1)} reduce-window(s32[16,8,128]{2,1,0:T(8,128)S(1)} %fusion.15, s32[]{:T(128)} %constant.77.clone.1), window={size=1x1x128 pad=0_0x0_0x127_0}, to_apply=%region_2.3 | reduce-window | flops 2080768 | bytes 131076 | tf_op jit(solution)/shard_map/reduce-window
  13.5 0.1 slice.16
  13.6 0.1 copy.17
  13.7 0.1 copy.18
  13.8 0.1 add_add_fusion
  14.0 4.3 %scatter_custom_fusion = s32[1152]{0:T(1024)S(1)} fusion(s32[1024]{0:T(1024)S(1)} %bitcast.63, s32[1024]{0:T(1024)S(1)} %iota.12, s32[]{:T(128)} %constant.82.clone.1), kind=kCustom, calls=%fused_computation.58 | custom fusion | bytes 4612 | tf_op jit(solution)/shard_map/scatter | solution.py:25
  18.3 0.7 reduce_sum.36
  19.0 0.7 broadcast_divide_fusion
  19.7 0.1 copy.15
  19.8 0.1 reshape.116
  19.9 0.0 copy-start.1
  19.9 4.6 %gather_fusion.2 = f32[1152]{0:T(1024)S(1)} fusion(f32[1024]{0:T(1024)S(1)} %reshape.116, s32[2048]{0:T(1024)S(1)} %pad_clamp_fusion.1), kind=kCustom, calls=%fused_computation.2 | custom fusion | bytes 13824 | tf_op jit(solution)/shard_map/jit(_take)/gather | solution.py:31
  24.6 0.1 broadcast_in_dim.87
  24.7 5.0 %gather_fusion = bf16[1152,1024]{1,0:T(8,128)(2,1)} fusion(bf16[128,1024]{1,0:T(8,128)(2,1)S(1)} %copy-done.1, s32[2048]{0:T(1024)S(1)} %pad_clamp_fusion.2), kind=kCustom, calls=%fused_computation | custom fusion | bytes 4723200 | tf_op jit(solution)/shard_map/jit(_take)/gather | solution.py:33
  29.7 1.9 broadcast_select_fusion
  31.6 61.1 %all_to_all.30 = bf16[16,72,1024]{2,1,0:T(8,128)(2,1)} all-to-all(bf16[16,72,1024]{2,1,0:T(8,128)(2,1)S(1)} %broadcast_select_fusion), channel_id=1, replica_groups=mesh['dp'=2,'expert'=16] {'expert'}, dimensions={0} | all-to-all | bytes 4718592 | tf_op jit(solution)/shard_map/all_to_all | solution.py:32
  92.7 0.0 all-gather.3.cloned.1.call-update
  92.7 0.0 reduce-scatter.2.cloned.1.call-start
  92.8 62.2 %all-gather.3.cloned.1.call-done = bf16[1152,2048]{1,0:T(8,128)(2,1)} async-done(((bf16[1152,1024]{1,0:T(8,128)(2,1)}), bf16[1152,2048]{1,0:T(8,128)(2,1)}) %all-gather.3.cloned.1.call-update) | async-done | bytes 4718608 | tf_op jit(solution)/shard_map/all_gather | solution.py:48
  155.0 0.0 copy-done.5
  155.0 4.8 %fusion.9 = f32[1152,384]{1,0:T(8,128)S(1)} fusion(bf16[1152,2048]{1,0:T(8,128)(2,1)} %all-gather.3.cloned.1.call-done, bf16[1,2048,384]{2,1,0:T(8,128)(2,1)S(1)} %copy-done.5), kind=kOutput, calls=%fused_computation.26 | convolution fusion | flops 1811939328 | bytes 8060928 | tf_op jit(solution)/shard_map/dot_general | solution.py:51
  159.8 4.0 %multiply_convert_fusion.3 = (bf16[1152,384]{1,0:T(8,128)(2,1)S(1)}, f32[1152,384]{1,0:T(8,128)}) fusion(f32[1152,384]{1,0:T(8,128)S(1)} %fusion.9, bf16[1152,2048]{1,0:T(8,128)(2,1)S(1)} %copy-done.3, bf16[1,2048,384]{2,1,0:T(8,128)(2,1)S(1)} %copy-done.6), kind=kOutput, calls=%fused_computation.18 | convolution fusion | flops 1814593536 | bytes 10715136 | tf_op jit(solution)/shard_map/dot_general | solution.py:52
  163.8 4.3 %convolution_convert_fusion = bf16[1152,2048]{1,0:T(8,128)(2,1)} fusion(bf16[1152,384]{1,0:T(8,128)(2,1)S(1)} %get-tuple-element.12, bf16[1,384,2048]{2,1,0:T(8,128)(2,1)S(1)} %copy-done), kind=kOutput, calls=%fused_computation.5 | convolution fusion | flops 1814298624 | bytes 7176192 | tf_op jit(solution)/shard_map/dot_general | solution.py:56
  168.1 0.0 reduce-scatter.2.cloned.1.call-update
  168.1 0.0 all-gather.5.cloned.1.call-start
  168.1 0.1 broadcast_in_dim.95
  168.2 0.1 mul.68
  168.3 0.7 copy-done.2
  169.0 5.0 %gather_fusion.3 = bf16[1152,1024]{1,0:T(8,128)(2,1)} fusion(bf16[128,1024]{1,0:T(8,128)(2,1)S(1)} %copy-done.2, s32[2048]{0:T(1024)S(1)} %pad_clamp_fusion), kind=kCustom, calls=%fused_computation.3 | custom fusion | bytes 4723200 | tf_op jit(solution)/shard_map/jit(_take)/gather | solution.py:39
  174.0 2.4 multiply_convert_fusion
  176.4 59.5 %all_to_all.31 = bf16[16,72,1024]{2,1,0:T(8,128)(2,1)} all-to-all(bf16[16,72,1024]{2,1,0:T(8,128)(2,1)S(1)} %multiply_convert_fusion), channel_id=1, replica_groups=mesh['dp'=2,'expert'=16] {'expert'}, dimensions={0} | all-to-all | bytes 4718592 | tf_op jit(solution)/shard_map/all_to_all | solution.py:40
  235.9 0.0 all-gather.5.cloned.1.call-update
  235.9 0.0 reduce-scatter.2.cloned.1.call-done
  235.9 4.6 %all-to-all-start.1 = ((bf16[16,72,1024]{2,1,0:T(8,128)(2,1)}), bf16[16,72,1024]{2,1,0:T(8,128)(2,1)}, u32[]{:S(2)}, u32[]{:S(2)}) async-start(bf16[16,72,1024]{2,1,0:T(8,128)(2,1)} %bitcast.58), calls=%async_computation.2 | async-start | bytes 4718592 | tf_op jit(solution)/shard_map/all_to_all | solution.py:76
  240.6 0.1 add.74
  240.7 56.5 %all-gather.5.cloned.1.call-done = bf16[1152,2048]{1,0:T(8,128)(2,1)} async-done(((bf16[1152,1024]{1,0:T(8,128)(2,1)}), bf16[1152,2048]{1,0:T(8,128)(2,1)}) %all-gather.5.cloned.1.call-update) | async-done | bytes 4718608 | tf_op jit(solution)/shard_map/all_gather | solution.py:49
  297.2 5.9 %fusion.2 = bf16[1,384,2048]{2,1,0:T(8,128)(2,1)} fusion(bf16[1152,384]{1,0:T(8,128)(2,1)S(1)} %get-tuple-element.12, bf16[1152,2048]{1,0:T(8,128)(2,1)} %all-gather.5.cloned.1.call-done), kind=kOutput, calls=%fused_computation.13 | convolution fusion | flops 1812725760 | bytes 7176192 | tf_op jit(solution)/shard_map/dot_general | solution.py:58
  303.1 2.6 fusion.4
  305.8 4.0 %fusion.1 = bf16[1,2048,384]{2,1,0:T(8,128)(2,1)} fusion(bf16[1152,2048]{1,0:T(8,128)(2,1)S(1)} %bitcast.66, f32[1152,384]{1,0:T(8,128)S(1)} %fusion.4, f32[1152,384]{1,0:T(8,128)S(1)} %copy-done.8), kind=kOutput, calls=%fused_computation.12 | convolution fusion | flops 1815379968 | bytes 9830400 | tf_op jit(solution)/shard_map/dot_general | solution.py:70
  309.8 4.1 %fusion = bf16[1,2048,384]{2,1,0:T(8,128)(2,1)} fusion(bf16[1152,2048]{1,0:T(8,128)(2,1)S(1)} %bitcast.66, f32[1152,384]{1,0:T(8,128)S(1)} %copy-done.8, f32[1152,384]{1,0:T(8,128)S(1)} %fusion.4, f32[1152,384]{1,0:T(8,128)S(1)} %copy-done.9), kind=kOutput, calls=%fused_computation.11 | convolution fusion | flops 1817149440 | bytes 11599872 | tf_op jit(solution)/shard_map/dot_general | solution.py:67
  313.8 0.0 all-to-all-done.1
  313.8 8.0 %gather_fusion.1 = bf16[1024,1024]{1,0:T(8,128)(2,1)} fusion(bf16[1152,1024]{1,0:T(8,128)(2,1)} %bitcast.11, s32[1024]{0:T(1024)S(1)} %broadcast_clamp_fusion), kind=kCustom, calls=%fused_computation.1 | custom fusion | bytes 4198400 | tf_op jit(solution)/shard_map/jit(_take)/gather | solution.py:78
  321.8 3.8 %multiply_reduce_fusion = bf16[128,1024]{1,0:T(8,128)(2,1)} fusion(bf16[1024,1024]{1,0:T(8,128)(2,1)} %gather_fusion.1, f32[128,8]{1,0:T(8,128)S(1)} %copy.15, pred[128,8]{1,0:T(8,128)(4,1)S(1)} %compare_and_fusion), kind=kLoop, calls=%fused_computation.7 | loop fusion | flops 4063232 | bytes 2364416 | tf_op jit(solution)/shard_map/reduce_sum | solution.py:79
  (36 shorter events, 0.2 us)
Async XLA Ops:
  7.2 156.6 %copy-start = (bf16[1,384,2048]{2,1,0:T(8,128)(2,1)S(1)}, bf16[1,384,2048]{2,1,0:T(8,128)(2,1)}, u32[]{:S(2)}) copy-start(bf16[1,384,2048]{2,1,0:T(8,128)(2,1)} %param.15) | copy-start | bytes 4718596
  7.2 147.8 %all-gather.3.cloned.1.call-start = ((), (), s32[]{:S(2)}) async-start(), calls=%async_computation.4 | async-start | bytes 7077888 | tf_op jit(solution)/shard_map/all_gather | solution.py:48
  19.9 4.7 %copy-start.1 = (bf16[128,1024]{1,0:T(8,128)(2,1)S(1)}, bf16[128,1024]{1,0:T(8,128)(2,1)}, u32[]{:S(2)}) copy-start(bf16[128,1024]{1,0:T(8,128)(2,1)} %param.8) | copy-start | bytes 786436
  92.7 62.3 %copy-start.5 = (bf16[1,2048,384]{2,1,0:T(8,128)(2,1)S(1)}, bf16[1,2048,384]{2,1,0:T(8,128)(2,1)}, u32[]{:S(2)}) copy-start(bf16[1,2048,384]{2,1,0:T(8,128)(2,1)} %param.13) | copy-start | bytes 4718596
  92.7 143.2 %reduce-scatter.2.cloned.1.call-start = ((), (), s32[]{:S(2)}) async-start(), calls=%async_computation.5 | async-start | bytes 7077888 | tf_op jit(solution)/shard_map/reduce_scatter | solution.py:73
  155.0 4.8 %copy-start.3 = (bf16[1152,2048]{1,0:T(8,128)(2,1)S(1)}, bf16[1152,2048]{1,0:T(8,128)(2,1)}, u32[]{:S(2)}) copy-start(bf16[1152,2048]{1,0:T(8,128)(2,1)} %all-gather.3.cloned.1.call-done) | copy-start | bytes 14155780
  155.0 4.8 %copy-start.6 = (bf16[1,2048,384]{2,1,0:T(8,128)(2,1)S(1)}, bf16[1,2048,384]{2,1,0:T(8,128)(2,1)}, u32[]{:S(2)}) copy-start(bf16[1,2048,384]{2,1,0:T(8,128)(2,1)} %param.14) | copy-start | bytes 4718596
  159.8 4.0 %copy-start.7 = (f32[1152,384]{1,0:T(8,128)}, f32[1152,384]{1,0:T(8,128)S(1)}, u32[]{:S(2)}) copy-start(f32[1152,384]{1,0:T(8,128)S(1)} %fusion.9) | copy-start | bytes 5308420
  168.1 0.9 copy-start.2
  168.1 129.1 %all-gather.5.cloned.1.call-start = ((), (), s32[]{:S(2)}) async-start(), calls=%async_computation.6 | async-start | bytes 7077888 | tf_op jit(solution)/shard_map/all_gather | solution.py:49
  235.9 77.9 %all-to-all-start.1 = ((bf16[16,72,1024]{2,1,0:T(8,128)(2,1)}), bf16[16,72,1024]{2,1,0:T(8,128)(2,1)}, u32[]{:S(2)}, u32[]{:S(2)}) async-start(bf16[16,72,1024]{2,1,0:T(8,128)(2,1)} %bitcast.58), calls=%async_computation.2 | async-start | bytes 4718592 | tf_op jit(solution)/shard_map/all_to_all | solution.py:76
  297.2 5.9 %copy-start.4 = (bf16[1152,2048]{1,0:T(8,128)(2,1)S(1)}, bf16[1152,2048]{1,0:T(8,128)(2,1)}, u32[]{:S(2)}) copy-start(bf16[1152,2048]{1,0:T(8,128)(2,1)} %all-gather.5.cloned.1.call-done) | copy-start | bytes 14155780
  297.2 8.5 %slice-start = ((s8[4718592]{0:T(1024)(128)(4,1)}), s8[4194304]{0:T(1024)(128)(4,1)S(1)}, s32[]{:S(2)}) async-start(s8[4718592]{0:T(1024)(128)(4,1)} %bitcast.65), calls=%async_computation.7 | async-start | bytes 8388608
  303.1 2.7 slice-start.1
  303.1 2.7 copy-start.8
  305.8 4.0 %copy-start.9 = (f32[1152,384]{1,0:T(8,128)S(1)}, f32[1152,384]{1,0:T(8,128)}, u32[]{:S(2)}) copy-start(f32[1152,384]{1,0:T(8,128)} %get-tuple-element.13) | copy-start | bytes 5308420
Sparse Core Ops, SparseCore 0:
  92.8 62.0 all-gather.2
  168.2 60.0 reduce-scatter.1
  236.0 61.1 all-gather.4
where the time goes:
time: 333 us; the launch traced here: 332 us
  blocking collectives  121 us (36%)
  waiting for transfers between devices  119 us (36%)
  matrix products  29.6 us (9%)
  local copies, waits for them, and re-layouts  29.3 us (9%)
  other arithmetic  15 us (5%)
  between operations  14 us (4%)
  starting transfers between devices  4.76 us (1%)
    all_gather x1, waiting for transfers between devices, on_device(): lax.all_gather(recv_rows, 'dp', axis=1, tiled=True)  62.2 us
    all_to_all x1, blocking collectives, on_device(): lax.all_to_all(jnp.take(tokens, token_ids, axis=0, mode='fill', fill_valu...  61.1 us
    all_to_all x1, blocking collectives, on_device(): lax.all_to_all((slot_mix[:, None] * gathered.astype(jnp.float32)).astype(...  59.5 us
    all_gather x1, waiting for transfers between devices, on_device(): lax.all_gather(recv_cot, 'dp', axis=1, tiled=True)  56.5 us
    gather x1, local copies, waits for them, and re-layouts, on_device(): jnp.take(merged, position, axis=0).reshape(token_count, fan_out, half_width)  7.96 us
  transfers between devices with their start and end apart: 4, of which 2 were waited for; matrix products, arithmetic and copies ran while one was open for 7% of the time, Pallas kernels for 0%

commit v1 on v0

--- a/solution.py
+++ b/solution.py
@@ -1,10 +1,21 @@
+import functools
+
 import jax
 import jax.numpy as jnp
 from jax import lax
+from jax.experimental import pallas as pl
+from jax.experimental.pallas import tpu as pltpu
 from jax.sharding import PartitionSpec as P
 
 
-def on_device(tokens, cotangent, routes, gate_probs, matching, gate_weight, up_weight, down_weight):
+AXES = ("dp", "expert")
+CORES = 2
+SIDE = 2
+F32 = jnp.float32
+BF16 = jnp.bfloat16
+
+
+def exchange_plan(tokens, cotangent, routes, gate_probs, matching, gate_weight, up_weight, down_weight):
     expert_count = lax.axis_size("expert")
     token_count, fan_out = routes.shape
     capacity = max(2, token_count * fan_out * 9 // (8 * expert_count))
@@ -82,7 +93,324 @@
     return (layer_out, gate_grad[None], up_grad[None], down_grad[None])
 
 
+def moves(expert_count):
+    depth = expert_count // (SIDE * CORES)
+
+    def table(step):
+        pairs = []
+        for y in range(2):
+            for z in range(depth):
+                for x in range(SIDE):
+                    for core in range(CORES):
+                        ty, tz, tx, tcore = step(y, z, x, core)
+                        pairs.append(
+                            (
+                                y * expert_count + (z * SIDE + x) * CORES + core,
+                                ty * expert_count + (tz * SIDE + tx) * CORES + tcore,
+                            )
+                        )
+        return pairs
+
+    shift = {
+        by: table(lambda y, z, x, core, by=by: (y, (z + by) % depth, x, core))
+        for by in range(1 - depth, depth)
+        if by
+    }
+    swap = table(lambda y, z, x, core: (y, z, x, 1 - core))
+    first = table(lambda y, z, x, core: (y, z, 1 - x, core) if core == 0 else (1 - y, z, x, core))
+    second = table(lambda y, z, x, core: (1 - y, z, x, core) if core == 0 else (y, z, 1 - x, core))
+    return depth, shift, swap, first, second
+
+
+def dot(a, b):
+    return jnp.dot(a, b, preferred_element_type=F32)
+
+
+def dot_rows(a, b):
+    return lax.dot_general(a, b, (((0,), (0,)), ((), ())), preferred_element_type=F32)
+
+
+def dot_columns(a, b):
+    return lax.dot_general(a, b, (((1,), (1,)), ((), ())), preferred_element_type=F32)
+
+
+def piece_windows(where_ref, rows, half):
+    y, core = where_ref[0], where_ref[3]
+
+    def window(lower, other):
+        side = jnp.where(other == 1, 1 - y, y)
+        return (
+            pl.ds(pl.multiple_of(lower * rows, rows), rows),
+            pl.ds(pl.multiple_of(side * half, half), half),
+        )
+
+    return window(0, 0), window(1 - core, core), window(core, 1 - core), window(1, 1)
+
+
+def row_weights(mix_ref, where_ref, back, depth, slot):
+    core = where_ref[3]
+    z, x = lax.rem(where_ref[1] + depth - back, depth), where_ref[2]
+    parity = core if slot == 0 else 1 - core
+    lanes = lax.broadcasted_iota(jnp.int32, mix_ref.shape, 1)
+    columns = []
+    for across in (x, 1 - x):
+        block = (z * SIDE + across) * CORES + core
+        hit = lanes == block * CORES + parity
+        columns.append(jnp.sum(jnp.where(hit, mix_ref[...], 0.0), axis=1, keepdims=True))
+    return jnp.concatenate(columns, axis=0)
+
+
+def forward_kernel(back, depth, fresh, where_ref, *refs):
+    pieces, refs = refs[:4], refs[4:]
+    mix_ref, ins, downs, refs = refs[0], refs[1:3], refs[3:5], refs[5 if fresh else 6 :]
+    outs, pre_ref, all_ref, x_buf, o_buf, sem = refs[:4], refs[4], refs[5], refs[6], refs[7], refs[8]
+    rows, half = pieces[0].shape
+    windows = piece_windows(where_ref, rows, half)
+    for window, piece in zip(windows, pieces):
+        x_buf[window] = piece[...]
+    keep = pltpu.make_async_copy(x_buf, all_ref.at[pl.ds(2 * rows * back, 2 * rows)], sem)
+    keep.start()
+    width = ins[0].shape[1]
+    units = width // 2
+    for slot in range(CORES):
+        pre = dot(x_buf[...], ins[slot][...])
+        pre_ref[:, slot * width : (slot + 1) * width] = pre
+        gate = pre[:, :units]
+        hidden = (gate * jax.nn.sigmoid(gate) * pre[:, units:]).astype(BF16)
+        out = row_weights(mix_ref, where_ref, back, depth, slot) * dot(hidden, downs[slot][...])
+        if slot == 0:
+            o_buf[...] = out
+        else:
+            o_buf[...] += out
+    for window, ref in zip(windows, outs):
+        ref[...] = o_buf[window].astype(BF16)
+    keep.wait()
+
+
+def forward(back, depth, where, pieces, mix, ins, downs, rows_all):
+    rows, half = pieces[0].shape
+    width = ins[0].shape[1]
+    total = 2 * rows
+    fresh = rows_all is None
+    vmem = pl.BlockSpec(memory_space=pltpu.VMEM)
+    hbm = pl.BlockSpec(memory_space=pl.ANY)
+    return pl.pallas_call(
+        functools.partial(forward_kernel, back, depth, fresh),
+        out_shape=tuple([jax.ShapeDtypeStruct((rows, half), BF16)] * 4)
+        + (
+            jax.ShapeDtypeStruct((total, CORES * width), F32),
+            jax.ShapeDtypeStruct((depth * total, 2 * half), BF16),
+        ),
+        in_specs=[pl.BlockSpec(memory_space=pltpu.SMEM)] + [vmem] * 9 + ([] if fresh else [hbm]),
+        out_specs=(vmem,) * 5 + (hbm,),
+        input_output_aliases={} if fresh else {10: 5},
+        scratch_shapes=[
+            pltpu.VMEM((total, 2 * half), BF16),
+            pltpu.VMEM((total, 2 * half), F32),
+            pltpu.SemaphoreType.DMA,
+        ],
+        compiler_params=pltpu.CompilerParams(vmem_limit_bytes=14 << 20),
+        cost_estimate=pl.CostEstimate(
+            flops=2 * total * half * width * 6, bytes_accessed=12 * total * half, transcendentals=total * width
+        ),
+    )(where, *pieces, mix, *ins, *downs, *([] if fresh else [rows_all]))
+
+
+def backward_kernel(back, depth, fresh, where_ref, *refs):
+    pair_ref, far_ref, pre_ref, mix_ref = refs[:4]
+    downs, refs = refs[4:6], refs[6 if fresh else 9 :]
+    cot_all, hid_all, pre_all, c_buf, w_buf, h_buf, g_buf, sems = refs
+    rows, half = pair_ref.shape[1:]
+    total = 2 * rows
+    windows = piece_windows(where_ref, rows, half)
+    for window, piece in zip(windows, (pair_ref.at[0], pair_ref.at[1], far_ref.at[0], far_ref.at[1])):
+        c_buf[window] = piece[...]
+    width = pre_ref.shape[1] // 2
+    units = width // 2
+    at = pl.ds(total * back, total)
+    copies = []
+    for slot in range(CORES):
+        weights = row_weights(mix_ref, where_ref, back, depth, slot)
+        cot = (weights * c_buf[...].astype(F32)).astype(BF16)
+        w_buf[slot] = cot
+        hidden_cot = dot_columns(cot, downs[slot][...])
+        gate = pre_ref[:, slot * width : slot * width + units]
+        up = pre_ref[:, slot * width + units : (slot + 1) * width]
+        sigma = jax.nn.sigmoid(gate)
+        silu = gate * sigma
+        h_buf[slot] = (silu * up).astype(BF16)
+        slope = sigma * (1.0 + gate * (1.0 - sigma))
+        g_buf[slot, :, :units] = (hidden_cot * up * slope).astype(BF16)
+        g_buf[slot, :, units:] = (hidden_cot * silu).astype(BF16)
+        for number, (buf, to) in enumerate(((w_buf, cot_all), (h_buf, hid_all), (g_buf, pre_all))):
+            copies.append(pltpu.make_async_copy(buf.at[slot], to.at[slot, at], sems.at[slot, number]))
+            copies[-1].start()
+    for copy in copies:
+        copy.wait()
+
+
+def backward(back, depth, where, pair, far, pre, mix, downs, kept):
+    rows, half = pair.shape[1:]
+    width = pre.shape[1] // 2
+    total = 2 * rows
+    fresh = kept is None
+    vmem = pl.BlockSpec(memory_space=pltpu.VMEM)
+    hbm = pl.BlockSpec(memory_space=pl.ANY)
+    return pl.pallas_call(
+        functools.partial(backward_kernel, back, depth, fresh),
+        out_shape=tuple(
+            jax.ShapeDtypeStruct((CORES, depth * total, columns), BF16)
+            for columns in (2 * half, width // 2, width)
+        ),
+        in_specs=[pl.BlockSpec(memory_space=pltpu.SMEM)] + [vmem] * 6 + ([] if fresh else [hbm] * 3),
+        out_specs=(hbm,) * 3,
+        input_output_aliases={} if fresh else {7: 0, 8: 1, 9: 2},
+        scratch_shapes=[
+            pltpu.VMEM((total, 2 * half), BF16),
+            pltpu.VMEM((CORES, total, 2 * half), BF16),
+            pltpu.VMEM((CORES, total, width // 2), BF16),
+            pltpu.VMEM((CORES, total, width), BF16),
+            pltpu.SemaphoreType.DMA((CORES, 3)),
+        ],
+        compiler_params=pltpu.CompilerParams(vmem_limit_bytes=16 << 20),
+        cost_estimate=pl.CostEstimate(
+            flops=2 * total * half * width * 2, bytes_accessed=20 * total * half, transcendentals=total * width
+        ),
+    )(where, pair, far, pre, mix, *downs, *([] if fresh else kept))
+
+
+def partner_grads_kernel(rows_ref, cot_ref, hid_ref, pre_ref, in_ref, down_ref):
+    in_ref[...] = dot_rows(rows_ref[...], pre_ref[0]).astype(BF16)
+    down_ref[...] = dot_rows(hid_ref[0], cot_ref[0]).astype(BF16)
+
+
+def own_grads_kernel(rows_ref, cot_ref, hid_ref, pre_ref, in_got, down_got, gate_ref, up_ref, down_ref):
+    units = gate_ref.shape[1]
+    grads = dot_rows(rows_ref[...], pre_ref[0]) + in_got[...].astype(F32)
+    gate_ref[...] = grads[:, :units].astype(BF16)
+    up_ref[...] = grads[:, units:].astype(BF16)
+    down_ref[...] = (dot_rows(hid_ref[0], cot_ref[0]) + down_got[...].astype(F32)).astype(BF16)
+
+
+def weight_grads(slot, rows_all, kept, got):
+    cot_all, hid_all, pre_all = kept
+    total, features = rows_all.shape
+    units, width = hid_all.shape[2], pre_all.shape[2]
+    tile = min(256, features)
+    steps = features // tile
+
+    def tall(columns):
+        return pl.BlockSpec((tile, columns), lambda i: (i, 0))
+
+    flat = pl.BlockSpec((units, tile), lambda i: (0, i))
+    in_specs = [
+        pl.BlockSpec((total, tile), lambda i: (0, i)),
+        pl.BlockSpec((1, total, tile), lambda i: (slot, 0, i)),
+        pl.BlockSpec((1, total, units), lambda i: (slot, 0, 0)),
+        pl.BlockSpec((1, total, width), lambda i: (slot, 0, 0)),
+    ]
+    shapes = {
+        "in": jax.ShapeDtypeStruct((features, width), BF16),
+        "half": jax.ShapeDtypeStruct((features, units), BF16),
+        "down": jax.ShapeDtypeStruct((units, features), BF16),
+    }
+    params = dict(
+        grid=(steps,),
+        compiler_params=pltpu.CompilerParams(vmem_limit_bytes=24 << 20),
+        cost_estimate=pl.CostEstimate(
+            flops=2 * total * features * (width + units),
+            bytes_accessed=2 * (2 * total * features + features * width * 3),
+            transcendentals=0,
+        ),
+    )
+    if got is None:
+        return pl.pallas_call(
+            partner_grads_kernel,
+            out_shape=(shapes["in"], shapes["down"]),
+            in_specs=in_specs,
+            out_specs=(tall(width), flat),
+            **params,
+        )(rows_all, cot_all, hid_all, pre_all)
+    return pl.pallas_call(
+        own_grads_kernel,
+        out_shape=(shapes["half"], shapes["half"], shapes["down"]),
+        in_specs=in_specs + [tall(width), flat],
+        out_specs=(tall(units), tall(units), flat),
+        **params,
+    )(rows_all, cot_all, hid_all, pre_all, *got)
+
+
+def gather_plan(tokens, cotangent, routes, gate_probs, matching, gate_weight, up_weight, down_weight):
+    expert_count = lax.axis_size("expert")
+    depth, shift, swap, first, second = moves(expert_count)
+
+    def send(value, pairs):
+        return lax.ppermute(value, AXES, pairs)
+
+    y, at = lax.axis_index("dp"), lax.axis_index("expert")
+    where = jnp.stack([y, at // (SIDE * CORES), (at // CORES) % SIDE, at % CORES]).astype(jnp.int32)
+
+    down = down_weight[0]
+    downs = (down, send(down, swap))
+    in_weight = jnp.concatenate([gate_weight[0], up_weight[0]], axis=1)
+    ins = (in_weight, send(in_weight, swap))
+
+    along = [tokens]
+    for _ in range(1, depth):
+        along.append(send(along[-1], shift[1]))
+    pieces = []
+    for piece in along:
+        a = send(piece, first)
+        b = send(piece, second)
+        d = send(a, second)
+        pieces.append((piece, a, b, d))
+
+    pairs = [jnp.stack([cotangent, send(cotangent, first)])]
+    for _ in range(1, depth):
+        pairs.append(send(pairs[-1], shift[1]))
+    fars = [send(pair, second) for pair in pairs]
+
+    mix = gate_probs / jnp.sum(gate_probs, axis=1, keepdims=True)
+    hit = routes[:, :, None] == jnp.arange(matching.shape[0], dtype=jnp.int32)
+    host = jnp.sum(jnp.where(hit, matching, 0), axis=2)
+    slots = jnp.arange(expert_count, dtype=jnp.int32)
+    slots = (slots[:, None] // CORES * CORES + jnp.arange(CORES, dtype=jnp.int32)).reshape(-1)
+    per_slot = jnp.sum(jnp.where(host[None] == slots[:, None, None], mix[None], 0.0), axis=2)
+    mix = lax.all_to_all(per_slot, "expert", split_axis=0, concat_axis=0, tiled=True).T
+
+    rows_all, pres, out = None, [], None
+    for back in range(depth):
+        *got, pre, rows_all = forward(back, depth, where, pieces[back], mix, ins, downs, rows_all)
+        pres.append(pre)
+        own, a, b, d = got
+        d = send(d, second)
+        b = send(b, second)
+        a = (a.astype(F32) + d).astype(BF16)
+        a = send(a, first)
+        own = own.astype(F32) + a + b
+        if back:
+            own = send(own.astype(BF16), shift[-back]).astype(F32)
+        out = own if out is None else out + own
+
+    kept = None
+    for back in range(depth):
+        kept = backward(back, depth, where, pairs[back], fars[back], pres[back], mix, downs, kept)
+    in_part, down_part = weight_grads(1, rows_all, kept, None)
+    got = (send(in_part, swap), send(down_part, swap))
+    gate_grad, up_grad, down_grad = weight_grads(0, rows_all, kept, got)
+    return out.astype(BF16), gate_grad[None], up_grad[None], down_grad[None]
+
+
 def solution(mesh):
+    experts = mesh.shape["expert"]
+    square = mesh.shape["dp"] == 2 and experts % (SIDE * CORES) == 0
+
+    def on_device(*args):
+        dense = 2 * args[2].shape[1] >= experts
+        if not (square and dense):
+            return exchange_plan(*args)
+        return gather_plan(*args)
+
     placed = (
         P("expert", "dp"),
         P("expert", "dp"),

time: 333 us -> 199 us (0.60)
  blocking collectives: 121 us -> 0 us
  Pallas kernels: 0 us -> 60.9 us
  waiting for transfers between devices: 119 us -> 70.8 us
  starting transfers between devices: 4.76 us -> 52.8 us
  matrix products: 29.6 us -> 0 us
  local copies, waits for them, and re-layouts: 29.3 us -> 6.14 us
  between operations: 14 us -> 1 us
  other arithmetic: 15 us -> 7.3 us
    all_to_all x2 -> x0, blocking collectives: 121 us -> none  [the longest x1 61.1 us: on_device(): lax.all_to_all(jnp.take(tokens, token_ids, axis=0, mode='fill', fill_valu...]
    all_gather x2 -> x0, waiting for transfers between devices: 119 us -> none  [the longest x1 62.2 us: on_device(): lax.all_gather(recv_rows, 'dp', axis=1, tiled=True)]
    ppermute x0 -> x42, waiting for transfers between devices: none -> 64.5 us  [send(): return lax.ppermute(value, AXES, pairs)]
    pallas_call x0 -> x10, Pallas kernels: none -> 60.9 us  [the longest x4 27.3 us: forward(): pl.pallas_call(functools.partial(forward_kernel, back, depth, fresh), out...]
    ppermute x0 -> x42, starting transfers between devices: none -> 49.3 us  [send(): return lax.ppermute(value, AXES, pairs)]
    dot_general x7 -> x0, matrix products: 29.6 us -> none  [the longest x1 5.86 us: on_device(): lax.dot_general(hidden, out_cot, contract_rows, preferred_element_type=jn...]
    gather x4 -> x0, local copies, waits for them, and re-layouts: 22.5 us -> none  [the longest x1 7.96 us: on_device(): jnp.take(merged, position, axis=0).reshape(token_count, fan_out, half_width)]
    all_to_all x1, waiting for transfers between devices: 0.01 us -> 6.35 us  [gather_plan(): lax.all_to_all(per_slot, 'expert', split_axis=0, concat_axis=0, tiled=True)]
  transfers between devices with their start and end apart: 4 -> 43, of which waited for: 2 -> 17; matrix products, arithmetic and copies ran while one was open for 7% -> 2% of each run, Pallas kernels for 0% -> 20%
where the time goes in v1:
time: 199 us
  waiting for transfers between devices  70.8 us (36%)
  Pallas kernels  60.9 us (31%)
  starting transfers between devices  52.8 us (27%)
  other arithmetic  7.3 us (4%)
  local copies, waits for them, and re-layouts  6.14 us (3%)
    ppermute x42, waiting for transfers between devices, send(): return lax.ppermute(value, AXES, pairs)  64.5 us
    ppermute x42, starting transfers between devices, send(): return lax.ppermute(value, AXES, pairs)  49.3 us
    pallas_call x4, Pallas kernels, forward(): pl.pallas_call(functools.partial(forward_kernel, back, depth, fresh), out...  27.3 us
    pallas_call x4, Pallas kernels, backward(): pl.pallas_call(functools.partial(backward_kernel, back, depth, fresh), ou...  16.5 us
    pallas_call x1, Pallas kernels, weight_grads(): pl.pallas_call(own_grads_kernel, out_shape=(shapes['half'], shapes['half'...  8.97 us
    pallas_call x1, Pallas kernels, weight_grads(): pl.pallas_call(partner_grads_kernel, out_shape=(shapes['in'], shapes['dow...  8.12 us
    all_to_all x1, waiting for transfers between devices, gather_plan(): lax.all_to_all(per_slot, 'expert', split_axis=0, concat_axis=0, tiled=True)  6.35 us
    unnamed x30, local copies, waits for them, and re-layouts  5.96 us
  transfers between devices with their start and end apart: 43, of which 17 were waited for; matrix products, arithmetic and copies ran while one was open for 2% of the time, Pallas kernels for 20%

profile of v1, /device:TPU:0, one launch (start us, length us, event | category | flops | bytes accessed | tf_op | source)
XLA Modules:
  0.0 198.9 jit_solution(16057342694440001881)
XLA Ops:
  0.7 3.9 %pad_maximum_fusion.refs_5_ = bf16[2048,768]{1,0:T(8,128)(2,1)} fusion(bf16[2048,384]{1,0:T(8,128)(2,1)} %bitcast.32, bf16[2048,384]{1,0:T(8,128)(2,1)} %bitcast.33), kind=kLoop, calls=%fused_computation | loop fusion | flops 6291456 | bytes 6291456 | tf_op jit(solution)/shard_map/concatenate | solution.py:355
  5.1 3.0 %collective-permute-start.32 = (bf16[128,1024]{1,0:T(8,128)(2,1)S(1)}, bf16[128,1024]{1,0:T(8,128)(2,1)S(1)}, u32[]{:S(2)}, u32[]{:S(2)}) collective-permute-start(bf16[128,1024]{1,0:T(8,128)(2,1)S(1)} %copy-done.11), channel_id=1, source_target_pairs={{0,2},{1,17},{2,0},{3,19},{4,6},{5,21},{6,4},{7,23},{8,10},{9,25},... | collective-permute-start | bytes 786440 | tf_op jit(solution)/shard_map/ppermute | solution.py:348
  8.1 2.0 collective-permute-start.1
  10.1 4.1 %collective-permute-done.32 = bf16[128,1024]{1,0:T(8,128)(2,1)S(1)} collective-permute-done((bf16[128,1024]{1,0:T(8,128)(2,1)S(1)}, bf16[128,1024]{1,0:T(8,128)(2,1)S(1)}, u32[]{:S(2)}, u32[]{:S(2)}) %collective-permute-start.32) | collective-permute-done | bytes 262176 | tf_op jit(solution)/shard_map/ppermute | solution.py:348
  14.3 2.5 %collective-permute-start.8 = (bf16[128,1024]{1,0:T(8,128)(2,1)S(1)}, bf16[128,1024]{1,0:T(8,128)(2,1)}, u32[]{:S(2)}, u32[]{:S(2)}) collective-permute-start(bf16[128,1024]{1,0:T(8,128)(2,1)S(1)} %copy-done.3), channel_id=1, source_target_pairs={{0,4},{1,5},{2,6},{3,7},{4,8},{5,9},{6,10},{7,11},{8,12},{9,13},{1... | collective-permute-start | bytes 786440 | tf_op jit(solution)/shard_map/ppermute | solution.py:348
  16.8 1.3 collective-permute-done.refs_1_
  18.0 2.1 %collective-permute-start.2 = (bf16[128,1024]{1,0:T(8,128)(2,1)S(1)}, bf16[128,1024]{1,0:T(8,128)(2,1)S(1)}, u32[]{:S(2)}, u32[]{:S(2)}) collective-permute-start(bf16[128,1024]{1,0:T(8,128)(2,1)S(1)} %collective-permute-done.refs_1_), channel_id=1, source_target_pairs={{0,16},{1,3},{2,18},{3,1},{4,20},{5,7},{6,22},{7,5},{8,24},{9,11},... | collective-permute-start | bytes 786440 | tf_op jit(solution)/shard_map/ppermute | solution.py:348
  21.6 1.6 collective-permute-start.33
  23.2 1.5 collective-permute-start.16
  25.5 1.7 collective-permute-start.10
  27.3 14.7 %collective-permute-done.16.refs_0_ = bf16[128,1024]{1,0:T(8,128)(2,1)S(1)} collective-permute-done((bf16[128,1024]{1,0:T(8,128)(2,1)}, bf16[128,1024]{1,0:T(8,128)(2,1)S(1)}, u32[]{:S(2)}, u32[]{:S(2)}) %collective-permute-start.16) | collective-permute-done | bytes 262176 | tf_op jit(solution)/shard_map/ppermute | solution.py:348
  41.9 1.5 collective-permute-start.39
  44.9 6.3 %collective-permute-done.9.refs_1_ = bf16[128,1024]{1,0:T(8,128)(2,1)} collective-permute-done((bf16[128,1024]{1,0:T(8,128)(2,1)}, bf16[128,1024]{1,0:T(8,128)(2,1)}, u32[]{:S(2)}, u32[]{:S(2)}) %collective-permute-start.9) | collective-permute-done | bytes 262176 | tf_op jit(solution)/shard_map/ppermute | solution.py:348
  51.3 2.7 %collective-permute-start.38 = (bf16[2,128,1024]{2,1,0:T(8,128)(2,1)}, bf16[2,128,1024]{2,1,0:T(8,128)(2,1)}, u32[]{:S(2)}, u32[]{:S(2)}) collective-permute-start(bf16[2,128,1024]{2,1,0:T(8,128)(2,1)} %collective-permute-done.33.refs_0_), channel_id=1, source_target_pairs={{0,16},{1,3},{2,18},{3,1},{4,20},{5,7},{6,22},{7,5},{8,24},{9,11},... | collective-permute-start | bytes 1572872 | tf_op jit(solution)/shard_map/ppermute | solution.py:348
  54.7 3.5 %all-to-all-start = ((f32[16,2,128]{2,1,0:T(2,128)}), f32[16,2,128]{2,1,0:T(2,128)S(1)}, u32[]{:S(2)}, u32[]{:S(2)}) async-start(f32[16,2,128]{2,1,0:T(2,128)} %bitcast.4), calls=%async_computation | async-start | bytes 32768 | tf_op jit(solution)/shard_map/all_to_all | solution.py:379
  58.3 6.3 %all-to-all-done = f32[16,2,128]{2,1,0:T(2,128)S(1)} async-done(((f32[16,2,128]{2,1,0:T(2,128)}), f32[16,2,128]{2,1,0:T(2,128)S(1)}, u32[]{:S(2)}, u32[]{:S(2)}) %all-to-all-start) | async-done | bytes 16416 | tf_op jit(solution)/shard_map/all_to_all | solution.py:379
  70.5 6.7 %shard_map.111 = (bf16[128,1024]{1,0:T(8,128)(2,1)S(1)}, bf16[128,1024]{1,0:T(8,128)(2,1)S(1)}, bf16[128,1024]{1,0:T(8,128)(2,1)S(1)}, bf16[128,1024]{1,0:T(8,12...) custom-call(s32[4]{0:T(128)S(1)} %pad_add_fusion.where_ref, bf16[128,1024]{1,0:T(8,128)(2,1)S(1)} %copy-done.4, ...), custom_call_target="tpu_custom_call" | custom-call | flops 2415919104 | bytes 3145728 | tf_op jit(solution)/shard_map/pallas_call | solution.py:197
  77.2 4.4 %shard_map.115 = (bf16[2,1024,2048]{2,1,0:T(8,128)(2,1)S(1)}, bf16[2,1024,384]{2,1,0:T(8,128)(2,1)S(1)}, bf16[2,1024,768]{2,1,0:T(8,128)(2,1)S(1)}) custom-call(s32[4]{0:T(128)S(1)} %pad_add_fusion.where_ref, bf16[2,128,1024]{2,1,0:T(8,128)(2,1)} %pad_maximum_fusion.1.refs_0_, bf16[2,128,1024]{2,1,0:T(8,128)(2,1)} %collective-permute-done.39.refs_1_, ...), custom_call_target="tpu_custom_call" | custom-call | flops 805306368 | bytes 5242880 | tf_op jit(solution)/shard_map/pallas_call | solution.py:259
  81.6 1.9 collective-permute-start.18
  83.5 1.4 collective-permute-start.25
  85.2 1.8 collective-permute-start.37
  87.0 6.9 %shard_map.112 = (bf16[128,1024]{1,0:T(8,128)(2,1)S(1)}, bf16[128,1024]{1,0:T(8,128)(2,1)S(1)}, bf16[128,1024]{1,0:T(8,128)(2,1)S(1)}, bf16[128,1024]{1,0:T(8,12...) custom-call(s32[4]{0:T(128)S(1)} %pad_add_fusion.where_ref, ...), custom_call_target="tpu_custom_call", output_to_operand_aliasing={{5}: (10, {})} | custom-call | flops 2415919104 | bytes 3145728 | tf_op jit(solution)/shard_map/pallas_call | solution.py:197
  93.9 4.3 %shard_map.116 = (bf16[2,1024,2048]{2,1,0:T(8,128)(2,1)S(1)}, bf16[2,1024,384]{2,1,0:T(8,128)(2,1)S(1)}, bf16[2,1024,768]{2,1,0:T(8,128)(2,1)S(1)}) custom-call(s32[4]{0:T(128)S(1)} %pad_add_fusion.where_ref, bf16[2,128,1024]{2,1,0:T(8,128)(2,1)} %collective-permute-done.33.refs_0_, ...), custom_call_target="tpu_custom_call", output_to_operand_aliasing={{0}: (7, {}), {1}: (8, {}), {2}: (9, {})} | custom-call | flops 805306368 | bytes 5242880 | tf_op jit(solution)/shard_map/pallas_call | solution.py:259
  98.5 1.8 collective-permute-start.27
  100.5 7.0 %shard_map.113 = (bf16[128,1024]{1,0:T(8,128)(2,1)S(1)}, bf16[128,1024]{1,0:T(8,128)(2,1)S(1)}, bf16[128,1024]{1,0:T(8,128)(2,1)S(1)}, bf16[128,1024]{1,0:T(8,12...) custom-call(s32[4]{0:T(128)S(1)} %pad_add_fusion.where_ref, ...), custom_call_target="tpu_custom_call", output_to_operand_aliasing={{5}: (10, {})} | custom-call | flops 2415919104 | bytes 3145728 | tf_op jit(solution)/shard_map/pallas_call | solution.py:197
  107.5 4.1 %shard_map.117 = (bf16[2,1024,2048]{2,1,0:T(8,128)(2,1)S(1)}, bf16[2,1024,384]{2,1,0:T(8,128)(2,1)S(1)}, bf16[2,1024,768]{2,1,0:T(8,128)(2,1)S(1)}) custom-call(s32[4]{0:T(128)S(1)} %pad_add_fusion.where_ref, bf16[2,128,1024]{2,1,0:T(8,128)(2,1)} %collective-permute-done.34.refs_0_, ...), custom_call_target="tpu_custom_call", output_to_operand_aliasing={{0}: (7, {}), {1}: (8, {}), {2}: (9, {})} | custom-call | flops 805306368 | bytes 5242880 | tf_op jit(solution)/shard_map/pallas_call | solution.py:259
  111.7 6.7 %shard_map.114 = (bf16[128,1024]{1,0:T(8,128)(2,1)S(1)}, bf16[128,1024]{1,0:T(8,128)(2,1)S(1)}, bf16[128,1024]{1,0:T(8,128)(2,1)S(1)}, bf16[128,1024]{1,0:T(8,12...) custom-call(s32[4]{0:T(128)S(1)} %pad_add_fusion.where_ref, ...), custom_call_target="tpu_custom_call", output_to_operand_aliasing={{5}: (10, {})} | custom-call | flops 2415919104 | bytes 3145728 | tf_op jit(solution)/shard_map/pallas_call | solution.py:197
  118.4 3.6 %shard_map.118 = (bf16[2,1024,2048]{2,1,0:T(8,128)(2,1)S(1)}, bf16[2,1024,384]{2,1,0:T(8,128)(2,1)S(1)}, bf16[2,1024,768]{2,1,0:T(8,128)(2,1)S(1)}) custom-call(s32[4]{0:T(128)S(1)} %pad_add_fusion.where_ref, bf16[2,128,1024]{2,1,0:T(8,128)(2,1)S(1)} %collective-permute-done.35.refs_0_, ...), custom_call_target="tpu_custom_call", output_to_operand_aliasing={{0}: (7, {}), {1}: (8, {}), {2}: (9, {})} | custom-call | flops 805306368 | bytes 5242880 | tf_op jit(solution)/shard_map/pallas_call | solution.py:259
  122.1 8.1 %shard_map.119 = (bf16[2048,768]{1,0:T(8,128)(2,1)S(1)}, bf16[384,2048]{1,0:T(8,128)(2,1)S(1)}) custom-call(bf16[1024,2048]{1,0:T(8,128)(2,1)S(1)} %get-tuple-element.64.rows_ref, bf16[2,1024,2048]{2,1,0:T(8,128)(2,1)S(1)} %get-tuple-element.78.cot_ref, bf16[2,1024,384]{2,1,0:T(8,128)(2,1)S(1)} %get-tuple-element.79.hid_ref, ...), custom_call_target="tpu_custom_call" | custom-call | flops 4831838208 | bytes 17825792 | tf_op jit(solution)/shard_map/pallas_call | solution.py:327
  130.3 1.9 collective-permute-start.5
  132.4 1.8 collective-permute-start.14
  134.4 2.3 %collective-permute-done.5 = bf16[128,1024]{1,0:T(8,128)(2,1)S(1)} collective-permute-done((bf16[128,1024]{1,0:T(8,128)(2,1)S(1)}, bf16[128,1024]{1,0:T(8,128)(2,1)S(1)}, u32[]{:S(2)}, u32[]{:S(2)}) %collective-permute-start.5) | collective-permute-done | bytes 262176 | tf_op jit(solution)/shard_map/ppermute | solution.py:348
  136.7 1.8 collective-permute-start.22
  139.6 1.8 collective-permute-start.28
  142.4 2.8 %collective-permute-done.20 = bf16[128,1024]{1,0:T(8,128)(2,1)S(1)} collective-permute-done((bf16[128,1024]{1,0:T(8,128)(2,1)S(1)}, bf16[128,1024]{1,0:T(8,128)(2,1)S(1)}, u32[]{:S(2)}, u32[]{:S(2)}) %collective-permute-start.20) | collective-permute-done | bytes 262176 | tf_op jit(solution)/shard_map/ppermute | solution.py:348
  145.8 2.8 %collective-permute-done.22 = bf16[128,1024]{1,0:T(8,128)(2,1)S(1)} collective-permute-done((bf16[128,1024]{1,0:T(8,128)(2,1)S(1)}, bf16[128,1024]{1,0:T(8,128)(2,1)S(1)}, u32[]{:S(2)}, u32[]{:S(2)}) %collective-permute-start.22) | collective-permute-done | bytes 262176 | tf_op jit(solution)/shard_map/ppermute | solution.py:348
  148.6 1.8 collective-permute-start.30
  150.4 3.2 %collective-permute-done.28 = bf16[128,1024]{1,0:T(8,128)(2,1)S(1)} collective-permute-done((bf16[128,1024]{1,0:T(8,128)(2,1)S(1)}, bf16[128,1024]{1,0:T(8,128)(2,1)S(1)}, u32[]{:S(2)}, u32[]{:S(2)}) %collective-permute-start.28) | collective-permute-done | bytes 262176 | tf_op jit(solution)/shard_map/ppermute | solution.py:348
  154.3 1.4 collective-permute-start.29
  155.9 2.4 %collective-permute-done.30 = bf16[128,1024]{1,0:T(8,128)(2,1)S(1)} collective-permute-done((bf16[128,1024]{1,0:T(8,128)(2,1)S(1)}, bf16[128,1024]{1,0:T(8,128)(2,1)S(1)}, u32[]{:S(2)}, u32[]{:S(2)}) %collective-permute-start.30) | collective-permute-done | bytes 262176 | tf_op jit(solution)/shard_map/ppermute | solution.py:348
  158.3 1.8 collective-permute-start.7
  160.1 1.2 collective-permute-done.21
  162.0 3.5 %collective-permute-done.29 = bf16[128,1024]{1,0:T(8,128)(2,1)S(1)} collective-permute-done((bf16[128,1024]{1,0:T(8,128)(2,1)S(1)}, bf16[128,1024]{1,0:T(8,128)(2,1)S(1)}, u32[]{:S(2)}, u32[]{:S(2)}) %collective-permute-start.29) | collective-permute-done | bytes 262176 | tf_op jit(solution)/shard_map/ppermute | solution.py:348
  165.6 3.2 %collective-permute-start.15 = (bf16[128,1024]{1,0:T(8,128)(2,1)S(1)}, bf16[128,1024]{1,0:T(8,128)(2,1)S(1)}, u32[]{:S(2)}, u32[]{:S(2)}) collective-permute-start(bf16[128,1024]{1,0:T(8,128)(2,1)S(1)} %add_convert_fusion.5), channel_id=1, source_target_pairs={{0,12},{1,13},{2,14},{3,15},{4,0},{5,1},{6,2},{7,3},{8,4},{9,5},{1... | collective-permute-start | bytes 786440 | tf_op jit(solution)/shard_map/ppermute | solution.py:348
  169.0 1.9 collective-permute-start.23
  171.3 4.2 %collective-permute-done.15 = bf16[128,1024]{1,0:T(8,128)(2,1)S(1)} collective-permute-done((bf16[128,1024]{1,0:T(8,128)(2,1)S(1)}, bf16[128,1024]{1,0:T(8,128)(2,1)S(1)}, u32[]{:S(2)}, u32[]{:S(2)}) %collective-permute-start.15) | collective-permute-done | bytes 262176 | tf_op jit(solution)/shard_map/ppermute | solution.py:348
  175.5 13.5 %collective-permute-done.23 = bf16[128,1024]{1,0:T(8,128)(2,1)S(1)} collective-permute-done((bf16[128,1024]{1,0:T(8,128)(2,1)S(1)}, bf16[128,1024]{1,0:T(8,128)(2,1)S(1)}, u32[]{:S(2)}, u32[]{:S(2)}) %collective-permute-start.23) | collective-permute-done | bytes 262176 | tf_op jit(solution)/shard_map/ppermute | solution.py:348
  190.0 9.0 %shard_map.120 = (bf16[2048,384]{1,0:T(8,128)(2,1)}, bf16[2048,384]{1,0:T(8,128)(2,1)}, bf16[384,2048]{1,0:T(8,128)(2,1)}) custom-call(bf16[1024,2048]{1,0:T(8,128)(2,1)S(1)} %get-tuple-element.64.rows_ref, bf16[2,1024,2048]{2,1,0:T(8,128)(2,1)S(1)} %get-tuple-element.78.cot_ref, bf16[2,1024,384]{2,1,0:T(8,128)(2,1)S(1)} %get-tuple-element.79.hid_ref, ...), custom_call_target="tpu_custom_call" | custom-call | flops 4831838208 | bytes 17825792 | tf_op jit(solution)/shard_map/pallas_call | solution.py:334
  (97 shorter events, 18.1 us)
Async XLA Ops:
  0.7 44.0 %copy-start.13 = (s32[128,8]{0,1:T(8,128)S(1)}, s32[128,8]{0,1:T(8,128)}, u32[]{:S(2)}) copy-start(s32[128,8]{0,1:T(8,128)} %param.10) | copy-start | bytes 12292
  0.7 44.0 %copy-start.14 = (s32[16]{0:T(128)S(1)}, s32[16]{0:T(128)}, u32[]{:S(2)}) copy-start(s32[16]{0:T(128)} %param.12) | copy-start | bytes 196
  0.7 44.2 %copy-start.12 = (f32[128,8]{0,1:T(8,128)S(1)}, f32[128,8]{0,1:T(8,128)}, u32[]{:S(2)}) copy-start(f32[128,8]{0,1:T(8,128)} %param.11) | copy-start | bytes 12292
  4.6 61.3 %collective-permute-start.3 = (bf16[2048,768]{1,0:T(8,128)(2,1)}, bf16[2048,768]{1,0:T(8,128)(2,1)}, u32[]{:S(2)}, u32[]{:S(2)}) collective-permute-start(bf16[2048,768]{1,0:T(8,128)(2,1)} %pad_maximum_fusion.refs_5_), channel_id=1, source_target_pairs={{0,1},{1,0},{2,3},{3,2},{4,5},{5,4},{6,7},{7,6},{8,9},{9,8},{10,11... | collective-permute-start | bytes 9437192 | tf_op jit(solution)/shard_map/ppermute | solution.py:348
  5.1 60.8 %collective-permute-start.4 = (bf16[384,2048]{1,0:T(8,128)(2,1)S(1)}, bf16[384,2048]{1,0:T(8,128)(2,1)S(1)}, u32[]{:S(2)}, u32[]{:S(2)}) collective-permute-start(bf16[384,2048]{1,0:T(8,128)(2,1)S(1)} %bitcast.15), channel_id=1, source_target_pairs={{0,1},{1,0},{2,3},{3,2},{4,5},{5,4},{6,7},{7,6},{8,9},{9,8},{10,11... | collective-permute-start | bytes 4718600 | tf_op jit(solution)/shard_map/ppermute | solution.py:348
  5.1 9.2 %collective-permute-start.32 = (bf16[128,1024]{1,0:T(8,128)(2,1)S(1)}, bf16[128,1024]{1,0:T(8,128)(2,1)S(1)}, u32[]{:S(2)}, u32[]{:S(2)}) collective-permute-start(bf16[128,1024]{1,0:T(8,128)(2,1)S(1)} %copy-done.11), channel_id=1, source_target_pairs={{0,2},{1,17},{2,0},{3,19},{4,6},{5,21},{6,4},{7,23},{8,10},{9,25},... | collective-permute-start | bytes 786440 | tf_op jit(solution)/shard_map/ppermute | solution.py:348
  8.1 10.0 %collective-permute-start = (bf16[128,1024]{1,0:T(8,128)(2,1)S(1)}, bf16[128,1024]{1,0:T(8,128)(2,1)S(1)}, u32[]{:S(2)}, u32[]{:S(2)}) collective-permute-start(bf16[128,1024]{1,0:T(8,128)(2,1)S(1)} %copy-done.3), channel_id=1, source_target_pairs={{0,2},{1,17},{2,0},{3,19},{4,6},{5,21},{6,4},{7,23},{8,10},{9,25},... | collective-permute-start | bytes 786440 | tf_op jit(solution)/shard_map/ppermute | solution.py:348
  8.1 12.8 %collective-permute-start.1 = (bf16[128,1024]{1,0:T(8,128)(2,1)S(1)}, bf16[128,1024]{1,0:T(8,128)(2,1)S(1)}, u32[]{:S(2)}, u32[]{:S(2)}) collective-permute-start(bf16[128,1024]{1,0:T(8,128)(2,1)S(1)} %copy-done.3), channel_id=1, source_target_pairs={{0,16},{1,3},{2,18},{3,1},{4,20},{5,7},{6,22},{7,5},{8,24},{9,11},... | collective-permute-start | bytes 786440 | tf_op jit(solution)/shard_map/ppermute | solution.py:348
  14.3 9.0 %collective-permute-start.8 = (bf16[128,1024]{1,0:T(8,128)(2,1)S(1)}, bf16[128,1024]{1,0:T(8,128)(2,1)}, u32[]{:S(2)}, u32[]{:S(2)}) collective-permute-start(bf16[128,1024]{1,0:T(8,128)(2,1)S(1)} %copy-done.3), channel_id=1, source_target_pairs={{0,4},{1,5},{2,6},{3,7},{4,8},{5,9},{6,10},{7,11},{8,12},{9,13},{1... | collective-permute-start | bytes 786440 | tf_op jit(solution)/shard_map/ppermute | solution.py:348
  18.0 25.4 %copy-start.5 = (bf16[128,1024]{1,0:T(8,128)(2,1)}, bf16[128,1024]{1,0:T(8,128)(2,1)S(1)}, u32[]{:S(2)}) copy-start(bf16[128,1024]{1,0:T(8,128)(2,1)S(1)} %collective-permute-done.refs_1_) | copy-start | bytes 786436
  18.0 6.8 %collective-permute-start.2 = (bf16[128,1024]{1,0:T(8,128)(2,1)S(1)}, bf16[128,1024]{1,0:T(8,128)(2,1)S(1)}, u32[]{:S(2)}, u32[]{:S(2)}) collective-permute-start(bf16[128,1024]{1,0:T(8,128)(2,1)S(1)} %collective-permute-done.refs_1_), channel_id=1, source_target_pairs={{0,16},{1,3},{2,18},{3,1},{4,20},{5,7},{6,22},{7,5},{8,24},{9,11},... | collective-permute-start | bytes 786440 | tf_op jit(solution)/shard_map/ppermute | solution.py:348
  21.6 23.1 %collective-permute-start.33 = (bf16[2,128,1024]{2,1,0:T(8,128)(2,1)}, bf16[2,128,1024]{2,1,0:T(8,128)(2,1)}, u32[]{:S(2)}, u32[]{:S(2)}) collective-permute-start(bf16[2,128,1024]{2,1,0:T(8,128)(2,1)} %pad_maximum_fusion.1.refs_0_), channel_id=1, source_target_pairs={{0,4},{1,5},{2,6},{3,7},{4,8},{5,9},{6,10},{7,11},{8,12},{9,13},{1... | collective-permute-start | bytes 1572872 | tf_op jit(solution)/shard_map/ppermute | solution.py:348
  23.2 18.7 %collective-permute-start.16 = (bf16[128,1024]{1,0:T(8,128)(2,1)}, bf16[128,1024]{1,0:T(8,128)(2,1)S(1)}, u32[]{:S(2)}, u32[]{:S(2)}) collective-permute-start(bf16[128,1024]{1,0:T(8,128)(2,1)} %collective-permute-done.8.refs_0_), channel_id=1, source_target_pairs={{0,4},{1,5},{2,6},{3,7},{4,8},{5,9},{6,10},{7,11},{8,12},{9,13},{1... | collective-permute-start | bytes 786440 | tf_op jit(solution)/shard_map/ppermute | solution.py:348
  25.5 17.9 %collective-permute-start.10 = (bf16[128,1024]{1,0:T(8,128)(2,1)}, bf16[128,1024]{1,0:T(8,128)(2,1)S(1)}, u32[]{:S(2)}, u32[]{:S(2)}) collective-permute-start(bf16[128,1024]{1,0:T(8,128)(2,1)} %collective-permute-done.8.refs_0_), channel_id=1, source_target_pairs={{0,16},{1,3},{2,18},{3,1},{4,20},{5,7},{6,22},{7,5},{8,24},{9,11},... | collective-permute-start | bytes 786440 | tf_op jit(solution)/shard_map/ppermute | solution.py:348
  41.9 22.8 %collective-permute-start.39 = (bf16[2,128,1024]{2,1,0:T(8,128)(2,1)}, bf16[2,128,1024]{2,1,0:T(8,128)(2,1)}, u32[]{:S(2)}, u32[]{:S(2)}) collective-permute-start(bf16[2,128,1024]{2,1,0:T(8,128)(2,1)} %pad_maximum_fusion.1.refs_0_), channel_id=1, source_target_pairs={{0,16},{1,3},{2,18},{3,1},{4,20},{5,7},{6,22},{7,5},{8,24},{9,11},... | collective-permute-start | bytes 1572872 | tf_op jit(solution)/shard_map/ppermute | solution.py:348
  44.2 7.1 %collective-permute-start.9 = (bf16[128,1024]{1,0:T(8,128)(2,1)}, bf16[128,1024]{1,0:T(8,128)(2,1)}, u32[]{:S(2)}, u32[]{:S(2)}) collective-permute-start(bf16[128,1024]{1,0:T(8,128)(2,1)} %collective-permute-done.8.refs_0_), channel_id=1, source_target_pairs={{0,2},{1,17},{2,0},{3,19},{4,6},{5,21},{6,4},{7,23},{8,10},{9,25},... | collective-permute-start | bytes 786440 | tf_op jit(solution)/shard_map/ppermute | solution.py:348
  44.7 20.6 %collective-permute-start.34 = (bf16[2,128,1024]{2,1,0:T(8,128)(2,1)}, bf16[2,128,1024]{2,1,0:T(8,128)(2,1)}, u32[]{:S(2)}, u32[]{:S(2)}) collective-permute-start(bf16[2,128,1024]{2,1,0:T(8,128)(2,1)} %collective-permute-done.33.refs_0_), channel_id=1, source_target_pairs={{0,4},{1,5},{2,6},{3,7},{4,8},{5,9},{6,10},{7,11},{8,12},{9,13},{1... | collective-permute-start | bytes 1572872 | tf_op jit(solution)/shard_map/ppermute | solution.py:348
  51.3 33.9 %collective-permute-start.38 = (bf16[2,128,1024]{2,1,0:T(8,128)(2,1)}, bf16[2,128,1024]{2,1,0:T(8,128)(2,1)}, u32[]{:S(2)}, u32[]{:S(2)}) collective-permute-start(bf16[2,128,1024]{2,1,0:T(8,128)(2,1)} %collective-permute-done.33.refs_0_), channel_id=1, source_target_pairs={{0,16},{1,3},{2,18},{3,1},{4,20},{5,7},{6,22},{7,5},{8,24},{9,11},... | collective-permute-start | bytes 1572872 | tf_op jit(solution)/shard_map/ppermute | solution.py:348
  54.7 9.9 %all-to-all-start = ((f32[16,2,128]{2,1,0:T(2,128)}), f32[16,2,128]{2,1,0:T(2,128)S(1)}, u32[]{:S(2)}, u32[]{:S(2)}) async-start(f32[16,2,128]{2,1,0:T(2,128)} %bitcast.4), calls=%async_computation | async-start | bytes 32768 | tf_op jit(solution)/shard_map/all_to_all | solution.py:379
  64.8 16.8 %collective-permute-start.24 = (bf16[128,1024]{1,0:T(8,128)(2,1)S(1)}, bf16[128,1024]{1,0:T(8,128)(2,1)S(1)}, u32[]{:S(2)}, u32[]{:S(2)}) collective-permute-start(bf16[128,1024]{1,0:T(8,128)(2,1)S(1)} %collective-permute-done.16.refs_0_), channel_id=1, source_target_pairs={{0,4},{1,5},{2,6},{3,7},{4,8},{5,9},{6,10},{7,11},{8,12},{9,13},{1... | collective-permute-start | bytes 786440 | tf_op jit(solution)/shard_map/ppermute | solution.py:348
  65.3 18.2 %collective-permute-start.17 = (bf16[128,1024]{1,0:T(8,128)(2,1)S(1)}, bf16[128,1024]{1,0:T(8,128)(2,1)S(1)}, u32[]{:S(2)}, u32[]{:S(2)}) collective-permute-start(bf16[128,1024]{1,0:T(8,128)(2,1)S(1)} %collective-permute-done.16.refs_0_), channel_id=1, source_target_pairs={{0,2},{1,17},{2,0},{3,19},{4,6},{5,21},{6,4},{7,23},{8,10},{9,25},... | collective-permute-start | bytes 786440 | tf_op jit(solution)/shard_map/ppermute | solution.py:348
  65.9 19.1 %collective-permute-start.11 = (bf16[128,1024]{1,0:T(8,128)(2,1)}, bf16[128,1024]{1,0:T(8,128)(2,1)S(1)}, u32[]{:S(2)}, u32[]{:S(2)}) collective-permute-start(bf16[128,1024]{1,0:T(8,128)(2,1)} %collective-permute-done.9.refs_1_), channel_id=1, source_target_pairs={{0,16},{1,3},{2,18},{3,1},{4,20},{5,7},{6,22},{7,5},{8,24},{9,11},... | collective-permute-start | bytes 786440 | tf_op jit(solution)/shard_map/ppermute | solution.py:348
  65.9 34.4 %collective-permute-start.35 = (bf16[2,128,1024]{2,1,0:T(8,128)(2,1)}, bf16[2,128,1024]{2,1,0:T(8,128)(2,1)S(1)}, u32[]{:S(2)}, u32[]{:S(2)}) collective-permute-start(bf16[2,128,1024]{2,1,0:T(8,128)(2,1)} %collective-permute-done.34.refs_0_), channel_id=1, source_target_pairs={{0,4},{1,5},{2,6},{3,7},{4,8},{5,9},{6,10},{7,11},{8,12},{9,13},{1... | collective-permute-start | bytes 1572872 | tf_op jit(solution)/shard_map/ppermute | solution.py:348
  77.2 9.7 %copy-start.2 = (bf16[128,1024]{1,0:T(8,128)(2,1)S(1)}, bf16[128,1024]{1,0:T(8,128)(2,1)}, u32[]{:S(2)}) copy-start(bf16[128,1024]{1,0:T(8,128)(2,1)} %copy-done.1) | copy-start | bytes 786436
  81.6 16.6 %collective-permute-start.18 = (bf16[128,1024]{1,0:T(8,128)(2,1)S(1)}, bf16[128,1024]{1,0:T(8,128)(2,1)S(1)}, u32[]{:S(2)}, u32[]{:S(2)}) collective-permute-start(bf16[128,1024]{1,0:T(8,128)(2,1)S(1)} %collective-permute-done.16.refs_0_), channel_id=1, source_target_pairs={{0,16},{1,3},{2,18},{3,1},{4,20},{5,7},{6,22},{7,5},{8,24},{9,11},... | collective-permute-start | bytes 786440 | tf_op jit(solution)/shard_map/ppermute | solution.py:348
  83.5 15.0 %collective-permute-start.25 = (bf16[128,1024]{1,0:T(8,128)(2,1)S(1)}, bf16[128,1024]{1,0:T(8,128)(2,1)S(1)}, u32[]{:S(2)}, u32[]{:S(2)}) collective-permute-start(bf16[128,1024]{1,0:T(8,128)(2,1)S(1)} %collective-permute-done.24.refs_0_), channel_id=1, source_target_pairs={{0,2},{1,17},{2,0},{3,19},{4,6},{5,21},{6,4},{7,23},{8,10},{9,25},... | collective-permute-start | bytes 786440 | tf_op jit(solution)/shard_map/ppermute | solution.py:348
  84.9 15.6 %collective-permute-start.19 = (bf16[128,1024]{1,0:T(8,128)(2,1)S(1)}, bf16[128,1024]{1,0:T(8,128)(2,1)S(1)}, u32[]{:S(2)}, u32[]{:S(2)}) collective-permute-start(bf16[128,1024]{1,0:T(8,128)(2,1)S(1)} %collective-permute-done.17.refs_1_), channel_id=1, source_target_pairs={{0,16},{1,3},{2,18},{3,1},{4,20},{5,7},{6,22},{7,5},{8,24},{9,11},... | collective-permute-start | bytes 786440 | tf_op jit(solution)/shard_map/ppermute | solution.py:348
  85.2 22.3 %collective-permute-start.37 = (bf16[2,128,1024]{2,1,0:T(8,128)(2,1)}, bf16[2,128,1024]{2,1,0:T(8,128)(2,1)S(1)}, u32[]{:S(2)}, u32[]{:S(2)}) collective-permute-start(bf16[2,128,1024]{2,1,0:T(8,128)(2,1)} %collective-permute-done.34.refs_0_), channel_id=1, source_target_pairs={{0,16},{1,3},{2,18},{3,1},{4,20},{5,7},{6,22},{7,5},{8,24},{9,11},... | collective-permute-start | bytes 1572872 | tf_op jit(solution)/shard_map/ppermute | solution.py:348
  98.2 13.5 %collective-permute-start.26 = (bf16[128,1024]{1,0:T(8,128)(2,1)S(1)}, bf16[128,1024]{1,0:T(8,128)(2,1)S(1)}, u32[]{:S(2)}, u32[]{:S(2)}) collective-permute-start(bf16[128,1024]{1,0:T(8,128)(2,1)S(1)} %collective-permute-done.24.refs_0_), channel_id=1, source_target_pairs={{0,16},{1,3},{2,18},{3,1},{4,20},{5,7},{6,22},{7,5},{8,24},{9,11},... | collective-permute-start | bytes 786440 | tf_op jit(solution)/shard_map/ppermute | solution.py:348
  98.5 13.2 %collective-permute-start.27 = (bf16[128,1024]{1,0:T(8,128)(2,1)S(1)}, bf16[128,1024]{1,0:T(8,128)(2,1)S(1)}, u32[]{:S(2)}, u32[]{:S(2)}) collective-permute-start(bf16[128,1024]{1,0:T(8,128)(2,1)S(1)} %collective-permute-done.25.refs_1_), channel_id=1, source_target_pairs={{0,16},{1,3},{2,18},{3,1},{4,20},{5,7},{6,22},{7,5},{8,24},{9,11},... | collective-permute-start | bytes 786440 | tf_op jit(solution)/shard_map/ppermute | solution.py:348
  100.3 18.1 %collective-permute-start.36 = (bf16[2,128,1024]{2,1,0:T(8,128)(2,1)S(1)}, bf16[2,128,1024]{2,1,0:T(8,128)(2,1)S(1)}, u32[]{:S(2)}, u32[]{:S(2)}) collective-permute-start(bf16[2,128,1024]{2,1,0:T(8,128)(2,1)S(1)} %collective-permute-done.35.refs_0_), channel_id=1, source_target_pairs={{0,16},{1,3},{2,18},{3,1},{4,20},{5,7},{6,22},{7,5},{8,24},{9,11},... | collective-permute-start | bytes 1572872 | tf_op jit(solution)/shard_map/ppermute | solution.py:348
  130.2 59.8 %collective-permute-start.40 = (bf16[2048,768]{1,0:T(8,128)(2,1)S(1)}, bf16[2048,768]{1,0:T(8,128)(2,1)S(1)}, u32[]{:S(2)}, u32[]{:S(2)}) collective-permute-start(bf16[2048,768]{1,0:T(8,128)(2,1)S(1)} %get-tuple-element.81), channel_id=1, source_target_pairs={{0,1},{1,0},{2,3},{3,2},{4,5},{5,4},{6,7},{7,6},{8,9},{9,8},{10,11... | collective-permute-start | bytes 9437192 | tf_op jit(solution)/shard_map/ppermute | solution.py:348
  130.3 6.4 %collective-permute-start.5 = (bf16[128,1024]{1,0:T(8,128)(2,1)S(1)}, bf16[128,1024]{1,0:T(8,128)(2,1)S(1)}, u32[]{:S(2)}, u32[]{:S(2)}) collective-permute-start(bf16[128,1024]{1,0:T(8,128)(2,1)S(1)} %get-tuple-element.47), channel_id=1, source_target_pairs={{0,16},{1,3},{2,18},{3,1},{4,20},{5,7},{6,22},{7,5},{8,24},{9,11},... | collective-permute-start | bytes 786440 | tf_op jit(solution)/shard_map/ppermute | solution.py:348
  132.2 7.4 %collective-permute-start.12 = (bf16[128,1024]{1,0:T(8,128)(2,1)S(1)}, bf16[128,1024]{1,0:T(8,128)(2,1)S(1)}, u32[]{:S(2)}, u32[]{:S(2)}) collective-permute-start(bf16[128,1024]{1,0:T(8,128)(2,1)S(1)} %get-tuple-element.52), channel_id=1, source_target_pairs={{0,16},{1,3},{2,18},{3,1},{4,20},{5,7},{6,22},{7,5},{8,24},{9,11},... | collective-permute-start | bytes 786440 | tf_op jit(solution)/shard_map/ppermute | solution.py:348
  132.4 10.0 %collective-permute-start.14 = (bf16[128,1024]{1,0:T(8,128)(2,1)S(1)}, bf16[128,1024]{1,0:T(8,128)(2,1)S(1)}, u32[]{:S(2)}, u32[]{:S(2)}) collective-permute-start(bf16[128,1024]{1,0:T(8,128)(2,1)S(1)} %get-tuple-element.53), channel_id=1, source_target_pairs={{0,16},{1,3},{2,18},{3,1},{4,20},{5,7},{6,22},{7,5},{8,24},{9,11},... | collective-permute-start | bytes 786440 | tf_op jit(solution)/shard_map/ppermute | solution.py:348
  134.2 11.0 %collective-permute-start.20 = (bf16[128,1024]{1,0:T(8,128)(2,1)S(1)}, bf16[128,1024]{1,0:T(8,128)(2,1)S(1)}, u32[]{:S(2)}, u32[]{:S(2)}) collective-permute-start(bf16[128,1024]{1,0:T(8,128)(2,1)S(1)} %get-tuple-element.57), channel_id=1, source_target_pairs={{0,16},{1,3},{2,18},{3,1},{4,20},{5,7},{6,22},{7,5},{8,24},{9,11},... | collective-permute-start | bytes 786440 | tf_op jit(solution)/shard_map/ppermute | solution.py:348
  136.7 11.8 %collective-permute-start.22 = (bf16[128,1024]{1,0:T(8,128)(2,1)S(1)}, bf16[128,1024]{1,0:T(8,128)(2,1)S(1)}, u32[]{:S(2)}, u32[]{:S(2)}) collective-permute-start(bf16[128,1024]{1,0:T(8,128)(2,1)S(1)} %get-tuple-element.58), channel_id=1, source_target_pairs={{0,16},{1,3},{2,18},{3,1},{4,20},{5,7},{6,22},{7,5},{8,24},{9,11},... | collective-permute-start | bytes 786440 | tf_op jit(solution)/shard_map/ppermute | solution.py:348
  139.6 14.0 %collective-permute-start.28 = (bf16[128,1024]{1,0:T(8,128)(2,1)S(1)}, bf16[128,1024]{1,0:T(8,128)(2,1)S(1)}, u32[]{:S(2)}, u32[]{:S(2)}) collective-permute-start(bf16[128,1024]{1,0:T(8,128)(2,1)S(1)} %get-tuple-element.62), channel_id=1, source_target_pairs={{0,16},{1,3},{2,18},{3,1},{4,20},{5,7},{6,22},{7,5},{8,24},{9,11},... | collective-permute-start | bytes 786440 | tf_op jit(solution)/shard_map/ppermute | solution.py:348
  142.4 47.6 %collective-permute-start.41 = (bf16[384,2048]{1,0:T(8,128)(2,1)S(1)}, bf16[384,2048]{1,0:T(8,128)(2,1)S(1)}, u32[]{:S(2)}, u32[]{:S(2)}) collective-permute-start(bf16[384,2048]{1,0:T(8,128)(2,1)S(1)} %get-tuple-element.82), channel_id=1, source_target_pairs={{0,1},{1,0},{2,3},{3,2},{4,5},{5,4},{6,7},{7,6},{8,9},{9,8},{10,11... | collective-permute-start | bytes 4718600 | tf_op jit(solution)/shard_map/ppermute | solution.py:348
  145.2 9.2 %collective-permute-start.13 = (bf16[128,1024]{1,0:T(8,128)(2,1)S(1)}, bf16[128,1024]{1,0:T(8,128)(2,1)S(1)}, u32[]{:S(2)}, u32[]{:S(2)}) collective-permute-start(bf16[128,1024]{1,0:T(8,128)(2,1)S(1)} %add_convert_fusion.6), channel_id=1, source_target_pairs={{0,2},{1,17},{2,0},{3,19},{4,6},{5,21},{6,4},{7,23},{8,10},{9,25},... | collective-permute-start | bytes 786440 | tf_op jit(solution)/shard_map/ppermute | solution.py:348
  148.6 9.7 %collective-permute-start.30 = (bf16[128,1024]{1,0:T(8,128)(2,1)S(1)}, bf16[128,1024]{1,0:T(8,128)(2,1)S(1)}, u32[]{:S(2)}, u32[]{:S(2)}) collective-permute-start(bf16[128,1024]{1,0:T(8,128)(2,1)S(1)} %get-tuple-element.63), channel_id=1, source_target_pairs={{0,16},{1,3},{2,18},{3,1},{4,20},{5,7},{6,22},{7,5},{8,24},{9,11},... | collective-permute-start | bytes 786440 | tf_op jit(solution)/shard_map/ppermute | solution.py:348
  153.6 7.8 %collective-permute-start.21 = (bf16[128,1024]{1,0:T(8,128)(2,1)S(1)}, bf16[128,1024]{1,0:T(8,128)(2,1)S(1)}, u32[]{:S(2)}, u32[]{:S(2)}) collective-permute-start(bf16[128,1024]{1,0:T(8,128)(2,1)S(1)} %add_convert_fusion.4), channel_id=1, source_target_pairs={{0,2},{1,17},{2,0},{3,19},{4,6},{5,21},{6,4},{7,23},{8,10},{9,25},... | collective-permute-start | bytes 786440 | tf_op jit(solution)/shard_map/ppermute | solution.py:348
  154.3 11.2 %collective-permute-start.29 = (bf16[128,1024]{1,0:T(8,128)(2,1)S(1)}, bf16[128,1024]{1,0:T(8,128)(2,1)S(1)}, u32[]{:S(2)}, u32[]{:S(2)}) collective-permute-start(bf16[128,1024]{1,0:T(8,128)(2,1)S(1)} %add_convert_fusion.2), channel_id=1, source_target_pairs={{0,2},{1,17},{2,0},{3,19},{4,6},{5,21},{6,4},{7,23},{8,10},{9,25},... | collective-permute-start | bytes 786440 | tf_op jit(solution)/shard_map/ppermute | solution.py:348
  158.3 10.7 %collective-permute-start.7 = (bf16[128,1024]{1,0:T(8,128)(2,1)S(1)}, bf16[128,1024]{1,0:T(8,128)(2,1)S(1)}, u32[]{:S(2)}, u32[]{:S(2)}) collective-permute-start(bf16[128,1024]{1,0:T(8,128)(2,1)S(1)} %get-tuple-element.48), channel_id=1, source_target_pairs={{0,16},{1,3},{2,18},{3,1},{4,20},{5,7},{6,22},{7,5},{8,24},{9,11},... | collective-permute-start | bytes 786440 | tf_op jit(solution)/shard_map/ppermute | solution.py:348
  161.4 9.5 %collective-permute-start.6 = (bf16[128,1024]{1,0:T(8,128)(2,1)S(1)}, bf16[128,1024]{1,0:T(8,128)(2,1)S(1)}, u32[]{:S(2)}, u32[]{:S(2)}) collective-permute-start(bf16[128,1024]{1,0:T(8,128)(2,1)S(1)} %add_convert_fusion.7), channel_id=1, source_target_pairs={{0,2},{1,17},{2,0},{3,19},{4,6},{5,21},{6,4},{7,23},{8,10},{9,25},... | collective-permute-start | bytes 786440 | tf_op jit(solution)/shard_map/ppermute | solution.py:348
  165.6 9.9 %collective-permute-start.15 = (bf16[128,1024]{1,0:T(8,128)(2,1)S(1)}, bf16[128,1024]{1,0:T(8,128)(2,1)S(1)}, u32[]{:S(2)}, u32[]{:S(2)}) collective-permute-start(bf16[128,1024]{1,0:T(8,128)(2,1)S(1)} %add_convert_fusion.5), channel_id=1, source_target_pairs={{0,12},{1,13},{2,14},{3,15},{4,0},{5,1},{6,2},{7,3},{8,4},{9,5},{1... | collective-permute-start | bytes 786440 | tf_op jit(solution)/shard_map/ppermute | solution.py:348
  169.0 20.0 %collective-permute-start.23 = (bf16[128,1024]{1,0:T(8,128)(2,1)S(1)}, bf16[128,1024]{1,0:T(8,128)(2,1)S(1)}, u32[]{:S(2)}, u32[]{:S(2)}) collective-permute-start(bf16[128,1024]{1,0:T(8,128)(2,1)S(1)} %add_convert_fusion.3), channel_id=1, source_target_pairs={{0,8},{1,9},{2,10},{3,11},{4,12},{5,13},{6,14},{7,15},{8,0},{9,1},... | collective-permute-start | bytes 786440 | tf_op jit(solution)/shard_map/ppermute | solution.py:348
  170.9 18.2 %collective-permute-start.31 = (bf16[128,1024]{1,0:T(8,128)(2,1)S(1)}, bf16[128,1024]{1,0:T(8,128)(2,1)S(1)}, u32[]{:S(2)}, u32[]{:S(2)}) collective-permute-start(bf16[128,1024]{1,0:T(8,128)(2,1)S(1)} %add_convert_fusion.1), channel_id=1, source_target_pairs={{0,4},{1,5},{2,6},{3,7},{4,8},{5,9},{6,10},{7,11},{8,12},{9,13},{1... | collective-permute-start | bytes 786440 | tf_op jit(solution)/shard_map/ppermute | solution.py:348
  (10 other events, 22.3 us)

commit v2 on v1

v2 whole, which is shorter than its diff:
```python
import functools

import jax
import jax.numpy as jnp
from jax import lax
from jax.experimental import pallas as pl
from jax.experimental.pallas import tpu as pltpu
from jax.sharding import PartitionSpec as P


AXES = ("dp", "expert")
CORES = 2
SIDE = 2
GROUP = 2
TILE = 512
F32 = jnp.float32
BF16 = jnp.bfloat16


def exchange_plan(tokens, cotangent, routes, gate_probs, matching, gate_weight, up_weight, down_weight):
    expert_count = lax.axis_size("expert")
    token_count, fan_out = routes.shape
    capacity = max(2, token_count * fan_out * 9 // (8 * expert_count))
    route_count = token_count * fan_out
    mix_weights = gate_probs / jnp.sum(gate_probs, axis=1, keepdims=True)
    flat_routes = routes.reshape(-1)
    expert_hit = flat_routes[:, None] == jnp.arange(matching.shape[0], dtype=jnp.int32)[None, :]
    host_of = jnp.sum(jnp.where(expert_hit, matching[None, :], 0), axis=1)
    host_hit = (host_of[:, None] == jnp.arange(expert_count, dtype=jnp.int32)[None, :]).astype(
        jnp.int32
    )
    running = jnp.cumsum(host_hit, axis=0)
    slot_rank = jnp.sum((running - 1) * host_hit, axis=1)
    position = host_of * capacity + slot_rank
    slot_table = (
        jnp.full((expert_count * capacity,), route_count, jnp.int32)
        .at[position]
        .set(jnp.arange(route_count, dtype=jnp.int32))
    )
    filled = slot_table < route_count
    route_ids = jnp.minimum(slot_table, route_count - 1)
    token_ids = jnp.where(filled, route_ids // fan_out, token_count)
    clamped_ids = route_ids // fan_out
    slot_mix = jnp.where(filled, jnp.take(mix_weights.reshape(-1), route_ids), 0.0)
    recv_rows = lax.all_to_all(
        jnp.take(tokens, token_ids, axis=0, mode="fill", fill_value=0),
        "expert",
        split_axis=0,
        concat_axis=0,
        tiled=True,
    )
    gathered = jnp.take(cotangent, clamped_ids, axis=0)
    recv_cot = lax.all_to_all(
        (slot_mix[:, None] * gathered.astype(jnp.float32)).astype(jnp.bfloat16),
        "expert",
        split_axis=0,
        concat_axis=0,
        tiled=True,
    )
    inputs, out_cot = (
        lax.all_gather(recv_rows, "dp", axis=1, tiled=True),
        lax.all_gather(recv_cot, "dp", axis=1, tiled=True),
    )
    gate_pre = jnp.dot(inputs, gate_weight[0], preferred_element_type=jnp.float32)
    up_pre = jnp.dot(inputs, up_weight[0], preferred_element_type=jnp.float32)
    sigma_gate = jax.nn.sigmoid(gate_pre)
    silu_gate = gate_pre * sigma_gate
    hidden = (silu_gate * up_pre).astype(jnp.bfloat16)
    partial_out = jnp.dot(hidden, down_weight[0], preferred_element_type=jnp.float32)
    contract_rows = (((0,), (0,)), ((), ()))
    down_grad = lax.dot_general(
        hidden, out_cot, contract_rows, preferred_element_type=jnp.float32
    ).astype(jnp.bfloat16)
    hidden_cot = lax.dot_general(
        out_cot, down_weight[0], (((1,), (1,)), ((), ())), preferred_element_type=jnp.float32
    )
    slope = sigma_gate * (1.0 + gate_pre * (1.0 - sigma_gate))
    gate_cot = (hidden_cot * up_pre * slope).astype(jnp.bfloat16)
    up_cot = (hidden_cot * silu_gate).astype(jnp.bfloat16)
    gate_grad = lax.dot_general(
        inputs, gate_cot, contract_rows, preferred_element_type=jnp.float32
    ).astype(jnp.bfloat16)
    up_grad = lax.dot_general(
        inputs, up_cot, contract_rows, preferred_element_type=jnp.float32
    ).astype(jnp.bfloat16)
    summed = lax.psum_scatter(
        partial_out.astype(jnp.bfloat16), "dp", scatter_dimension=1, tiled=True
    )
    merged = lax.all_to_all(summed, "expert", split_axis=0, concat_axis=0, tiled=True)
    half_width = merged.shape[1]
    expert_out = jnp.take(merged, position, axis=0).reshape(token_count, fan_out, half_width)
    layer_out = jnp.sum(mix_weights[:, :, None] * expert_out.astype(jnp.float32), axis=1).astype(
        jnp.bfloat16
    )
    return (layer_out, gate_grad[None], up_grad[None], down_grad[None])


def moves(expert_count):
    depth = expert_count // (SIDE * CORES)

    def table(step):
        pairs = []
        for y in range(2):
            for z in range(depth):
                for x in range(SIDE):
                    for core in range(CORES):
                        ty, tz, tx, tcore = step(y, z, x, core)
                        pairs.append(
                            (
                                y * expert_count + (z * SIDE + x) * CORES + core,
                                ty * expert_count + (tz * SIDE + tx) * CORES + tcore,
                            )
                        )
        return pairs

    shift = {
        by: table(lambda y, z, x, core, by=by: (y, (z + by) % depth, x, core))
        for by in range(1 - depth, depth)
        if by
    }
    swap = table(lambda y, z, x, core: (y, z, x, 1 - core))
    first = table(lambda y, z, x, core: (y, z, 1 - x, core) if core == 0 else (1 - y, z, x, core))
    second = table(lambda y, z, x, core: (1 - y, z, x, core) if core == 0 else (y, z, 1 - x, core))
    return depth, shift, swap, first, second


def dot(a, b):
    return jnp.dot(a, b, preferred_element_type=F32)


def dot_rows(a, b):
    return lax.dot_general(a, b, (((0,), (0,)), ((), ())), preferred_element_type=F32)


def dot_columns(a, b):
    return lax.dot_general(a, b, (((1,), (1,)), ((), ())), preferred_element_type=F32)


def piece_windows(where_ref, member, rows, half):
    y, core = where_ref[0], where_ref[3]

    def window(lower, other):
        side = jnp.where(other == 1, 1 - y, y)
        return (
            pl.ds(pl.multiple_of((2 * member + lower) * rows, rows), rows),
            pl.ds(pl.multiple_of(side * half, half), half),
        )

    return window(0, 0), window(1 - core, core), window(core, 1 - core), window(1, 1)


def row_weights(mix_ref, where_ref, backs, depth, slot):
    core, x = where_ref[3], where_ref[2]
    parity = core if slot == 0 else 1 - core
    lanes = lax.broadcasted_iota(jnp.int32, mix_ref.shape, 1)
    columns = []
    for back in backs:
        z = lax.rem(where_ref[1] + depth - back, depth)
        for across in (x, 1 - x):
            block = (z * SIDE + across) * CORES + core
            hit = lanes == block * CORES + parity
            columns.append(jnp.sum(jnp.where(hit, mix_ref[...], 0.0), axis=1, keepdims=True))
    return jnp.concatenate(columns, axis=0)


def forward_kernel(backs, depth, sets, fresh, where_ref, *refs):
    pieces, refs = refs[: 4 * sets], refs[4 * sets :]
    mix_ref, ins, downs, refs = refs[0], refs[1:3], refs[3:5], refs[5 if fresh else 6 :]
    outs, pre_ref, all_ref, x_buf, o_buf, sem = refs[:4], refs[4], refs[5], refs[6], refs[7], refs[8]
    rows, half = pieces[0].shape[1:]
    member = 0
    for number in range(sets):
        group = pieces[4 * number : 4 * number + 4]
        for inner in range(group[0].shape[0]):
            for window, piece in zip(piece_windows(where_ref, member, rows, half), group):
                x_buf[window] = piece[inner]
            member += 1
    total = 2 * rows * len(backs)
    keep = pltpu.make_async_copy(x_buf, all_ref.at[pl.ds(2 * rows * backs[0], total)], sem)
    keep.start()
    width = ins[0].shape[1]
    units = width // 2
    cut = width * 2 // 3
    for slot in range(CORES):
        pre_ref[:, slot * width : slot * width + cut] = dot(x_buf[...], ins[slot][:, :cut])
    last = dot(x_buf[...], jnp.concatenate([ins[0][:, cut:], ins[1][:, cut:]], axis=1))
    pre_ref[:, cut:width] = last[:, : width - cut]
    pre_ref[:, width + cut :] = last[:, width - cut :]
    hiddens = []
    for slot in range(CORES):
        gate = pre_ref[:, slot * width : slot * width + units]
        up = pre_ref[:, slot * width + units : (slot + 1) * width]
        weights = row_weights(mix_ref, where_ref, backs, depth, slot)
        hiddens.append((weights * (gate * jax.nn.sigmoid(gate) * up)).astype(BF16))
    o_buf[...] = dot(
        jnp.concatenate(hiddens, axis=1), jnp.concatenate([downs[0][...], downs[1][...]], axis=0)
    ).astype(BF16)
    for member in range(len(backs)):
        for window, ref in zip(piece_windows(where_ref, member, rows, half), outs):
            ref[member] = o_buf[window]
    keep.wait()


def forward(backs, depth, where, sets, mix, ins, downs, rows_all):
    rows, half = sets[0][0].shape[1:]
    width = ins[0].shape[1]
    total = 2 * rows * len(backs)
    fresh = rows_all is None
    flat = [piece for pieces in sets for piece in pieces]
    vmem = pl.BlockSpec(memory_space=pltpu.VMEM)
    hbm = pl.BlockSpec(memory_space=pl.ANY)
    return pl.pallas_call(
        functools.partial(forward_kernel, backs, depth, len(sets), fresh),
        out_shape=tuple([jax.ShapeDtypeStruct((len(backs), rows, half), BF16)] * 4)
        + (
            jax.ShapeDtypeStruct((total, CORES * width), F32),
            jax.ShapeDtypeStruct((depth * 2 * rows, 2 * half), BF16),
        ),
        in_specs=[pl.BlockSpec(memory_space=pltpu.SMEM)]
        + [vmem] * (len(flat) + 5)
        + ([] if fresh else [hbm]),
        out_specs=(vmem,) * 5 + (hbm,),
        input_output_aliases={} if fresh else {len(flat) + 6: 5},
        scratch_shapes=[
            pltpu.VMEM((total, 2 * half), BF16),
            pltpu.VMEM((total, 2 * half), BF16),
            pltpu.SemaphoreType.DMA,
        ],
        compiler_params=pltpu.CompilerParams(vmem_limit_bytes=20 << 20),
        cost_estimate=pl.CostEstimate(
            flops=2 * total * half * width * 6, bytes_accessed=12 * total * half, transcendentals=total * width
        ),
    )(where, *flat, mix, *ins, *downs, *([] if fresh else [rows_all]))


def backward_kernel(backs, depth, fresh, where_ref, *refs):
    count = len(backs)
    pairs, fars, refs = refs[:count], refs[count : 2 * count], refs[2 * count :]
    pre_ref, mix_ref, downs, refs = refs[0], refs[1], refs[2:4], refs[4 if fresh else 7 :]
    cot_all, hid_all, pre_all, c_buf, h_buf, g_buf, sems = refs
    rows, half = pairs[0].shape[1:]
    total = 2 * rows * count
    for member in range(count):
        pieces = (pairs[member].at[0], pairs[member].at[1], fars[member].at[0], fars[member].at[1])
        for window, piece in zip(piece_windows(where_ref, member, rows, half), pieces):
            c_buf[window] = piece[...]
    at = pl.ds(2 * rows * backs[0], total)
    copies = [pltpu.make_async_copy(c_buf, cot_all.at[at], sems.at[CORES, 0])]
    copies[0].start()
    width = pre_ref.shape[1] // 2
    units = width // 2
    for slot in range(CORES):
        weights = row_weights(mix_ref, where_ref, backs, depth, slot)
        hidden_cot = weights * dot_columns(c_buf[...], downs[slot][...])
        gate = pre_ref[:, slot * width : slot * width + units]
        up = pre_ref[:, slot * width + units : (slot + 1) * width]
        sigma = jax.nn.sigmoid(gate)
        silu = gate * sigma
        h_buf[slot] = (weights * (silu * up)).astype(BF16)
        slope = sigma * (1.0 + gate * (1.0 - sigma))
        g_buf[slot, :, :units] = (hidden_cot * up * slope).astype(BF16)
        g_buf[slot, :, units:] = (hidden_cot * silu).astype(BF16)
        for number, (buf, to) in enumerate(((h_buf, hid_all), (g_buf, pre_all))):
            copies.append(pltpu.make_async_copy(buf.at[slot], to.at[slot, at], sems.at[slot, number]))
            copies[-1].start()
    for copy in copies:
        copy.wait()


def backward(backs, depth, where, pairs, fars, pre, mix, downs, kept):
    rows, half = pairs[0].shape[1:]
    width = pre.shape[1] // 2
    total = 2 * rows * len(backs)
    every = 2 * rows * depth
    fresh = kept is None
    first = 2 * len(backs) + 5
    vmem = pl.BlockSpec(memory_space=pltpu.VMEM)
    hbm = pl.BlockSpec(memory_space=pl.ANY)
    return pl.pallas_call(
        functools.partial(backward_kernel, backs, depth, fresh),
        out_shape=(
            jax.ShapeDtypeStruct((every, 2 * half), BF16),
            jax.ShapeDtypeStruct((CORES, every, width // 2), BF16),
            jax.ShapeDtypeStruct((CORES, every, width), BF16),
        ),
        in_specs=[pl.BlockSpec(memory_space=pltpu.SMEM)]
        + [vmem] * (first - 1)
        + ([] if fresh else [hbm] * 3),
        out_specs=(hbm,) * 3,
        input_output_aliases={} if fresh else {first: 0, first + 1: 1, first + 2: 2},
        scratch_shapes=[
            pltpu.VMEM((total, 2 * half), BF16),
            pltpu.VMEM((CORES, total, width // 2), BF16),
            pltpu.VMEM((CORES, total, width), BF16),
            pltpu.SemaphoreType.DMA((CORES + 1, 2)),
        ],
        compiler_params=pltpu.CompilerParams(vmem_limit_bytes=16 << 20),
        cost_estimate=pl.CostEstimate(
            flops=2 * total * half * width * 2, bytes_accessed=20 * total * half, transcendentals=total * width
        ),
    )(where, *pairs, *fars, pre, mix, *downs, *([] if fresh else kept))


def in_grads_kernel(rows_ref, pre_ref, *refs):
    grads = dot_rows(rows_ref[...], pre_ref[0])
    if len(refs) == 1:
        refs[0][...] = grads.astype(BF16)
        return
    got, gate_ref, up_ref = refs
    grads += got[...].astype(F32)
    units = gate_ref.shape[1]
    gate_ref[...] = grads[:, :units].astype(BF16)
    up_ref[...] = grads[:, units:].astype(BF16)


def down_grads_kernel(cot_ref, hid_ref, *refs):
    grads = dot_rows(hid_ref[0], cot_ref[...])
    if len(refs) == 2:
        grads += refs[0][...].astype(F32)
    refs[-1][...] = grads.astype(BF16)


def in_grads(slot, rows_all, pre_all, got=None):
    total, features = rows_all.shape
    width = pre_all.shape[2]
    tile = min(TILE, features)

    def tall(columns):
        return pl.BlockSpec((tile, columns), lambda i: (i, 0))

    columns = (width,) if got is None else (width // 2, width // 2)
    return pl.pallas_call(
        in_grads_kernel,
        grid=(features // tile,),
        out_shape=tuple(jax.ShapeDtypeStruct((features, some), BF16) for some in columns),
        in_specs=[
            pl.BlockSpec((total, tile), lambda i: (0, i)),
            pl.BlockSpec((1, total, width), lambda i: (slot, 0, 0)),
        ]
        + ([] if got is None else [tall(width)]),
        out_specs=tuple(tall(some) for some in columns),
        compiler_params=pltpu.CompilerParams(vmem_limit_bytes=20 << 20),
        cost_estimate=pl.CostEstimate(
            flops=2 * total * features * width, bytes_accessed=2 * features * (total + width), transcendentals=0
        ),
    )(rows_all, pre_all, *([] if got is None else [got]))


def down_grads(slot, cot_all, hid_all, got=None):
    total, features = cot_all.shape
    units = hid_all.shape[2]
    tile = min(TILE, features)
    flat = pl.BlockSpec((units, tile), lambda i: (0, i))
    return pl.pallas_call(
        down_grads_kernel,
        grid=(features // tile,),
        out_shape=jax.ShapeDtypeStruct((units, features), BF16),
        in_specs=[
            pl.BlockSpec((total, tile), lambda i: (0, i)),
            pl.BlockSpec((1, total, units), lambda i: (slot, 0, 0)),
        ]
        + ([] if got is None else [flat]),
        out_specs=flat,
        compiler_params=pltpu.CompilerParams(vmem_limit_bytes=16 << 20),
        cost_estimate=pl.CostEstimate(
            flops=2 * total * features * units, bytes_accessed=2 * features * (total + units), transcendentals=0
        ),
    )(cot_all, hid_all, *([] if got is None else [got]))


def gather_plan(tokens, cotangent, routes, gate_probs, matching, gate_weight, up_weight, down_weight):
    expert_count = lax.axis_size("expert")
    depth, shift, swap, first, second = moves(expert_count)

    def send(value, pairs):
        return lax.ppermute(value, AXES, pairs)

    y, at = lax.axis_index("dp"), lax.axis_index("expert")
    where = jnp.stack([y, at // (SIDE * CORES), (at // CORES) % SIDE, at % CORES]).astype(jnp.int32)

    down = down_weight[0]
    downs = (down, send(down, swap))
    in_weight = jnp.concatenate([gate_weight[0], up_weight[0]], axis=1)
    ins = (in_weight, send(in_weight, swap))

    groups = [tuple(range(at, min(at + GROUP, depth))) for at in range(0, depth, GROUP)]

    along = [tokens]
    for _ in range(1, depth):
        along.append(send(along[-1], shift[1]))
    around = []
    for piece in along:
        piece = piece[None]
        a = send(piece, first)
        b = send(piece, second)
        d = send(a, second)
        around.append((piece, a, b, d))
    sets = [[around[back] for back in backs] for backs in groups]

    pairs = [jnp.stack([cotangent, send(cotangent, first)])]
    for _ in range(1, depth):
        pairs.append(send(pairs[-1], shift[1]))
    fars = [send(pair, second) for pair in pairs]

    mix = gate_probs / jnp.sum(gate_probs, axis=1, keepdims=True)
    hit = routes[:, :, None] == jnp.arange(matching.shape[0], dtype=jnp.int32)
    host = jnp.sum(jnp.where(hit, matching, 0), axis=2)
    slots = jnp.arange(expert_count, dtype=jnp.int32)
    slots = (slots[:, None] // CORES * CORES + jnp.arange(CORES, dtype=jnp.int32)).reshape(-1)
    per_slot = jnp.sum(jnp.where(host[None] == slots[:, None, None], mix[None], 0.0), axis=2)
    mix = lax.all_to_all(per_slot, "expert", split_axis=0, concat_axis=0, tiled=True)
    mix = mix.T

    rows_all, pres, out = None, [], None
    for number, backs in enumerate(groups):
        *got, pre, rows_all = forward(
            backs, depth, where, sets[number], mix, ins, downs, rows_all
        )
        pres.append(pre)
        own, a, b, d = got
        d = send(d, second)
        b = send(b, second)
        a = (a.astype(F32) + d).astype(BF16)
        a = send(a, first)
        own = own.astype(F32) + a + b
        for member, back in enumerate(backs):
            part = own[member]
            if back:
                part = send(part.astype(BF16), shift[-back]).astype(F32)
            out = part if out is None else out + part

    kept = None
    for number, backs in enumerate(groups):
        some = slice(backs[0], backs[-1] + 1)
        kept = backward(
            backs, depth, where, pairs[some], fars[some], pres[number], mix, downs, kept
        )
    cot_all, hid_all, pre_all = kept
    (in_got,) = in_grads(1, rows_all, pre_all)
    in_got = send(in_got, swap)
    down_got = down_grads(1, cot_all, hid_all)
    down_got = send(down_got, swap)
    gate_grad, up_grad = in_grads(0, rows_all, pre_all, in_got)
    down_grad = down_grads(0, cot_all, hid_all, down_got)
    out = out.astype(BF16)
    return out, gate_grad[None], up_grad[None], down_grad[None]


def solution(mesh):
    experts = mesh.shape["expert"]
    square = mesh.shape["dp"] == 2 and experts % (SIDE * CORES) == 0

    def on_device(*args):
        dense = 2 * args[2].shape[1] >= experts
        if not (square and dense):
            return exchange_plan(*args)
        return gather_plan(*args)

    placed = (
        P("expert", "dp"),
        P("expert", "dp"),
        P("expert", None),
        P("expert", None),
        P(),
        P("expert", None, "dp"),
        P("expert", None, "dp"),
        P("expert", "dp", None),
    )
    return jax.shard_map(
        on_device,
        mesh=mesh,
        in_specs=placed,
        out_specs=(
            P("expert", "dp"),
            P("expert", None, "dp"),
            P("expert", None, "dp"),
            P("expert", "dp", None),
        ),
        check_vma=False,
    )
```

time: 199 us -> 177 us (0.89)
  the two profiles are of different devices: /device:TPU:0 before, /device:TPU:9 now
where the time goes in v2:
time: 177 us; the launch traced here: 176 us
  waiting for transfers between devices  63.2 us (36%)
  starting transfers between devices  48.8 us (28%)
  Pallas kernels  44.6 us (25%)
  local copies, waits for them, and re-layouts  11.1 us (6%)
  other arithmetic  7.48 us (4%)
    ppermute x36, waiting for transfers between devices, send(): return lax.ppermute(value, AXES, pairs)  60.7 us
    ppermute x36, starting transfers between devices, send(): return lax.ppermute(value, AXES, pairs)  35.5 us
    pallas_call x2, Pallas kernels, forward(): pl.pallas_call(functools.partial(forward_kernel, backs, depth, len(sets),...  17.4 us
    all_to_all x1, starting transfers between devices, gather_plan(): lax.all_to_all(per_slot, 'expert', split_axis=0, concat_axis=0, tiled=True)  13.3 us
    unnamed x40, local copies, waits for them, and re-layouts  10.9 us
    pallas_call x2, Pallas kernels, backward(): pl.pallas_call(functools.partial(backward_kernel, backs, depth, fresh), o...  10.7 us
    pallas_call x2, Pallas kernels, in_grads(): pl.pallas_call(in_grads_kernel, grid=(features // tile,), out_shape=tuple...  9.91 us
    pallas_call x2, Pallas kernels, down_grads(): pl.pallas_call(down_grads_kernel, grid=(features // tile,), out_shape=jax...  6.59 us
  transfers between devices with their start and end apart: 37, of which 15 were waited for; matrix products, arithmetic and copies ran while one was open for 2% of the time, Pallas kernels for 17%

profile of v2, /device:TPU:9, one launch (start us, length us, event | category | flops | bytes accessed | tf_op | source)
XLA Modules:
  0.0 176.1 jit_solution(7070735881359677013)
XLA Ops:
  0.7 3.9 %pad_maximum_fusion.refs_9_ = bf16[2048,768]{1,0:T(8,128)(2,1)} fusion(bf16[2048,384]{1,0:T(8,128)(2,1)} %bitcast.50, bf16[2048,384]{1,0:T(8,128)(2,1)} %bitcast.51), kind=kLoop, calls=%fused_computation | loop fusion | flops 6291456 | bytes 6291456 | tf_op jit(solution)/shard_map/concatenate | solution.py:383
  5.3 1.2 collective-permute-start
  6.5 1.3 collective-permute-start.3
  7.8 1.2 collective-permute-start.1
  9.3 1.5 collective-permute-done.refs_1_
  10.8 1.4 collective-permute-start.2
  12.9 1.2 collective-permute-done.3
  15.8 2.2 %collective-permute-start.8 = (bf16[384,2048]{1,0:T(8,128)(2,1)S(1)}, bf16[384,2048]{1,0:T(8,128)(2,1)S(1)}, u32[]{:S(2)}, u32[]{:S(2)}) collective-permute-start(bf16[384,2048]{1,0:T(8,128)(2,1)S(1)} %bitcast.35), channel_id=1, source_target_pairs={{0,1},{1,0},{2,3},{3,2},{4,5},{5,4},{6,7},{7,6},{8,9},{9,8},{10,11... | collective-permute-start | bytes 4718600 | tf_op jit(solution)/shard_map/ppermute | solution.py:376
  18.5 2.1 %collective-permute-done.2.refs_3_ = bf16[1,128,1024]{2,1,0:T(8,128)(2,1)S(1)} collective-permute-done((bf16[1,128,1024]{2,1,0:T(8,128)(2,1)S(1)}, bf16[1,128,1024]{2,1,0:T(8,128)(2,1)S(1)}, u32[]{:S(2)}, u32[]{:S(2)}) %collective-permute-start.2) | collective-permute-done | bytes 262176 | tf_op jit(solution)/shard_map/ppermute | solution.py:376
  21.3 1.3 collective-permute-start.13
  23.3 1.2 collective-permute-start.6
  26.0 1.3 collective-permute-start.27
  27.3 1.7 collective-permute-start.14
  29.7 1.2 collective-permute-start.15
  30.9 3.9 %collective-permute-done.14.refs_1_ = bf16[1,128,1024]{2,1,0:T(8,128)(2,1)} collective-permute-done((bf16[1,128,1024]{2,1,0:T(8,128)(2,1)}, bf16[1,128,1024]{2,1,0:T(8,128)(2,1)}, u32[]{:S(2)}, u32[]{:S(2)}) %collective-permute-start.14) | collective-permute-done | bytes 262176 | tf_op jit(solution)/shard_map/ppermute | solution.py:376
  35.3 1.4 collective-permute-done.15.refs_2_
  36.8 1.3 collective-permute-start.17
  39.5 4.9 %collective-permute-done.17 = bf16[128,1024]{1,0:T(8,128)(2,1)} collective-permute-done((bf16[128,1024]{1,0:T(8,128)(2,1)}, bf16[128,1024]{1,0:T(8,128)(2,1)}, u32[]{:S(2)}, u32[]{:S(2)}) %collective-permute-start.17) | collective-permute-done | bytes 262176 | tf_op jit(solution)/shard_map/ppermute | solution.py:376
  46.1 13.3 %all-to-all-start = ((f32[16,2,128]{2,1,0:T(2,128)}), f32[16,2,128]{2,1,0:T(2,128)S(1)}, u32[]{:S(2)}, u32[]{:S(2)}) async-start(f32[16,2,128]{2,1,0:T(2,128)} %bitcast.6), calls=%async_computation | async-start | bytes 32768 | tf_op jit(solution)/shard_map/all_to_all | solution.py:411
  59.3 1.3 collective-permute-start.33
  60.6 1.2 collective-permute-start.29
  61.9 2.5 %all-to-all-done = f32[16,2,128]{2,1,0:T(2,128)S(1)} async-done(((f32[16,2,128]{2,1,0:T(2,128)}), f32[16,2,128]{2,1,0:T(2,128)S(1)}, u32[]{:S(2)}, u32[]{:S(2)}) %all-to-all-start) | async-done | bytes 16416 | tf_op jit(solution)/shard_map/all_to_all | solution.py:411
  64.9 1.2 collective-permute-start.16
  66.4 0.9 copy-done.3
  67.3 0.9 copy-done.5
  68.3 0.9 copy-done.7
  69.2 0.9 copy-done.9
  73.0 8.6 %shard_map.111 = (bf16[2,128,1024]{2,1,0:T(8,128)(2,1)S(1)}, bf16[2,128,1024]{2,1,0:T(8,128)(2,1)S(1)}, bf16[2,128,1024]{2,1,0:T(8,128)(2,1)S(1)}, bf16[2,128,10...) custom-call(s32[4]{0:T(128)S(1)} %pad_add_fusion.where_ref, ...), custom_call_target="tpu_custom_call" | custom-call | flops 4831838208 | bytes 6291456 | tf_op jit(solution)/shard_map/pallas_call | solution.py:212
  81.6 1.2 collective-permute-start.30
  83.2 5.4 %shard_map.113 = (bf16[1024,2048]{1,0:T(8,128)(2,1)S(1)}, bf16[2,1024,384]{2,1,0:T(8,128)(2,1)S(1)}, bf16[2,1024,768]{2,1,0:T(8,128)(2,1)S(1)}) custom-call(s32[4]{0:T(128)S(1)} %pad_add_fusion.where_ref, bf16[2,128,1024]{2,1,0:T(8,128)(2,1)} %pad_maximum_fusion.1.refs_0_, bf16[2,128,1024]{2,1,0:T(8,128)(2,1)} %collective-permute-done.27.refs_1_, ...), custom_call_target="tpu_custom_call" | custom-call | flops 1610612736 | bytes 10485760 | tf_op jit(solution)/shard_map/pallas_call | solution.py:279
  88.6 8.8 %shard_map.112 = (bf16[2,128,1024]{2,1,0:T(8,128)(2,1)S(1)}, bf16[2,128,1024]{2,1,0:T(8,128)(2,1)S(1)}, bf16[2,128,1024]{2,1,0:T(8,128)(2,1)S(1)}, bf16[2,128,10...) custom-call(s32[4]{0:T(128)S(1)} %pad_add_fusion.where_ref, ...), custom_call_target="tpu_custom_call", output_to_operand_aliasing={{5}: (14, {})} | custom-call | flops 4831838208 | bytes 6291456 | tf_op jit(solution)/shard_map/pallas_call | solution.py:212
  97.4 5.3 %shard_map.114 = (bf16[1024,2048]{1,0:T(8,128)(2,1)S(1)}, bf16[2,1024,384]{2,1,0:T(8,128)(2,1)S(1)}, bf16[2,1024,768]{2,1,0:T(8,128)(2,1)S(1)}) custom-call(s32[4]{0:T(128)S(1)} %pad_add_fusion.where_ref, bf16[2,128,1024]{2,1,0:T(8,128)(2,1)} %collective-permute-done.28.refs_0_, ...), custom_call_target="tpu_custom_call", output_to_operand_aliasing={{0}: (9, {}), {1}: (10, {}), {2}: (11, {})} | custom-call | flops 1610612736 | bytes 10485760 | tf_op jit(solution)/shard_map/pallas_call | solution.py:279
  102.7 4.5 %shard_map.115 = bf16[2048,768]{1,0:T(8,128)(2,1)S(1)} custom-call(bf16[1024,2048]{1,0:T(8,128)(2,1)S(1)} %get-tuple-element.33.rows_ref, bf16[2,1024,768]{2,1,0:T(8,128)(2,1)S(1)} %get-tuple-element.39.pre_ref), custom_call_target="tpu_custom_call" | custom-call | flops 3221225472 | bytes 7340032 | tf_op jit(solution)/shard_map/pallas_call | solution.py:332
  107.2 2.1 %collective-permute-start.34 = (bf16[2048,768]{1,0:T(8,128)(2,1)S(1)}, bf16[2048,768]{1,0:T(8,128)(2,1)S(1)}, u32[]{:S(2)}, u32[]{:S(2)}) collective-permute-start(bf16[2048,768]{1,0:T(8,128)(2,1)S(1)} %shard_map.115), channel_id=1, source_target_pairs={{0,1},{1,0},{2,3},{3,2},{4,5},{5,4},{6,7},{7,6},{8,9},{9,8},{10,11... | collective-permute-start | bytes 9437192 | tf_op jit(solution)/shard_map/ppermute | solution.py:376
  109.7 1.2 collective-permute-start.9
  111.1 6.6 %collective-permute-done.21 = bf16[2,128,1024]{2,1,0:T(8,128)(2,1)S(1)} collective-permute-done((bf16[2,128,1024]{2,1,0:T(8,128)(2,1)S(1)}, bf16[2,128,1024]{2,1,0:T(8,128)(2,1)S(1)}, u32[]{:S(2)}, u32[]{:S(2)}) %collective-permute-start.21) | collective-permute-done | bytes 524320 | tf_op jit(solution)/shard_map/ppermute | solution.py:376
  117.9 1.0 collective-permute-start.22
  119.2 5.4 %collective-permute-done.9 = bf16[2,128,1024]{2,1,0:T(8,128)(2,1)S(1)} collective-permute-done((bf16[2,128,1024]{2,1,0:T(8,128)(2,1)S(1)}, bf16[2,128,1024]{2,1,0:T(8,128)(2,1)S(1)}, u32[]{:S(2)}, u32[]{:S(2)}) %collective-permute-start.9) | collective-permute-done | bytes 524320 | tf_op jit(solution)/shard_map/ppermute | solution.py:376
  124.8 1.0 collective-permute-start.10
  125.7 2.9 %shard_map.117 = bf16[384,2048]{1,0:T(8,128)(2,1)S(1)} custom-call(bf16[1024,2048]{1,0:T(8,128)(2,1)S(1)} %get-tuple-element.42.cot_ref, bf16[2,1024,384]{2,1,0:T(8,128)(2,1)S(1)} %get-tuple-element.43.hid_ref), custom_call_target="tpu_custom_call" | custom-call | flops 1610612736 | bytes 5767168 | tf_op jit(solution)/shard_map/pallas_call | solution.py:354
  128.6 7.2 %collective-permute-done.23 = bf16[2,128,1024]{2,1,0:T(8,128)(2,1)S(1)} collective-permute-done((bf16[2,128,1024]{2,1,0:T(8,128)(2,1)S(1)}, bf16[2,128,1024]{2,1,0:T(8,128)(2,1)S(1)}, u32[]{:S(2)}, u32[]{:S(2)}) %collective-permute-start.23) | collective-permute-done | bytes 524320 | tf_op jit(solution)/shard_map/ppermute | solution.py:376
  135.8 2.9 %collective-permute-start.35 = (bf16[384,2048]{1,0:T(8,128)(2,1)S(1)}, bf16[384,2048]{1,0:T(8,128)(2,1)S(1)}, u32[]{:S(2)}, u32[]{:S(2)}) collective-permute-start(bf16[384,2048]{1,0:T(8,128)(2,1)S(1)} %shard_map.117), channel_id=1, source_target_pairs={{0,1},{1,0},{2,3},{3,2},{4,5},{5,4},{6,7},{7,6},{8,9},{9,8},{10,11... | collective-permute-start | bytes 4718600 | tf_op jit(solution)/shard_map/ppermute | solution.py:376
  139.4 6.4 %collective-permute-done.11 = bf16[2,128,1024]{2,1,0:T(8,128)(2,1)S(1)} collective-permute-done((bf16[2,128,1024]{2,1,0:T(8,128)(2,1)S(1)}, bf16[2,128,1024]{2,1,0:T(8,128)(2,1)S(1)}, u32[]{:S(2)}, u32[]{:S(2)}) %collective-permute-start.11) | collective-permute-done | bytes 524320 | tf_op jit(solution)/shard_map/ppermute | solution.py:376
  146.4 1.2 collective-permute-start.12
  147.7 14.8 %collective-permute-done.24 = bf16[128,1024]{1,0:T(8,128)(2,1)S(1)} collective-permute-done((bf16[128,1024]{1,0:T(8,128)(2,1)S(1)}, bf16[128,1024]{1,0:T(8,128)(2,1)S(1)}, u32[]{:S(2)}, u32[]{:S(2)}) %collective-permute-start.24) | collective-permute-done | bytes 262176 | tf_op jit(solution)/shard_map/ppermute | solution.py:376
  162.5 3.7 %collective-permute-done.12 = bf16[128,1024]{1,0:T(8,128)(2,1)S(1)} collective-permute-done((bf16[128,1024]{1,0:T(8,128)(2,1)S(1)}, bf16[128,1024]{1,0:T(8,128)(2,1)S(1)}, u32[]{:S(2)}, u32[]{:S(2)}) %collective-permute-start.12) | collective-permute-done | bytes 262176 | tf_op jit(solution)/shard_map/ppermute | solution.py:376
  167.0 3.7 %shard_map.118 = bf16[384,2048]{1,0:T(8,128)(2,1)} custom-call(bf16[1024,2048]{1,0:T(8,128)(2,1)S(1)} %get-tuple-element.42.cot_ref, bf16[2,1024,384]{2,1,0:T(8,128)(2,1)S(1)} %get-tuple-element.43.hid_ref, bf16[384,2048]{1,0:T(8,128)(2,1)S(1)} %collective-permute-done.35.refs_0_), custom_call_target="tpu_custom_call" | custom-call | flops 1610612736 | bytes 5767168 | tf_op jit(solution)/shard_map/pallas_call | solution.py:354
  170.7 5.4 %shard_map.116 = (bf16[2048,384]{1,0:T(8,128)(2,1)}, bf16[2048,384]{1,0:T(8,128)(2,1)}) custom-call(bf16[1024,2048]{1,0:T(8,128)(2,1)S(1)} %get-tuple-element.33.rows_ref, bf16[2,1024,768]{2,1,0:T(8,128)(2,1)S(1)} %get-tuple-element.39.pre_ref, bf16[2048,768]{1,0:T(8,128)(2,1)S(1)} %collective-permute-done.34.refs_0_), custom_call_target="tpu_custom_call" | custom-call | flops 3221225472 | bytes 7340032 | tf_op jit(solution)/shard_map/pallas_call | solution.py:332
  (92 shorter events, 18.6 us)
Async XLA Ops:
  0.6 4.6 %copy-start.1 = (bf16[128,1024]{1,0:T(8,128)(2,1)S(1)}, bf16[128,1024]{1,0:T(8,128)(2,1)}, u32[]{:S(2)}) copy-start(bf16[128,1024]{1,0:T(8,128)(2,1)} %param.8) | copy-start | bytes 786436
  0.6 8.4 %copy-start.16 = (bf16[128,1024]{1,0:T(8,128)(2,1)S(1)}, bf16[128,1024]{1,0:T(8,128)(2,1)}, u32[]{:S(2)}) copy-start(bf16[128,1024]{1,0:T(8,128)(2,1)} %param.9) | copy-start | bytes 786436
  0.7 15.1 %copy-start = (bf16[1,384,2048]{2,1,0:T(8,128)(2,1)S(1)}, bf16[1,384,2048]{2,1,0:T(8,128)(2,1)}, u32[]{:S(2)}) copy-start(bf16[1,384,2048]{2,1,0:T(8,128)(2,1)} %param.15) | copy-start | bytes 4718596
  0.7 30.2 %copy-start.17 = (f32[128,8]{0,1:T(8,128)S(1)}, f32[128,8]{0,1:T(8,128)}, u32[]{:S(2)}) copy-start(f32[128,8]{0,1:T(8,128)} %param.11) | copy-start | bytes 12292
  0.7 44.5 %copy-start.18 = (s32[128,8]{0,1:T(8,128)S(1)}, s32[128,8]{0,1:T(8,128)}, u32[]{:S(2)}) copy-start(s32[128,8]{0,1:T(8,128)} %param.10) | copy-start | bytes 12292
  0.7 44.5 %copy-start.19 = (s32[16]{0:T(128)S(1)}, s32[16]{0:T(128)}, u32[]{:S(2)}) copy-start(s32[16]{0:T(128)} %param.12) | copy-start | bytes 196
  4.6 61.5 %collective-permute-start.7 = (bf16[2048,768]{1,0:T(8,128)(2,1)}, bf16[2048,768]{1,0:T(8,128)(2,1)}, u32[]{:S(2)}, u32[]{:S(2)}) collective-permute-start(bf16[2048,768]{1,0:T(8,128)(2,1)} %pad_maximum_fusion.refs_9_), channel_id=1, source_target_pairs={{0,1},{1,0},{2,3},{3,2},{4,5},{5,4},{6,7},{7,6},{8,9},{9,8},{10,11... | collective-permute-start | bytes 9437192 | tf_op jit(solution)/shard_map/ppermute | solution.py:376
  5.3 5.5 %collective-permute-start = (bf16[1,128,1024]{2,1,0:T(8,128)(2,1)S(1)}, bf16[1,128,1024]{2,1,0:T(8,128)(2,1)S(1)}, u32[]{:S(2)}, u32[]{:S(2)}) collective-permute-start(bf16[1,128,1024]{2,1,0:T(8,128)(2,1)S(1)} %bitcast.44), channel_id=1, source_target_pairs={{0,2},{1,17},{2,0},{3,19},{4,6},{5,21},{6,4},{7,23},{8,10},{9,25},... | collective-permute-start | bytes 786440 | tf_op jit(solution)/shard_map/ppermute | solution.py:376
  6.5 7.6 %collective-permute-start.3 = (bf16[128,1024]{1,0:T(8,128)(2,1)S(1)}, bf16[128,1024]{1,0:T(8,128)(2,1)S(1)}, u32[]{:S(2)}, u32[]{:S(2)}) collective-permute-start(bf16[128,1024]{1,0:T(8,128)(2,1)S(1)} %copy-done.1), channel_id=1, source_target_pairs={{0,4},{1,5},{2,6},{3,7},{4,8},{5,9},{6,10},{7,11},{8,12},{9,13},{1... | collective-permute-start | bytes 786440 | tf_op jit(solution)/shard_map/ppermute | solution.py:376
  7.8 7.3 %collective-permute-start.1 = (bf16[1,128,1024]{2,1,0:T(8,128)(2,1)S(1)}, bf16[1,128,1024]{2,1,0:T(8,128)(2,1)S(1)}, u32[]{:S(2)}, u32[]{:S(2)}) collective-permute-start(bf16[1,128,1024]{2,1,0:T(8,128)(2,1)S(1)} %bitcast.45), channel_id=1, source_target_pairs={{0,16},{1,3},{2,18},{3,1},{4,20},{5,7},{6,22},{7,5},{8,24},{9,11},... | collective-permute-start | bytes 786440 | tf_op jit(solution)/shard_map/ppermute | solution.py:376
  9.0 9.0 %collective-permute-start.26 = (bf16[128,1024]{1,0:T(8,128)(2,1)S(1)}, bf16[128,1024]{1,0:T(8,128)(2,1)S(1)}, u32[]{:S(2)}, u32[]{:S(2)}) collective-permute-start(bf16[128,1024]{1,0:T(8,128)(2,1)S(1)} %copy-done.16), channel_id=1, source_target_pairs={{0,2},{1,17},{2,0},{3,19},{4,6},{5,21},{6,4},{7,23},{8,10},{9,25},... | collective-permute-start | bytes 786440 | tf_op jit(solution)/shard_map/ppermute | solution.py:376
  10.8 9.8 %collective-permute-start.2 = (bf16[1,128,1024]{2,1,0:T(8,128)(2,1)S(1)}, bf16[1,128,1024]{2,1,0:T(8,128)(2,1)S(1)}, u32[]{:S(2)}, u32[]{:S(2)}) collective-permute-start(bf16[1,128,1024]{2,1,0:T(8,128)(2,1)S(1)} %collective-permute-done.refs_1_), channel_id=1, source_target_pairs={{0,16},{1,3},{2,18},{3,1},{4,20},{5,7},{6,22},{7,5},{8,24},{9,11},... | collective-permute-start | bytes 786440 | tf_op jit(solution)/shard_map/ppermute | solution.py:376
  14.1 9.2 %collective-permute-start.4 = (bf16[1,128,1024]{2,1,0:T(8,128)(2,1)S(1)}, bf16[1,128,1024]{2,1,0:T(8,128)(2,1)S(1)}, u32[]{:S(2)}, u32[]{:S(2)}) collective-permute-start(bf16[1,128,1024]{2,1,0:T(8,128)(2,1)S(1)} %bitcast.47), channel_id=1, source_target_pairs={{0,2},{1,17},{2,0},{3,19},{4,6},{5,21},{6,4},{7,23},{8,10},{9,25},... | collective-permute-start | bytes 786440 | tf_op jit(solution)/shard_map/ppermute | solution.py:376
  15.8 49.1 %collective-permute-start.8 = (bf16[384,2048]{1,0:T(8,128)(2,1)S(1)}, bf16[384,2048]{1,0:T(8,128)(2,1)S(1)}, u32[]{:S(2)}, u32[]{:S(2)}) collective-permute-start(bf16[384,2048]{1,0:T(8,128)(2,1)S(1)} %bitcast.35), channel_id=1, source_target_pairs={{0,1},{1,0},{2,3},{3,2},{4,5},{5,4},{6,7},{7,6},{8,9},{9,8},{10,11... | collective-permute-start | bytes 4718600 | tf_op jit(solution)/shard_map/ppermute | solution.py:376
  18.0 7.3 %collective-permute-start.5 = (bf16[1,128,1024]{2,1,0:T(8,128)(2,1)S(1)}, bf16[1,128,1024]{2,1,0:T(8,128)(2,1)S(1)}, u32[]{:S(2)}, u32[]{:S(2)}) collective-permute-start(bf16[1,128,1024]{2,1,0:T(8,128)(2,1)S(1)} %bitcast.48), channel_id=1, source_target_pairs={{0,16},{1,3},{2,18},{3,1},{4,20},{5,7},{6,22},{7,5},{8,24},{9,11},... | collective-permute-start | bytes 786440 | tf_op jit(solution)/shard_map/ppermute | solution.py:376
  21.3 6.0 %collective-permute-start.13 = (bf16[128,1024]{1,0:T(8,128)(2,1)S(1)}, bf16[128,1024]{1,0:T(8,128)(2,1)}, u32[]{:S(2)}, u32[]{:S(2)}) collective-permute-start(bf16[128,1024]{1,0:T(8,128)(2,1)S(1)} %collective-permute-done.3), channel_id=1, source_target_pairs={{0,4},{1,5},{2,6},{3,7},{4,8},{5,9},{6,10},{7,11},{8,12},{9,13},{1... | collective-permute-start | bytes 786440 | tf_op jit(solution)/shard_map/ppermute | solution.py:376
  23.3 4.0 %copy-start.10 = (bf16[1,128,1024]{2,1,0:T(8,128)(2,1)}, bf16[1,128,1024]{2,1,0:T(8,128)(2,1)S(1)}, u32[]{:S(2)}) copy-start(bf16[1,128,1024]{2,1,0:T(8,128)(2,1)S(1)} %collective-permute-done.4.refs_5_) | copy-start | bytes 786436
  23.3 5.7 %collective-permute-start.6 = (bf16[1,128,1024]{2,1,0:T(8,128)(2,1)S(1)}, bf16[1,128,1024]{2,1,0:T(8,128)(2,1)S(1)}, u32[]{:S(2)}, u32[]{:S(2)}) collective-permute-start(bf16[1,128,1024]{2,1,0:T(8,128)(2,1)S(1)} %collective-permute-done.4.refs_5_), channel_id=1, source_target_pairs={{0,16},{1,3},{2,18},{3,1},{4,20},{5,7},{6,22},{7,5},{8,24},{9,11},... | collective-permute-start | bytes 786440 | tf_op jit(solution)/shard_map/ppermute | solution.py:376
  26.0 12.6 %collective-permute-start.27 = (bf16[2,128,1024]{2,1,0:T(8,128)(2,1)}, bf16[2,128,1024]{2,1,0:T(8,128)(2,1)}, u32[]{:S(2)}, u32[]{:S(2)}) collective-permute-start(bf16[2,128,1024]{2,1,0:T(8,128)(2,1)} %pad_maximum_fusion.1.refs_0_), channel_id=1, source_target_pairs={{0,4},{1,5},{2,6},{3,7},{4,8},{5,9},{6,10},{7,11},{8,12},{9,13},{1... | collective-permute-start | bytes 1572872 | tf_op jit(solution)/shard_map/ppermute | solution.py:376
  27.3 7.5 %collective-permute-start.14 = (bf16[1,128,1024]{2,1,0:T(8,128)(2,1)}, bf16[1,128,1024]{2,1,0:T(8,128)(2,1)}, u32[]{:S(2)}, u32[]{:S(2)}) collective-permute-start(bf16[1,128,1024]{2,1,0:T(8,128)(2,1)} %bitcast.14.refs_0_), channel_id=1, source_target_pairs={{0,2},{1,17},{2,0},{3,19},{4,6},{5,21},{6,4},{7,23},{8,10},{9,25},... | collective-permute-start | bytes 786440 | tf_op jit(solution)/shard_map/ppermute | solution.py:376
  29.7 7.1 %collective-permute-start.15 = (bf16[1,128,1024]{2,1,0:T(8,128)(2,1)}, bf16[1,128,1024]{2,1,0:T(8,128)(2,1)}, u32[]{:S(2)}, u32[]{:S(2)}) collective-permute-start(bf16[1,128,1024]{2,1,0:T(8,128)(2,1)} %bitcast.14.refs_0_), channel_id=1, source_target_pairs={{0,16},{1,3},{2,18},{3,1},{4,20},{5,7},{6,22},{7,5},{8,24},{9,11},... | collective-permute-start | bytes 786440 | tf_op jit(solution)/shard_map/ppermute | solution.py:376
  34.8 24.5 %collective-permute-start.32 = (bf16[2,128,1024]{2,1,0:T(8,128)(2,1)}, bf16[2,128,1024]{2,1,0:T(8,128)(2,1)}, u32[]{:S(2)}, u32[]{:S(2)}) collective-permute-start(bf16[2,128,1024]{2,1,0:T(8,128)(2,1)} %pad_maximum_fusion.1.refs_0_), channel_id=1, source_target_pairs={{0,16},{1,3},{2,18},{3,1},{4,20},{5,7},{6,22},{7,5},{8,24},{9,11},... | collective-permute-start | bytes 1572872 | tf_op jit(solution)/shard_map/ppermute | solution.py:376
  36.8 7.6 %collective-permute-start.17 = (bf16[128,1024]{1,0:T(8,128)(2,1)}, bf16[128,1024]{1,0:T(8,128)(2,1)}, u32[]{:S(2)}, u32[]{:S(2)}) collective-permute-start(bf16[128,1024]{1,0:T(8,128)(2,1)} %collective-permute-done.13), channel_id=1, source_target_pairs={{0,4},{1,5},{2,6},{3,7},{4,8},{5,9},{6,10},{7,11},{8,12},{9,13},{1... | collective-permute-start | bytes 786440 | tf_op jit(solution)/shard_map/ppermute | solution.py:376
  38.7 21.9 %collective-permute-start.28 = (bf16[2,128,1024]{2,1,0:T(8,128)(2,1)}, bf16[2,128,1024]{2,1,0:T(8,128)(2,1)}, u32[]{:S(2)}, u32[]{:S(2)}) collective-permute-start(bf16[2,128,1024]{2,1,0:T(8,128)(2,1)} %collective-permute-done.27.refs_1_), channel_id=1, source_target_pairs={{0,4},{1,5},{2,6},{3,7},{4,8},{5,9},{6,10},{7,11},{8,12},{9,13},{1... | collective-permute-start | bytes 1572872 | tf_op jit(solution)/shard_map/ppermute | solution.py:376
  44.3 20.2 %collective-permute-start.18 = (bf16[1,128,1024]{2,1,0:T(8,128)(2,1)}, bf16[1,128,1024]{2,1,0:T(8,128)(2,1)}, u32[]{:S(2)}, u32[]{:S(2)}) collective-permute-start(bf16[1,128,1024]{2,1,0:T(8,128)(2,1)} %bitcast.15.refs_4_), channel_id=1, source_target_pairs={{0,2},{1,17},{2,0},{3,19},{4,6},{5,21},{6,4},{7,23},{8,10},{9,25},... | collective-permute-start | bytes 786440 | tf_op jit(solution)/shard_map/ppermute | solution.py:376
  46.1 18.3 %all-to-all-start = ((f32[16,2,128]{2,1,0:T(2,128)}), f32[16,2,128]{2,1,0:T(2,128)S(1)}, u32[]{:S(2)}, u32[]{:S(2)}) async-start(f32[16,2,128]{2,1,0:T(2,128)} %bitcast.6), calls=%async_computation | async-start | bytes 32768 | tf_op jit(solution)/shard_map/all_to_all | solution.py:411
  59.3 22.3 %collective-permute-start.33 = (bf16[2,128,1024]{2,1,0:T(8,128)(2,1)}, bf16[2,128,1024]{2,1,0:T(8,128)(2,1)}, u32[]{:S(2)}, u32[]{:S(2)}) collective-permute-start(bf16[2,128,1024]{2,1,0:T(8,128)(2,1)} %collective-permute-done.27.refs_1_), channel_id=1, source_target_pairs={{0,16},{1,3},{2,18},{3,1},{4,20},{5,7},{6,22},{7,5},{8,24},{9,11},... | collective-permute-start | bytes 1572872 | tf_op jit(solution)/shard_map/ppermute | solution.py:376
  60.6 22.3 %collective-permute-start.29 = (bf16[2,128,1024]{2,1,0:T(8,128)(2,1)}, bf16[2,128,1024]{2,1,0:T(8,128)(2,1)}, u32[]{:S(2)}, u32[]{:S(2)}) collective-permute-start(bf16[2,128,1024]{2,1,0:T(8,128)(2,1)} %collective-permute-done.28.refs_0_), channel_id=1, source_target_pairs={{0,4},{1,5},{2,6},{3,7},{4,8},{5,9},{6,10},{7,11},{8,12},{9,13},{1... | collective-permute-start | bytes 1572872 | tf_op jit(solution)/shard_map/ppermute | solution.py:376
  64.5 24.1 %collective-permute-start.19 = (bf16[1,128,1024]{2,1,0:T(8,128)(2,1)}, bf16[1,128,1024]{2,1,0:T(8,128)(2,1)S(1)}, u32[]{:S(2)}, u32[]{:S(2)}) collective-permute-start(bf16[1,128,1024]{2,1,0:T(8,128)(2,1)} %bitcast.15.refs_4_), channel_id=1, source_target_pairs={{0,16},{1,3},{2,18},{3,1},{4,20},{5,7},{6,22},{7,5},{8,24},{9,11},... | collective-permute-start | bytes 786440 | tf_op jit(solution)/shard_map/ppermute | solution.py:376
  64.9 23.7 %collective-permute-start.16 = (bf16[1,128,1024]{2,1,0:T(8,128)(2,1)}, bf16[1,128,1024]{2,1,0:T(8,128)(2,1)S(1)}, u32[]{:S(2)}, u32[]{:S(2)}) collective-permute-start(bf16[1,128,1024]{2,1,0:T(8,128)(2,1)} %collective-permute-done.14.refs_1_), channel_id=1, source_target_pairs={{0,16},{1,3},{2,18},{3,1},{4,20},{5,7},{6,22},{7,5},{8,24},{9,11},... | collective-permute-start | bytes 786440 | tf_op jit(solution)/shard_map/ppermute | solution.py:376
  66.0 22.6 %collective-permute-start.20 = (bf16[1,128,1024]{2,1,0:T(8,128)(2,1)}, bf16[1,128,1024]{2,1,0:T(8,128)(2,1)S(1)}, u32[]{:S(2)}, u32[]{:S(2)}) collective-permute-start(bf16[1,128,1024]{2,1,0:T(8,128)(2,1)} %collective-permute-done.18.refs_5_), channel_id=1, source_target_pairs={{0,16},{1,3},{2,18},{3,1},{4,20},{5,7},{6,22},{7,5},{8,24},{9,11},... | collective-permute-start | bytes 786440 | tf_op jit(solution)/shard_map/ppermute | solution.py:376
  66.4 0.9 copy-start.3
  67.3 0.9 copy-start.5
  68.3 0.9 copy-start.7
  69.2 0.9 copy-start.9
  81.6 15.7 %collective-permute-start.30 = (bf16[2,128,1024]{2,1,0:T(8,128)(2,1)}, bf16[2,128,1024]{2,1,0:T(8,128)(2,1)S(1)}, u32[]{:S(2)}, u32[]{:S(2)}) collective-permute-start(bf16[2,128,1024]{2,1,0:T(8,128)(2,1)} %collective-permute-done.28.refs_0_), channel_id=1, source_target_pairs={{0,16},{1,3},{2,18},{3,1},{4,20},{5,7},{6,22},{7,5},{8,24},{9,11},... | collective-permute-start | bytes 1572872 | tf_op jit(solution)/shard_map/ppermute | solution.py:376
  82.9 14.5 %collective-permute-start.31 = (bf16[2,128,1024]{2,1,0:T(8,128)(2,1)}, bf16[2,128,1024]{2,1,0:T(8,128)(2,1)S(1)}, u32[]{:S(2)}, u32[]{:S(2)}) collective-permute-start(bf16[2,128,1024]{2,1,0:T(8,128)(2,1)} %collective-permute-done.29.refs_1_), channel_id=1, source_target_pairs={{0,16},{1,3},{2,18},{3,1},{4,20},{5,7},{6,22},{7,5},{8,24},{9,11},... | collective-permute-start | bytes 1572872 | tf_op jit(solution)/shard_map/ppermute | solution.py:376
  107.2 63.5 %collective-permute-start.34 = (bf16[2048,768]{1,0:T(8,128)(2,1)S(1)}, bf16[2048,768]{1,0:T(8,128)(2,1)S(1)}, u32[]{:S(2)}, u32[]{:S(2)}) collective-permute-start(bf16[2048,768]{1,0:T(8,128)(2,1)S(1)} %shard_map.115), channel_id=1, source_target_pairs={{0,1},{1,0},{2,3},{3,2},{4,5},{5,4},{6,7},{7,6},{8,9},{9,8},{10,11... | collective-permute-start | bytes 9437192 | tf_op jit(solution)/shard_map/ppermute | solution.py:376
  109.4 8.3 %collective-permute-start.21 = (bf16[2,128,1024]{2,1,0:T(8,128)(2,1)S(1)}, bf16[2,128,1024]{2,1,0:T(8,128)(2,1)S(1)}, u32[]{:S(2)}, u32[]{:S(2)}) collective-permute-start(bf16[2,128,1024]{2,1,0:T(8,128)(2,1)S(1)} %get-tuple-element.31), channel_id=1, source_target_pairs={{0,16},{1,3},{2,18},{3,1},{4,20},{5,7},{6,22},{7,5},{8,24},{9,11},... | collective-permute-start | bytes 1572872 | tf_op jit(solution)/shard_map/ppermute | solution.py:376
  109.7 14.9 %collective-permute-start.9 = (bf16[2,128,1024]{2,1,0:T(8,128)(2,1)S(1)}, bf16[2,128,1024]{2,1,0:T(8,128)(2,1)S(1)}, u32[]{:S(2)}, u32[]{:S(2)}) collective-permute-start(bf16[2,128,1024]{2,1,0:T(8,128)(2,1)S(1)} %get-tuple-element.26), channel_id=1, source_target_pairs={{0,16},{1,3},{2,18},{3,1},{4,20},{5,7},{6,22},{7,5},{8,24},{9,11},... | collective-permute-start | bytes 1572872 | tf_op jit(solution)/shard_map/ppermute | solution.py:376
  110.8 25.0 %collective-permute-start.23 = (bf16[2,128,1024]{2,1,0:T(8,128)(2,1)S(1)}, bf16[2,128,1024]{2,1,0:T(8,128)(2,1)S(1)}, u32[]{:S(2)}, u32[]{:S(2)}) collective-permute-start(bf16[2,128,1024]{2,1,0:T(8,128)(2,1)S(1)} %get-tuple-element.32), channel_id=1, source_target_pairs={{0,16},{1,3},{2,18},{3,1},{4,20},{5,7},{6,22},{7,5},{8,24},{9,11},... | collective-permute-start | bytes 1572872 | tf_op jit(solution)/shard_map/ppermute | solution.py:376
  117.9 20.8 %collective-permute-start.22 = (bf16[2,128,1024]{2,1,0:T(8,128)(2,1)S(1)}, bf16[2,128,1024]{2,1,0:T(8,128)(2,1)S(1)}, u32[]{:S(2)}, u32[]{:S(2)}) collective-permute-start(bf16[2,128,1024]{2,1,0:T(8,128)(2,1)S(1)} %add_convert_fusion.1), channel_id=1, source_target_pairs={{0,2},{1,17},{2,0},{3,19},{4,6},{5,21},{6,4},{7,23},{8,10},{9,25},... | collective-permute-start | bytes 1572872 | tf_op jit(solution)/shard_map/ppermute | solution.py:376
  118.9 26.9 %collective-permute-start.11 = (bf16[2,128,1024]{2,1,0:T(8,128)(2,1)S(1)}, bf16[2,128,1024]{2,1,0:T(8,128)(2,1)S(1)}, u32[]{:S(2)}, u32[]{:S(2)}) collective-permute-start(bf16[2,128,1024]{2,1,0:T(8,128)(2,1)S(1)} %get-tuple-element.27), channel_id=1, source_target_pairs={{0,16},{1,3},{2,18},{3,1},{4,20},{5,7},{6,22},{7,5},{8,24},{9,11},... | collective-permute-start | bytes 1572872 | tf_op jit(solution)/shard_map/ppermute | solution.py:376
  124.8 21.3 %collective-permute-start.10 = (bf16[2,128,1024]{2,1,0:T(8,128)(2,1)S(1)}, bf16[2,128,1024]{2,1,0:T(8,128)(2,1)S(1)}, u32[]{:S(2)}, u32[]{:S(2)}) collective-permute-start(bf16[2,128,1024]{2,1,0:T(8,128)(2,1)S(1)} %add_convert_fusion.2), channel_id=1, source_target_pairs={{0,2},{1,17},{2,0},{3,19},{4,6},{5,21},{6,4},{7,23},{8,10},{9,25},... | collective-permute-start | bytes 1572872 | tf_op jit(solution)/shard_map/ppermute | solution.py:376
  135.8 31.2 %collective-permute-start.35 = (bf16[384,2048]{1,0:T(8,128)(2,1)S(1)}, bf16[384,2048]{1,0:T(8,128)(2,1)S(1)}, u32[]{:S(2)}, u32[]{:S(2)}) collective-permute-start(bf16[384,2048]{1,0:T(8,128)(2,1)S(1)} %shard_map.117), channel_id=1, source_target_pairs={{0,1},{1,0},{2,3},{3,2},{4,5},{5,4},{6,7},{7,6},{8,9},{9,8},{10,11... | collective-permute-start | bytes 4718600 | tf_op jit(solution)/shard_map/ppermute | solution.py:376
  139.0 8.7 %collective-permute-start.25 = (bf16[128,1024]{1,0:T(8,128)(2,1)S(1)}, bf16[128,1024]{1,0:T(8,128)(2,1)S(1)}, u32[]{:S(2)}, u32[]{:S(2)}) collective-permute-start(bf16[128,1024]{1,0:T(8,128)(2,1)S(1)} %get-tuple-element.45), channel_id=1, source_target_pairs={{0,4},{1,5},{2,6},{3,7},{4,8},{5,9},{6,10},{7,11},{8,12},{9,13},{1... | collective-permute-start | bytes 786440 | tf_op jit(solution)/shard_map/ppermute | solution.py:376
  145.8 16.7 %collective-permute-start.24 = (bf16[128,1024]{1,0:T(8,128)(2,1)S(1)}, bf16[128,1024]{1,0:T(8,128)(2,1)S(1)}, u32[]{:S(2)}, u32[]{:S(2)}) collective-permute-start(bf16[128,1024]{1,0:T(8,128)(2,1)S(1)} %get-tuple-element.44), channel_id=1, source_target_pairs={{0,8},{1,9},{2,10},{3,11},{4,12},{5,13},{6,14},{7,15},{8,0},{9,1},... | collective-permute-start | bytes 786440 | tf_op jit(solution)/shard_map/ppermute | solution.py:376
  146.4 19.7 %collective-permute-start.12 = (bf16[128,1024]{1,0:T(8,128)(2,1)S(1)}, bf16[128,1024]{1,0:T(8,128)(2,1)S(1)}, u32[]{:S(2)}, u32[]{:S(2)}) collective-permute-start(bf16[128,1024]{1,0:T(8,128)(2,1)S(1)} %fusion.4), channel_id=1, source_target_pairs={{0,12},{1,13},{2,14},{3,15},{4,0},{5,1},{6,2},{7,3},{8,4},{9,5},{1... | collective-permute-start | bytes 786440 | tf_op jit(solution)/shard_map/ppermute | solution.py:376
  (9 other events, 7.1 us)

commit v3 on v2

--- a/solution.py
+++ b/solution.py
@@ -12,6 +12,7 @@
 CORES = 2
 SIDE = 2
 GROUP = 2
+ALONG = {3: -1}
 TILE = 512
 F32 = jnp.float32
 BF16 = jnp.bfloat16
@@ -152,21 +153,23 @@
 def row_weights(mix_ref, where_ref, backs, depth, slot):
     core, x = where_ref[3], where_ref[2]
     parity = core if slot == 0 else 1 - core
-    lanes = lax.broadcasted_iota(jnp.int32, mix_ref.shape, 1)
+    rows = mix_ref.shape[1]
+    down = lax.broadcasted_iota(jnp.int32, (rows, rows), 0)
+    along = lax.broadcasted_iota(jnp.int32, (rows, rows), 1)
     columns = []
     for back in backs:
         z = lax.rem(where_ref[1] + depth - back, depth)
         for across in (x, 1 - x):
             block = (z * SIDE + across) * CORES + core
-            hit = lanes == block * CORES + parity
-            columns.append(jnp.sum(jnp.where(hit, mix_ref[...], 0.0), axis=1, keepdims=True))
+            row = mix_ref[pl.ds(block * CORES + parity, 1), :]
+            columns.append(jnp.sum(jnp.where(down == along, row, 0.0), axis=1, keepdims=True))
     return jnp.concatenate(columns, axis=0)
 
 
-def forward_kernel(backs, depth, sets, fresh, where_ref, *refs):
+def forward_kernel(backs, depth, sets, where_ref, *refs):
     pieces, refs = refs[: 4 * sets], refs[4 * sets :]
-    mix_ref, ins, downs, refs = refs[0], refs[1:3], refs[3:5], refs[5 if fresh else 6 :]
-    outs, pre_ref, all_ref, x_buf, o_buf, sem = refs[:4], refs[4], refs[5], refs[6], refs[7], refs[8]
+    mix_ref, ins, downs, refs = refs[0], refs[1:3], refs[3:5], refs[5:]
+    outs, pre_ref, rows_ref, x_buf, o_buf, sem = refs[:4], refs[4], refs[5], refs[6], refs[7], refs[8]
     rows, half = pieces[0].shape[1:]
     member = 0
     for number in range(sets):
@@ -175,8 +178,7 @@
             for window, piece in zip(piece_windows(where_ref, member, rows, half), group):
                 x_buf[window] = piece[inner]
             member += 1
-    total = 2 * rows * len(backs)
-    keep = pltpu.make_async_copy(x_buf, all_ref.at[pl.ds(2 * rows * backs[0], total)], sem)
+    keep = pltpu.make_async_copy(x_buf, rows_ref, sem)
     keep.start()
     width = ins[0].shape[1]
     units = width // 2
@@ -201,51 +203,45 @@
     keep.wait()
 
 
-def forward(backs, depth, where, sets, mix, ins, downs, rows_all):
+def forward(backs, depth, where, sets, mix, ins, downs):
     rows, half = sets[0][0].shape[1:]
     width = ins[0].shape[1]
     total = 2 * rows * len(backs)
-    fresh = rows_all is None
     flat = [piece for pieces in sets for piece in pieces]
     vmem = pl.BlockSpec(memory_space=pltpu.VMEM)
     hbm = pl.BlockSpec(memory_space=pl.ANY)
     return pl.pallas_call(
-        functools.partial(forward_kernel, backs, depth, len(sets), fresh),
+        functools.partial(forward_kernel, backs, depth, len(sets)),
         out_shape=tuple([jax.ShapeDtypeStruct((len(backs), rows, half), BF16)] * 4)
         + (
             jax.ShapeDtypeStruct((total, CORES * width), F32),
-            jax.ShapeDtypeStruct((depth * 2 * rows, 2 * half), BF16),
-        ),
-        in_specs=[pl.BlockSpec(memory_space=pltpu.SMEM)]
-        + [vmem] * (len(flat) + 5)
-        + ([] if fresh else [hbm]),
+            jax.ShapeDtypeStruct((total, 2 * half), BF16),
+        ),
+        in_specs=[pl.BlockSpec(memory_space=pltpu.SMEM)] + [vmem] * (len(flat) + 5),
         out_specs=(vmem,) * 5 + (hbm,),
-        input_output_aliases={} if fresh else {len(flat) + 6: 5},
         scratch_shapes=[
             pltpu.VMEM((total, 2 * half), BF16),
             pltpu.VMEM((total, 2 * half), BF16),
             pltpu.SemaphoreType.DMA,
         ],
-        compiler_params=pltpu.CompilerParams(vmem_limit_bytes=20 << 20),
+        compiler_params=pltpu.CompilerParams(vmem_limit_bytes=14 << 20),
         cost_estimate=pl.CostEstimate(
             flops=2 * total * half * width * 6, bytes_accessed=12 * total * half, transcendentals=total * width
         ),
-    )(where, *flat, mix, *ins, *downs, *([] if fresh else [rows_all]))
-
-
-def backward_kernel(backs, depth, fresh, where_ref, *refs):
+    )(where, *flat, mix, *ins, *downs)
+
+
+def backward_kernel(backs, depth, where_ref, *refs):
     count = len(backs)
     pairs, fars, refs = refs[:count], refs[count : 2 * count], refs[2 * count :]
-    pre_ref, mix_ref, downs, refs = refs[0], refs[1], refs[2:4], refs[4 if fresh else 7 :]
-    cot_all, hid_all, pre_all, c_buf, h_buf, g_buf, sems = refs
+    pre_ref, mix_ref, downs, refs = refs[0], refs[1], refs[2:4], refs[4:]
+    cot_ref, hid_ref, both_ref, c_buf, h_buf, g_buf, sems = refs
     rows, half = pairs[0].shape[1:]
-    total = 2 * rows * count
     for member in range(count):
         pieces = (pairs[member].at[0], pairs[member].at[1], fars[member].at[0], fars[member].at[1])
         for window, piece in zip(piece_windows(where_ref, member, rows, half), pieces):
             c_buf[window] = piece[...]
-    at = pl.ds(2 * rows * backs[0], total)
-    copies = [pltpu.make_async_copy(c_buf, cot_all.at[at], sems.at[CORES, 0])]
+    copies = [pltpu.make_async_copy(c_buf, cot_ref, sems.at[CORES, 0])]
     copies[0].start()
     width = pre_ref.shape[1] // 2
     units = width // 2
@@ -260,112 +256,99 @@
         slope = sigma * (1.0 + gate * (1.0 - sigma))
         g_buf[slot, :, :units] = (hidden_cot * up * slope).astype(BF16)
         g_buf[slot, :, units:] = (hidden_cot * silu).astype(BF16)
-        for number, (buf, to) in enumerate(((h_buf, hid_all), (g_buf, pre_all))):
-            copies.append(pltpu.make_async_copy(buf.at[slot], to.at[slot, at], sems.at[slot, number]))
+        for number, (buf, to) in enumerate(((h_buf, hid_ref), (g_buf, both_ref))):
+            copies.append(pltpu.make_async_copy(buf.at[slot], to.at[slot], sems.at[slot, number]))
             copies[-1].start()
     for copy in copies:
         copy.wait()
 
 
-def backward(backs, depth, where, pairs, fars, pre, mix, downs, kept):
+def backward(backs, depth, where, pairs, fars, pre, mix, downs):
     rows, half = pairs[0].shape[1:]
     width = pre.shape[1] // 2
     total = 2 * rows * len(backs)
-    every = 2 * rows * depth
-    fresh = kept is None
-    first = 2 * len(backs) + 5
     vmem = pl.BlockSpec(memory_space=pltpu.VMEM)
     hbm = pl.BlockSpec(memory_space=pl.ANY)
     return pl.pallas_call(
-        functools.partial(backward_kernel, backs, depth, fresh),
+        functools.partial(backward_kernel, backs, depth),
         out_shape=(
-            jax.ShapeDtypeStruct((every, 2 * half), BF16),
-            jax.ShapeDtypeStruct((CORES, every, width // 2), BF16),
-            jax.ShapeDtypeStruct((CORES, every, width), BF16),
-        ),
-        in_specs=[pl.BlockSpec(memory_space=pltpu.SMEM)]
-        + [vmem] * (first - 1)
-        + ([] if fresh else [hbm] * 3),
+            jax.ShapeDtypeStruct((total, 2 * half), BF16),
+            jax.ShapeDtypeStruct((CORES, total, width // 2), BF16),
+            jax.ShapeDtypeStruct((CORES, total, width), BF16),
+        ),
+        in_specs=[pl.BlockSpec(memory_space=pltpu.SMEM)] + [vmem] * (2 * len(backs) + 4),
         out_specs=(hbm,) * 3,
-        input_output_aliases={} if fresh else {first: 0, first + 1: 1, first + 2: 2},
         scratch_shapes=[
             pltpu.VMEM((total, 2 * half), BF16),
             pltpu.VMEM((CORES, total, width // 2), BF16),
             pltpu.VMEM((CORES, total, width), BF16),
             pltpu.SemaphoreType.DMA((CORES + 1, 2)),
         ],
-        compiler_params=pltpu.CompilerParams(vmem_limit_bytes=16 << 20),
+        compiler_params=pltpu.CompilerParams(vmem_limit_bytes=12 << 20),
         cost_estimate=pl.CostEstimate(
             flops=2 * total * half * width * 2, bytes_accessed=20 * total * half, transcendentals=total * width
         ),
-    )(where, *pairs, *fars, pre, mix, *downs, *([] if fresh else kept))
-
-
-def in_grads_kernel(rows_ref, pre_ref, *refs):
-    grads = dot_rows(rows_ref[...], pre_ref[0])
-    if len(refs) == 1:
-        refs[0][...] = grads.astype(BF16)
-        return
-    got, gate_ref, up_ref = refs
-    grads += got[...].astype(F32)
-    units = gate_ref.shape[1]
-    gate_ref[...] = grads[:, :units].astype(BF16)
-    up_ref[...] = grads[:, units:].astype(BF16)
-
-
-def down_grads_kernel(cot_ref, hid_ref, *refs):
-    grads = dot_rows(hid_ref[0], cot_ref[...])
-    if len(refs) == 2:
-        grads += refs[0][...].astype(F32)
-    refs[-1][...] = grads.astype(BF16)
-
-
-def in_grads(slot, rows_all, pre_all, got=None):
-    total, features = rows_all.shape
-    width = pre_all.shape[2]
+    )(where, *pairs, *fars, pre, mix, *downs)
+
+
+def grads_kernel(added, left_ref, right_ref, *refs):
+    left = left_ref[...] if left_ref.ndim == 2 else left_ref[0]
+    right = right_ref[...] if right_ref.ndim == 2 else right_ref[0]
+    grads = dot_rows(left, right)
+    for ref in refs[:added]:
+        grads += ref[...].astype(F32)
+    outs = refs[added:]
+    columns = outs[0].shape[1]
+    for number, ref in enumerate(outs):
+        ref[...] = grads[:, number * columns : (number + 1) * columns].astype(ref.dtype)
+
+
+def in_grads(slot, rows_ref, both, add, kinds):
+    total, features = rows_ref.shape
+    width = both.shape[2]
     tile = min(TILE, features)
 
     def tall(columns):
         return pl.BlockSpec((tile, columns), lambda i: (i, 0))
 
-    columns = (width,) if got is None else (width // 2, width // 2)
+    columns = width // len(kinds)
     return pl.pallas_call(
-        in_grads_kernel,
+        functools.partial(grads_kernel, len(add)),
         grid=(features // tile,),
-        out_shape=tuple(jax.ShapeDtypeStruct((features, some), BF16) for some in columns),
+        out_shape=tuple(jax.ShapeDtypeStruct((features, columns), kind) for kind in kinds),
         in_specs=[
             pl.BlockSpec((total, tile), lambda i: (0, i)),
             pl.BlockSpec((1, total, width), lambda i: (slot, 0, 0)),
         ]
-        + ([] if got is None else [tall(width)]),
-        out_specs=tuple(tall(some) for some in columns),
+        + [tall(width)] * len(add),
+        out_specs=tuple(tall(columns) for _ in kinds),
         compiler_params=pltpu.CompilerParams(vmem_limit_bytes=20 << 20),
         cost_estimate=pl.CostEstimate(
             flops=2 * total * features * width, bytes_accessed=2 * features * (total + width), transcendentals=0
         ),
-    )(rows_all, pre_all, *([] if got is None else [got]))
-
-
-def down_grads(slot, cot_all, hid_all, got=None):
-    total, features = cot_all.shape
-    units = hid_all.shape[2]
+    )(rows_ref, both, *add)
+
+
+def down_grads(slot, cot, hid, add, kind):
+    total, features = cot.shape
+    units = hid.shape[2]
     tile = min(TILE, features)
     flat = pl.BlockSpec((units, tile), lambda i: (0, i))
     return pl.pallas_call(
-        down_grads_kernel,
+        functools.partial(grads_kernel, len(add)),
         grid=(features // tile,),
-        out_shape=jax.ShapeDtypeStruct((units, features), BF16),
+        out_shape=(jax.ShapeDtypeStruct((units, features), kind),),
         in_specs=[
+            pl.BlockSpec((1, total, units), lambda i: (slot, 0, 0)),
             pl.BlockSpec((total, tile), lambda i: (0, i)),
-            pl.BlockSpec((1, total, units), lambda i: (slot, 0, 0)),
         ]
-        + ([] if got is None else [flat]),
-        out_specs=flat,
+        + [flat] * len(add),
+        out_specs=(flat,),
         compiler_params=pltpu.CompilerParams(vmem_limit_bytes=16 << 20),
         cost_estimate=pl.CostEstimate(
             flops=2 * total * features * units, bytes_accessed=2 * features * (total + units), transcendentals=0
         ),
-    )(cot_all, hid_all, *([] if got is None else [got]))
+    )(hid, cot, *add)
 
 
 def gather_plan(tokens, cotangent, routes, gate_probs, matching, gate_weight, up_weight, down_weight):
@@ -375,6 +358,7 @@
     def send(value, pairs):
         return lax.ppermute(value, AXES, pairs)
 
+    rows, _ = tokens.shape
     y, at = lax.axis_index("dp"), lax.axis_index("expert")
     where = jnp.stack([y, at // (SIDE * CORES), (at // CORES) % SIDE, at % CORES]).astype(jnp.int32)
 
@@ -398,9 +382,18 @@
     sets = [[around[back] for back in backs] for backs in groups]
 
     pairs = [jnp.stack([cotangent, send(cotangent, first)])]
-    for _ in range(1, depth):
-        pairs.append(send(pairs[-1], shift[1]))
-    fars = [send(pair, second) for pair in pairs]
+    late = depth // 2
+    for back in range(1, depth):
+        if back > late:
+            pairs.append(send(pairs[0], shift[back - depth]))
+        else:
+            pairs.append(send(pairs[-1], shift[1]))
+    fars = []
+    for back, pair in enumerate(pairs):
+        if back in ALONG:
+            fars.append(send(fars[0], shift[ALONG[back]]))
+        else:
+            fars.append(send(pair, second))
 
     mix = gate_probs / jnp.sum(gate_probs, axis=1, keepdims=True)
     hit = routes[:, :, None] == jnp.arange(matching.shape[0], dtype=jnp.int32)
@@ -409,14 +402,13 @@
     slots = (slots[:, None] // CORES * CORES + jnp.arange(CORES, dtype=jnp.int32)).reshape(-1)
     per_slot = jnp.sum(jnp.where(host[None] == slots[:, None, None], mix[None], 0.0), axis=2)
     mix = lax.all_to_all(per_slot, "expert", split_axis=0, concat_axis=0, tiled=True)
-    mix = mix.T
-
-    rows_all, pres, out = None, [], None
+    mix = mix.reshape(CORES * expert_count, rows)
+
+    kept_rows, pres, out = [], [], None
     for number, backs in enumerate(groups):
-        *got, pre, rows_all = forward(
-            backs, depth, where, sets[number], mix, ins, downs, rows_all
-        )
+        *got, pre, kept = forward(backs, depth, where, sets[number], mix, ins, downs)
         pres.append(pre)
+        kept_rows.append(kept)
         own, a, b, d = got
         d = send(d, second)
         b = send(b, second)
@@ -429,19 +421,23 @@
                 part = send(part.astype(BF16), shift[-back]).astype(F32)
             out = part if out is None else out + part
 
-    kept = None
+    in_sums, down_sums = [[], []], [[], []]
     for number, backs in enumerate(groups):
         some = slice(backs[0], backs[-1] + 1)
-        kept = backward(
-            backs, depth, where, pairs[some], fars[some], pres[number], mix, downs, kept
+        cot, hid, both = backward(
+            backs, depth, where, pairs[some], fars[some], pres[number], mix, downs
         )
-    cot_all, hid_all, pre_all = kept
-    (in_got,) = in_grads(1, rows_all, pre_all)
+        if number == len(groups) - 1:
+            break
+        for slot in (1, 0):
+            in_sums[slot] = in_grads(slot, kept_rows[number], both, in_sums[slot], (F32,))
+            down_sums[slot] = down_grads(slot, cot, hid, down_sums[slot], F32)
+    (in_got,) = in_grads(1, kept_rows[-1], both, in_sums[1], (BF16,))
     in_got = send(in_got, swap)
-    down_got = down_grads(1, cot_all, hid_all)
+    (down_got,) = down_grads(1, cot, hid, down_sums[1], BF16)
     down_got = send(down_got, swap)
-    gate_grad, up_grad = in_grads(0, rows_all, pre_all, in_got)
-    down_grad = down_grads(0, cot_all, hid_all, down_got)
+    gate_grad, up_grad = in_grads(0, kept_rows[-1], both, [*in_sums[0], in_got], (BF16, BF16))
+    (down_grad,) = down_grads(0, cot, hid, [*down_sums[0], down_got], BF16)
     out = out.astype(BF16)
     return out, gate_grad[None], up_grad[None], down_grad[None]
 

time: 177 us -> 173 us (0.977)
  the two profiles are of different devices: /device:TPU:9 before, /device:TPU:0 now
where the time goes in v3:
time: 173 us; the launch traced here: 170 us
  waiting for transfers between devices  56.8 us (33%)
  starting transfers between devices  49.8 us (29%)
  Pallas kernels  49 us (28%)
  other arithmetic  8.51 us (5%)
  local copies, waits for them, and re-layouts  5.13 us (3%)
    ppermute x36, waiting for transfers between devices, send(): return lax.ppermute(value, AXES, pairs)  56.5 us
    ppermute x36, starting transfers between devices, send(): return lax.ppermute(value, AXES, pairs)  45.2 us
    pallas_call x2, Pallas kernels, forward(): pl.pallas_call(functools.partial(forward_kernel, backs, depth, len(sets))...  17.7 us
    pallas_call x4, Pallas kernels, in_grads(): pl.pallas_call(functools.partial(grads_kernel, len(add)), grid=(features...  11.9 us
    pallas_call x2, Pallas kernels, backward(): pl.pallas_call(functools.partial(backward_kernel, backs, depth), out_shap...  10.2 us
    pallas_call x4, Pallas kernels, down_grads(): pl.pallas_call(functools.partial(grads_kernel, len(add)), grid=(features...  9.19 us
    unnamed x22, local copies, waits for them, and re-layouts  4.98 us
    all_to_all x1, starting transfers between devices, gather_plan(): lax.all_to_all(per_slot, 'expert', split_axis=0, concat_axis=0, tiled=True)  4.56 us
  transfers between devices with their start and end apart: 37, of which 15 were waited for; matrix products, arithmetic and copies ran while one was open for 3% of the time, Pallas kernels for 22%

profile of v3, /device:TPU:0, one launch (start us, length us, event | category | flops | bytes accessed | tf_op | source)
XLA Modules:
  0.0 170.2 jit_solution(9384556603297472873)
XLA Ops:
  0.7 3.9 %pad_maximum_fusion.refs_9_ = bf16[2048,768]{1,0:T(8,128)(2,1)} fusion(bf16[2048,384]{1,0:T(8,128)(2,1)} %bitcast.47, bf16[2048,384]{1,0:T(8,128)(2,1)} %bitcast.48), kind=kLoop, calls=%fused_computation | loop fusion | flops 6291456 | bytes 6291456 | tf_op jit(solution)/shard_map/concatenate | solution.py:367
  5.1 3.0 %collective-permute-start = (bf16[1,128,1024]{2,1,0:T(8,128)(2,1)S(1)}, bf16[1,128,1024]{2,1,0:T(8,128)(2,1)}, u32[]{:S(2)}, u32[]{:S(2)}) collective-permute-start(bf16[1,128,1024]{2,1,0:T(8,128)(2,1)S(1)} %bitcast.43), channel_id=1, source_target_pairs={{0,2},{1,17},{2,0},{3,19},{4,6},{5,21},{6,4},{7,23},{8,10},{9,25},... | collective-permute-start | bytes 786440 | tf_op jit(solution)/shard_map/ppermute | solution.py:359
  8.1 1.5 collective-permute-start.1
  9.6 1.6 collective-permute-start.3
  11.2 3.3 %collective-permute-done.refs_1_ = bf16[1,128,1024]{2,1,0:T(8,128)(2,1)} collective-permute-done((bf16[1,128,1024]{2,1,0:T(8,128)(2,1)S(1)}, bf16[1,128,1024]{2,1,0:T(8,128)(2,1)}, u32[]{:S(2)}, u32[]{:S(2)}) %collective-permute-start) | collective-permute-done | bytes 262176 | tf_op jit(solution)/shard_map/ppermute | solution.py:359
  14.5 2.5 %collective-permute-start.26 = (bf16[128,1024]{1,0:T(8,128)(2,1)}, bf16[128,1024]{1,0:T(8,128)(2,1)}, u32[]{:S(2)}, u32[]{:S(2)}) collective-permute-start(bf16[128,1024]{1,0:T(8,128)(2,1)} %param.9), channel_id=1, source_target_pairs={{0,2},{1,17},{2,0},{3,19},{4,6},{5,21},{6,4},{7,23},{8,10},{9,25},... | collective-permute-start | bytes 786440 | tf_op jit(solution)/shard_map/ppermute | solution.py:359
  17.7 1.2 collective-permute-start.2
  19.8 4.2 %collective-permute-done.26 = bf16[128,1024]{1,0:T(8,128)(2,1)} collective-permute-done((bf16[128,1024]{1,0:T(8,128)(2,1)}, bf16[128,1024]{1,0:T(8,128)(2,1)}, u32[]{:S(2)}, u32[]{:S(2)}) %collective-permute-start.26) | collective-permute-done | bytes 262176 | tf_op jit(solution)/shard_map/ppermute | solution.py:359
  24.0 2.1 %collective-permute-start.5 = (bf16[1,128,1024]{2,1,0:T(8,128)(2,1)}, bf16[1,128,1024]{2,1,0:T(8,128)(2,1)S(1)}, u32[]{:S(2)}, u32[]{:S(2)}) collective-permute-start(bf16[1,128,1024]{2,1,0:T(8,128)(2,1)} %bitcast.5.refs_4_), channel_id=1, source_target_pairs={{0,16},{1,3},{2,18},{3,1},{4,20},{5,7},{6,22},{7,5},{8,24},{9,11},... | collective-permute-start | bytes 786440 | tf_op jit(solution)/shard_map/ppermute | solution.py:359
  26.5 1.5 collective-permute-start.13
  28.0 1.6 collective-permute-done.4.refs_5_
  29.6 2.0 %collective-permute-start.6 = (bf16[1,128,1024]{2,1,0:T(8,128)(2,1)}, bf16[1,128,1024]{2,1,0:T(8,128)(2,1)S(1)}, u32[]{:S(2)}, u32[]{:S(2)}) collective-permute-start(bf16[1,128,1024]{2,1,0:T(8,128)(2,1)} %collective-permute-done.4.refs_5_), channel_id=1, source_target_pairs={{0,16},{1,3},{2,18},{3,1},{4,20},{5,7},{6,22},{7,5},{8,24},{9,11},... | collective-permute-start | bytes 786440 | tf_op jit(solution)/shard_map/ppermute | solution.py:359
  31.7 1.9 %pad_maximum_fusion.1.refs_0_ = bf16[2,128,1024]{2,1,0:T(8,128)(2,1)} fusion(bf16[1,128,1024]{2,1,0:T(8,128)(2,1)} %bitcast.18, bf16[1,128,1024]{2,1,0:T(8,128)(2,1)} %bitcast.17), kind=kLoop, calls=%fused_computation.11 | loop fusion | flops 262144 | bytes 1048576 | tf_op jit(solution)/shard_map/stack | solution.py:384
  34.3 1.7 %collective-permute-start.27 = (bf16[2,128,1024]{2,1,0:T(8,128)(2,1)}, bf16[2,128,1024]{2,1,0:T(8,128)(2,1)}, u32[]{:S(2)}, u32[]{:S(2)}) collective-permute-start(bf16[2,128,1024]{2,1,0:T(8,128)(2,1)} %pad_maximum_fusion.1.refs_0_), channel_id=1, source_target_pairs={{0,4},{1,5},{2,6},{3,7},{4,8},{5,9},{6,10},{7,11},{8,12},{9,13},{1... | collective-permute-start | bytes 1572872 | tf_op jit(solution)/shard_map/ppermute | solution.py:359
  36.0 1.5 collective-permute-start.14
  38.2 2.2 %collective-permute-start.31 = (bf16[2,128,1024]{2,1,0:T(8,128)(2,1)}, bf16[2,128,1024]{2,1,0:T(8,128)(2,1)}, u32[]{:S(2)}, u32[]{:S(2)}) collective-permute-start(bf16[2,128,1024]{2,1,0:T(8,128)(2,1)} %pad_maximum_fusion.1.refs_0_), channel_id=1, source_target_pairs={{0,16},{1,3},{2,18},{3,1},{4,20},{5,7},{6,22},{7,5},{8,24},{9,11},... | collective-permute-start | bytes 1572872 | tf_op jit(solution)/shard_map/ppermute | solution.py:359
  40.5 5.0 %collective-permute-done.14.refs_1_ = bf16[1,128,1024]{2,1,0:T(8,128)(2,1)} collective-permute-done((bf16[1,128,1024]{2,1,0:T(8,128)(2,1)}, bf16[1,128,1024]{2,1,0:T(8,128)(2,1)}, u32[]{:S(2)}, u32[]{:S(2)}) %collective-permute-start.14) | collective-permute-done | bytes 262176 | tf_op jit(solution)/shard_map/ppermute | solution.py:359
  45.5 1.6 collective-permute-start.17
  48.0 4.6 %all-to-all-start = ((f32[16,2,128]{2,1,0:T(2,128)}), f32[16,2,128]{2,1,0:T(2,128)S(1)}, u32[]{:S(2)}, u32[]{:S(2)}) async-start(f32[16,2,128]{2,1,0:T(2,128)} %bitcast.6), calls=%async_computation | async-start | bytes 32768 | tf_op jit(solution)/shard_map/all_to_all | solution.py:404
  54.8 1.9 %collective-permute-start.18 = (bf16[1,128,1024]{2,1,0:T(8,128)(2,1)}, bf16[1,128,1024]{2,1,0:T(8,128)(2,1)}, u32[]{:S(2)}, u32[]{:S(2)}) collective-permute-start(bf16[1,128,1024]{2,1,0:T(8,128)(2,1)} %bitcast.14.refs_4_), channel_id=1, source_target_pairs={{0,2},{1,17},{2,0},{3,19},{4,6},{5,21},{6,4},{7,23},{8,10},{9,25},... | collective-permute-start | bytes 786440 | tf_op jit(solution)/shard_map/ppermute | solution.py:359
  56.6 1.5 collective-permute-start.28
  59.1 0.9 copy-done.3
  61.9 8.7 %shard_map.111 = (bf16[2,128,1024]{2,1,0:T(8,128)(2,1)S(1)}, bf16[2,128,1024]{2,1,0:T(8,128)(2,1)S(1)}, bf16[2,128,1024]{2,1,0:T(8,128)(2,1)S(1)}, bf16[2,128,10...) custom-call(s32[4]{0:T(128)S(1)} %pad_add_fusion.where_ref, ...), custom_call_target="tpu_custom_call" | custom-call | flops 4831838208 | bytes 6291456 | tf_op jit(solution)/shard_map/pallas_call | solution.py:213
  70.7 1.1 collective-permute-start.19
  71.8 1.0 collective-permute-start.20
  72.8 5.3 %shard_map.114 = (bf16[512,2048]{1,0:T(8,128)(2,1)S(1)}, bf16[2,512,384]{2,1,0:T(8,128)(2,1)S(1)}, bf16[2,512,768]{2,1,0:T(8,128)(2,1)S(1)}) custom-call(s32[4]{0:T(128)S(1)} %pad_add_fusion.where_ref, bf16[2,128,1024]{2,1,0:T(8,128)(2,1)} %pad_maximum_fusion.1.refs_0_, bf16[2,128,1024]{2,1,0:T(8,128)(2,1)} %collective-permute-done.27.refs_1_, ...), custom_call_target="tpu_custom_call" | custom-call | flops 1610612736 | bytes 10485760 | tf_op jit(solution)/shard_map/pallas_call | solution.py:272
  78.1 2.3 %collective-permute-start.29 = (bf16[2,128,1024]{2,1,0:T(8,128)(2,1)}, bf16[2,128,1024]{2,1,0:T(8,128)(2,1)S(1)}, u32[]{:S(2)}, u32[]{:S(2)}) collective-permute-start(bf16[2,128,1024]{2,1,0:T(8,128)(2,1)} %pad_maximum_fusion.1.refs_0_), channel_id=1, source_target_pairs={{0,12},{1,13},{2,14},{3,15},{4,0},{5,1},{6,2},{7,3},{8,4},{9,5},{1... | collective-permute-start | bytes 1572872 | tf_op jit(solution)/shard_map/ppermute | solution.py:359
  80.4 1.2 collective-permute-start.32
  81.7 1.4 collective-permute-start.30
  83.1 2.7 %shard_map.116.refs_0_ = f32[2048,768]{1,0:T(8,128)S(1)} custom-call(bf16[512,2048]{1,0:T(8,128)(2,1)S(1)} %get-tuple-element.35.left_ref, bf16[2,512,768]{2,1,0:T(8,128)(2,1)S(1)} %get-tuple-element.37.right_ref), custom_call_target="tpu_custom_call" | custom-call | flops 1610612736 | bytes 5242880 | tf_op jit(solution)/shard_map/pallas_call | solution.py:315
  85.8 8.9 %shard_map.112 = (bf16[2,128,1024]{2,1,0:T(8,128)(2,1)S(1)}, bf16[2,128,1024]{2,1,0:T(8,128)(2,1)S(1)}, bf16[2,128,1024]{2,1,0:T(8,128)(2,1)S(1)}, bf16[2,128,10...) custom-call(s32[4]{0:T(128)S(1)} %pad_add_fusion.where_ref, ...), custom_call_target="tpu_custom_call" | custom-call | flops 4831838208 | bytes 6291456 | tf_op jit(solution)/shard_map/pallas_call | solution.py:213
  94.7 7.9 %collective-permute-done.32.refs_3_ = bf16[2,128,1024]{2,1,0:T(8,128)(2,1)S(1)} collective-permute-done((bf16[2,128,1024]{2,1,0:T(8,128)(2,1)}, bf16[2,128,1024]{2,1,0:T(8,128)(2,1)S(1)}, u32[]{:S(2)}, u32[]{:S(2)}) %collective-permute-start.32) | collective-permute-done | bytes 524320 | tf_op jit(solution)/shard_map/ppermute | solution.py:359
  102.6 4.9 %shard_map.113 = (bf16[512,2048]{1,0:T(8,128)(2,1)S(1)}, bf16[2,512,384]{2,1,0:T(8,128)(2,1)S(1)}, bf16[2,512,768]{2,1,0:T(8,128)(2,1)S(1)}) custom-call(s32[4]{0:T(128)S(1)} %pad_add_fusion.where_ref, bf16[2,128,1024]{2,1,0:T(8,128)(2,1)} %collective-permute-done.28.refs_0_, bf16[2,128,1024]{2,1,0:T(8,128)(2,1)S(1)} %collective-permute-done.29.refs_1_, ...), custom_call_target="tpu_custom_call" | custom-call | flops 1610612736 | bytes 10485760 | tf_op jit(solution)/shard_map/pallas_call | solution.py:272
  107.5 2.7 %shard_map.117 = bf16[2048,768]{1,0:T(8,128)(2,1)S(1)} custom-call(bf16[512,2048]{1,0:T(8,128)(2,1)S(1)} %get-tuple-element.32.left_ref, bf16[2,512,768]{2,1,0:T(8,128)(2,1)S(1)} %get-tuple-element.34.right_ref, f32[2048,768]{1,0:T(8,128)S(1)} %shard_map.116.refs_0_), custom_call_target="tpu_custom_call" | custom-call | flops 1610612736 | bytes 5242880 | tf_op jit(solution)/shard_map/pallas_call | solution.py:315
  111.0 1.4 collective-permute-start.9
  113.1 6.5 %collective-permute-done.21 = bf16[2,128,1024]{2,1,0:T(8,128)(2,1)S(1)} collective-permute-done((bf16[2,128,1024]{2,1,0:T(8,128)(2,1)S(1)}, bf16[2,128,1024]{2,1,0:T(8,128)(2,1)S(1)}, u32[]{:S(2)}, u32[]{:S(2)}) %collective-permute-start.21) | collective-permute-done | bytes 524320 | tf_op jit(solution)/shard_map/ppermute | solution.py:359
  121.3 2.0 %shard_map.120.refs_0_ = f32[384,2048]{1,0:T(8,128)S(1)} custom-call(bf16[2,512,384]{2,1,0:T(8,128)(2,1)S(1)} %get-tuple-element.42.left_ref, bf16[512,2048]{1,0:T(8,128)(2,1)S(1)} %get-tuple-element.43.right_ref), custom_call_target="tpu_custom_call" | custom-call | flops 805306368 | bytes 3670016 | tf_op jit(solution)/shard_map/pallas_call | solution.py:337
  123.3 5.1 %collective-permute-done.9 = bf16[2,128,1024]{2,1,0:T(8,128)(2,1)S(1)} collective-permute-done((bf16[2,128,1024]{2,1,0:T(8,128)(2,1)S(1)}, bf16[2,128,1024]{2,1,0:T(8,128)(2,1)S(1)}, u32[]{:S(2)}, u32[]{:S(2)}) %collective-permute-start.9) | collective-permute-done | bytes 524320 | tf_op jit(solution)/shard_map/ppermute | solution.py:359
  129.4 2.1 %shard_map.121 = bf16[384,2048]{1,0:T(8,128)(2,1)S(1)} custom-call(bf16[2,512,384]{2,1,0:T(8,128)(2,1)S(1)} %get-tuple-element.40.left_ref, bf16[512,2048]{1,0:T(8,128)(2,1)S(1)} %get-tuple-element.41.right_ref, f32[384,2048]{1,0:T(8,128)S(1)} %shard_map.120.refs_0_), custom_call_target="tpu_custom_call" | custom-call | flops 805306368 | bytes 3670016 | tf_op jit(solution)/shard_map/pallas_call | solution.py:337
  131.5 8.1 %collective-permute-done.23 = bf16[2,128,1024]{2,1,0:T(8,128)(2,1)S(1)} collective-permute-done((bf16[2,128,1024]{2,1,0:T(8,128)(2,1)S(1)}, bf16[2,128,1024]{2,1,0:T(8,128)(2,1)S(1)}, u32[]{:S(2)}, u32[]{:S(2)}) %collective-permute-start.23) | collective-permute-done | bytes 524320 | tf_op jit(solution)/shard_map/ppermute | solution.py:359
  140.8 6.9 %collective-permute-done.11 = bf16[2,128,1024]{2,1,0:T(8,128)(2,1)S(1)} collective-permute-done((bf16[2,128,1024]{2,1,0:T(8,128)(2,1)S(1)}, bf16[2,128,1024]{2,1,0:T(8,128)(2,1)S(1)}, u32[]{:S(2)}, u32[]{:S(2)}) %collective-permute-start.11) | collective-permute-done | bytes 524320 | tf_op jit(solution)/shard_map/ppermute | solution.py:359
  147.7 1.0 collective-permute-start.24
  149.0 2.2 %collective-permute-start.12 = (bf16[128,1024]{1,0:T(8,128)(2,1)S(1)}, bf16[128,1024]{1,0:T(8,128)(2,1)S(1)}, u32[]{:S(2)}, u32[]{:S(2)}) collective-permute-start(bf16[128,1024]{1,0:T(8,128)(2,1)S(1)} %fusion.4), channel_id=1, source_target_pairs={{0,12},{1,13},{2,14},{3,15},{4,0},{5,1},{6,2},{7,3},{8,4},{9,5},{1... | collective-permute-start | bytes 786440 | tf_op jit(solution)/shard_map/ppermute | solution.py:359
  151.2 2.0 %shard_map.119.refs_0_ = f32[384,2048]{1,0:T(8,128)S(1)} custom-call(bf16[2,512,384]{2,1,0:T(8,128)(2,1)S(1)} %get-tuple-element.42.left_ref, bf16[512,2048]{1,0:T(8,128)(2,1)S(1)} %get-tuple-element.43.right_ref), custom_call_target="tpu_custom_call" | custom-call | flops 805306368 | bytes 3670016 | tf_op jit(solution)/shard_map/pallas_call | solution.py:337
  153.2 2.7 %shard_map.115.refs_0_ = f32[2048,768]{1,0:T(8,128)S(1)} custom-call(bf16[512,2048]{1,0:T(8,128)(2,1)S(1)} %get-tuple-element.35.left_ref, bf16[2,512,768]{2,1,0:T(8,128)(2,1)S(1)} %get-tuple-element.37.right_ref), custom_call_target="tpu_custom_call" | custom-call | flops 1610612736 | bytes 5242880 | tf_op jit(solution)/shard_map/pallas_call | solution.py:315
  155.9 6.4 %collective-permute-done.24 = bf16[128,1024]{1,0:T(8,128)(2,1)S(1)} collective-permute-done((bf16[128,1024]{1,0:T(8,128)(2,1)S(1)}, bf16[128,1024]{1,0:T(8,128)(2,1)S(1)}, u32[]{:S(2)}, u32[]{:S(2)}) %collective-permute-start.24) | collective-permute-done | bytes 262176 | tf_op jit(solution)/shard_map/ppermute | solution.py:359
  163.3 3.1 %shard_map.122 = bf16[384,2048]{1,0:T(8,128)(2,1)} custom-call(bf16[2,512,384]{2,1,0:T(8,128)(2,1)S(1)} %get-tuple-element.40.left_ref, bf16[512,2048]{1,0:T(8,128)(2,1)S(1)} %get-tuple-element.41.right_ref, f32[384,2048]{1,0:T(8,128)S(1)} %shard_map.119.refs_0_, bf16[384,2048]{1,0:T(8,128)(2,1)S(1)} %collective-permute-done.35.refs_1_), custom_call_target="tpu_custom_call" | custom-call | flops 805306368 | bytes 3670016 | tf_op jit(solution)/shard_map/pallas_call | solution.py:337
  166.4 3.8 %shard_map.118 = (bf16[2048,384]{1,0:T(8,128)(2,1)}, bf16[2048,384]{1,0:T(8,128)(2,1)}) custom-call(bf16[512,2048]{1,0:T(8,128)(2,1)S(1)} %get-tuple-element.32.left_ref, bf16[2,512,768]{2,1,0:T(8,128)(2,1)S(1)} %get-tuple-element.34.right_ref, f32[2048,768]{1,0:T(8,128)S(1)} %shard_map.115.refs_0_, bf16[2048,768]{1,0:T(8,128)(2,1)S(1)} %collective-permute-done.34.refs_1_), custom_call_target="tpu_custom_call" | custom-call | flops 1610612736 | bytes 5242880 | tf_op jit(solution)/shard_map/pallas_call | solution.py:315
  (77 shorter events, 16.6 us)
Async XLA Ops:
  0.6 4.4 %copy-start = (bf16[1,384,2048]{2,1,0:T(8,128)(2,1)S(1)}, bf16[1,384,2048]{2,1,0:T(8,128)(2,1)}, u32[]{:S(2)}) copy-start(bf16[1,384,2048]{2,1,0:T(8,128)(2,1)} %param.15) | copy-start | bytes 4718596
  0.6 4.5 %copy-start.1 = (bf16[128,1024]{1,0:T(8,128)(2,1)S(1)}, bf16[128,1024]{1,0:T(8,128)(2,1)}, u32[]{:S(2)}) copy-start(bf16[128,1024]{1,0:T(8,128)(2,1)} %param.8) | copy-start | bytes 786436
  0.7 19.2 %copy-start.8 = (f32[128,8]{0,1:T(8,128)S(1)}, f32[128,8]{0,1:T(8,128)}, u32[]{:S(2)}) copy-start(f32[128,8]{0,1:T(8,128)} %param.11) | copy-start | bytes 12292
  0.7 46.4 %copy-start.9 = (s32[128,8]{0,1:T(8,128)S(1)}, s32[128,8]{0,1:T(8,128)}, u32[]{:S(2)}) copy-start(s32[128,8]{0,1:T(8,128)} %param.10) | copy-start | bytes 12292
  0.7 46.4 %copy-start.10 = (s32[16]{0:T(128)S(1)}, s32[16]{0:T(128)}, u32[]{:S(2)}) copy-start(s32[16]{0:T(128)} %param.12) | copy-start | bytes 196
  4.6 53.5 %collective-permute-start.7 = (bf16[2048,768]{1,0:T(8,128)(2,1)}, bf16[2048,768]{1,0:T(8,128)(2,1)}, u32[]{:S(2)}, u32[]{:S(2)}) collective-permute-start(bf16[2048,768]{1,0:T(8,128)(2,1)} %pad_maximum_fusion.refs_9_), channel_id=1, source_target_pairs={{0,1},{1,0},{2,3},{3,2},{4,5},{5,4},{6,7},{7,6},{8,9},{9,8},{10,11... | collective-permute-start | bytes 9437192 | tf_op jit(solution)/shard_map/ppermute | solution.py:359
  5.1 51.6 %collective-permute-start.8 = (bf16[384,2048]{1,0:T(8,128)(2,1)S(1)}, bf16[384,2048]{1,0:T(8,128)(2,1)S(1)}, u32[]{:S(2)}, u32[]{:S(2)}) collective-permute-start(bf16[384,2048]{1,0:T(8,128)(2,1)S(1)} %bitcast.34), channel_id=1, source_target_pairs={{0,1},{1,0},{2,3},{3,2},{4,5},{5,4},{6,7},{7,6},{8,9},{9,8},{10,11... | collective-permute-start | bytes 4718600 | tf_op jit(solution)/shard_map/ppermute | solution.py:359
  5.1 9.4 %collective-permute-start = (bf16[1,128,1024]{2,1,0:T(8,128)(2,1)S(1)}, bf16[1,128,1024]{2,1,0:T(8,128)(2,1)}, u32[]{:S(2)}, u32[]{:S(2)}) collective-permute-start(bf16[1,128,1024]{2,1,0:T(8,128)(2,1)S(1)} %bitcast.43), channel_id=1, source_target_pairs={{0,2},{1,17},{2,0},{3,19},{4,6},{5,21},{6,4},{7,23},{8,10},{9,25},... | collective-permute-start | bytes 786440 | tf_op jit(solution)/shard_map/ppermute | solution.py:359
  8.1 8.9 %collective-permute-start.1 = (bf16[1,128,1024]{2,1,0:T(8,128)(2,1)S(1)}, bf16[1,128,1024]{2,1,0:T(8,128)(2,1)S(1)}, u32[]{:S(2)}, u32[]{:S(2)}) collective-permute-start(bf16[1,128,1024]{2,1,0:T(8,128)(2,1)S(1)} %bitcast.44), channel_id=1, source_target_pairs={{0,16},{1,3},{2,18},{3,1},{4,20},{5,7},{6,22},{7,5},{8,24},{9,11},... | collective-permute-start | bytes 786440 | tf_op jit(solution)/shard_map/ppermute | solution.py:359
  9.6 9.7 %collective-permute-start.3 = (bf16[128,1024]{1,0:T(8,128)(2,1)S(1)}, bf16[128,1024]{1,0:T(8,128)(2,1)}, u32[]{:S(2)}, u32[]{:S(2)}) collective-permute-start(bf16[128,1024]{1,0:T(8,128)(2,1)S(1)} %copy-done.1), channel_id=1, source_target_pairs={{0,4},{1,5},{2,6},{3,7},{4,8},{5,9},{6,10},{7,11},{8,12},{9,13},{1... | collective-permute-start | bytes 786440 | tf_op jit(solution)/shard_map/ppermute | solution.py:359
  14.5 9.5 %collective-permute-start.26 = (bf16[128,1024]{1,0:T(8,128)(2,1)}, bf16[128,1024]{1,0:T(8,128)(2,1)}, u32[]{:S(2)}, u32[]{:S(2)}) collective-permute-start(bf16[128,1024]{1,0:T(8,128)(2,1)} %param.9), channel_id=1, source_target_pairs={{0,2},{1,17},{2,0},{3,19},{4,6},{5,21},{6,4},{7,23},{8,10},{9,25},... | collective-permute-start | bytes 786440 | tf_op jit(solution)/shard_map/ppermute | solution.py:359
  17.0 0.7 copy-start.2
  17.7 8.8 %collective-permute-start.2 = (bf16[1,128,1024]{2,1,0:T(8,128)(2,1)}, bf16[1,128,1024]{2,1,0:T(8,128)(2,1)}, u32[]{:S(2)}, u32[]{:S(2)}) collective-permute-start(bf16[1,128,1024]{2,1,0:T(8,128)(2,1)} %collective-permute-done.refs_1_), channel_id=1, source_target_pairs={{0,16},{1,3},{2,18},{3,1},{4,20},{5,7},{6,22},{7,5},{8,24},{9,11},... | collective-permute-start | bytes 786440 | tf_op jit(solution)/shard_map/ppermute | solution.py:359
  19.3 10.3 %collective-permute-start.4 = (bf16[1,128,1024]{2,1,0:T(8,128)(2,1)}, bf16[1,128,1024]{2,1,0:T(8,128)(2,1)}, u32[]{:S(2)}, u32[]{:S(2)}) collective-permute-start(bf16[1,128,1024]{2,1,0:T(8,128)(2,1)} %bitcast.5.refs_4_), channel_id=1, source_target_pairs={{0,2},{1,17},{2,0},{3,19},{4,6},{5,21},{6,4},{7,23},{8,10},{9,25},... | collective-permute-start | bytes 786440 | tf_op jit(solution)/shard_map/ppermute | solution.py:359
  24.0 9.6 %collective-permute-start.5 = (bf16[1,128,1024]{2,1,0:T(8,128)(2,1)}, bf16[1,128,1024]{2,1,0:T(8,128)(2,1)S(1)}, u32[]{:S(2)}, u32[]{:S(2)}) collective-permute-start(bf16[1,128,1024]{2,1,0:T(8,128)(2,1)} %bitcast.5.refs_4_), channel_id=1, source_target_pairs={{0,16},{1,3},{2,18},{3,1},{4,20},{5,7},{6,22},{7,5},{8,24},{9,11},... | collective-permute-start | bytes 786440 | tf_op jit(solution)/shard_map/ppermute | solution.py:359
  26.5 9.5 %collective-permute-start.13 = (bf16[128,1024]{1,0:T(8,128)(2,1)}, bf16[128,1024]{1,0:T(8,128)(2,1)}, u32[]{:S(2)}, u32[]{:S(2)}) collective-permute-start(bf16[128,1024]{1,0:T(8,128)(2,1)} %collective-permute-done.3), channel_id=1, source_target_pairs={{0,4},{1,5},{2,6},{3,7},{4,8},{5,9},{6,10},{7,11},{8,12},{9,13},{1... | collective-permute-start | bytes 786440 | tf_op jit(solution)/shard_map/ppermute | solution.py:359
  29.6 7.9 %collective-permute-start.6 = (bf16[1,128,1024]{2,1,0:T(8,128)(2,1)}, bf16[1,128,1024]{2,1,0:T(8,128)(2,1)S(1)}, u32[]{:S(2)}, u32[]{:S(2)}) collective-permute-start(bf16[1,128,1024]{2,1,0:T(8,128)(2,1)} %collective-permute-done.4.refs_5_), channel_id=1, source_target_pairs={{0,16},{1,3},{2,18},{3,1},{4,20},{5,7},{6,22},{7,5},{8,24},{9,11},... | collective-permute-start | bytes 786440 | tf_op jit(solution)/shard_map/ppermute | solution.py:359
  33.6 0.7 copy-start.4
  34.3 18.3 %collective-permute-start.27 = (bf16[2,128,1024]{2,1,0:T(8,128)(2,1)}, bf16[2,128,1024]{2,1,0:T(8,128)(2,1)}, u32[]{:S(2)}, u32[]{:S(2)}) collective-permute-start(bf16[2,128,1024]{2,1,0:T(8,128)(2,1)} %pad_maximum_fusion.1.refs_0_), channel_id=1, source_target_pairs={{0,4},{1,5},{2,6},{3,7},{4,8},{5,9},{6,10},{7,11},{8,12},{9,13},{1... | collective-permute-start | bytes 1572872 | tf_op jit(solution)/shard_map/ppermute | solution.py:359
  36.0 9.5 %collective-permute-start.14 = (bf16[1,128,1024]{2,1,0:T(8,128)(2,1)}, bf16[1,128,1024]{2,1,0:T(8,128)(2,1)}, u32[]{:S(2)}, u32[]{:S(2)}) collective-permute-start(bf16[1,128,1024]{2,1,0:T(8,128)(2,1)} %bitcast.13.refs_0_), channel_id=1, source_target_pairs={{0,2},{1,17},{2,0},{3,19},{4,6},{5,21},{6,4},{7,23},{8,10},{9,25},... | collective-permute-start | bytes 786440 | tf_op jit(solution)/shard_map/ppermute | solution.py:359
  37.5 0.7 copy-start.6
  38.2 16.6 %collective-permute-start.31 = (bf16[2,128,1024]{2,1,0:T(8,128)(2,1)}, bf16[2,128,1024]{2,1,0:T(8,128)(2,1)}, u32[]{:S(2)}, u32[]{:S(2)}) collective-permute-start(bf16[2,128,1024]{2,1,0:T(8,128)(2,1)} %pad_maximum_fusion.1.refs_0_), channel_id=1, source_target_pairs={{0,16},{1,3},{2,18},{3,1},{4,20},{5,7},{6,22},{7,5},{8,24},{9,11},... | collective-permute-start | bytes 1572872 | tf_op jit(solution)/shard_map/ppermute | solution.py:359
  45.5 8.5 %collective-permute-start.17 = (bf16[128,1024]{1,0:T(8,128)(2,1)}, bf16[128,1024]{1,0:T(8,128)(2,1)}, u32[]{:S(2)}, u32[]{:S(2)}) collective-permute-start(bf16[128,1024]{1,0:T(8,128)(2,1)} %collective-permute-done.13), channel_id=1, source_target_pairs={{0,4},{1,5},{2,6},{3,7},{4,8},{5,9},{6,10},{7,11},{8,12},{9,13},{1... | collective-permute-start | bytes 786440 | tf_op jit(solution)/shard_map/ppermute | solution.py:359
  48.0 11.1 %all-to-all-start = ((f32[16,2,128]{2,1,0:T(2,128)}), f32[16,2,128]{2,1,0:T(2,128)S(1)}, u32[]{:S(2)}, u32[]{:S(2)}) async-start(f32[16,2,128]{2,1,0:T(2,128)} %bitcast.6), calls=%async_computation | async-start | bytes 32768 | tf_op jit(solution)/shard_map/all_to_all | solution.py:404
  52.6 19.2 %collective-permute-start.33 = (bf16[2,128,1024]{2,1,0:T(8,128)(2,1)}, bf16[2,128,1024]{2,1,0:T(8,128)(2,1)}, u32[]{:S(2)}, u32[]{:S(2)}) collective-permute-start(bf16[2,128,1024]{2,1,0:T(8,128)(2,1)} %collective-permute-done.27.refs_1_), channel_id=1, source_target_pairs={{0,16},{1,3},{2,18},{3,1},{4,20},{5,7},{6,22},{7,5},{8,24},{9,11},... | collective-permute-start | bytes 1572872 | tf_op jit(solution)/shard_map/ppermute | solution.py:359
  54.0 24.1 %collective-permute-start.15 = (bf16[1,128,1024]{2,1,0:T(8,128)(2,1)}, bf16[1,128,1024]{2,1,0:T(8,128)(2,1)}, u32[]{:S(2)}, u32[]{:S(2)}) collective-permute-start(bf16[1,128,1024]{2,1,0:T(8,128)(2,1)} %bitcast.13.refs_0_), channel_id=1, source_target_pairs={{0,16},{1,3},{2,18},{3,1},{4,20},{5,7},{6,22},{7,5},{8,24},{9,11},... | collective-permute-start | bytes 786440 | tf_op jit(solution)/shard_map/ppermute | solution.py:359
  54.8 15.9 %collective-permute-start.18 = (bf16[1,128,1024]{2,1,0:T(8,128)(2,1)}, bf16[1,128,1024]{2,1,0:T(8,128)(2,1)}, u32[]{:S(2)}, u32[]{:S(2)}) collective-permute-start(bf16[1,128,1024]{2,1,0:T(8,128)(2,1)} %bitcast.14.refs_4_), channel_id=1, source_target_pairs={{0,2},{1,17},{2,0},{3,19},{4,6},{5,21},{6,4},{7,23},{8,10},{9,25},... | collective-permute-start | bytes 786440 | tf_op jit(solution)/shard_map/ppermute | solution.py:359
  56.6 25.0 %collective-permute-start.28 = (bf16[2,128,1024]{2,1,0:T(8,128)(2,1)}, bf16[2,128,1024]{2,1,0:T(8,128)(2,1)}, u32[]{:S(2)}, u32[]{:S(2)}) collective-permute-start(bf16[2,128,1024]{2,1,0:T(8,128)(2,1)} %collective-permute-done.27.refs_1_), channel_id=1, source_target_pairs={{0,4},{1,5},{2,6},{3,7},{4,8},{5,9},{6,10},{7,11},{8,12},{9,13},{1... | collective-permute-start | bytes 1572872 | tf_op jit(solution)/shard_map/ppermute | solution.py:359
  58.1 22.3 %collective-permute-start.16 = (bf16[1,128,1024]{2,1,0:T(8,128)(2,1)}, bf16[1,128,1024]{2,1,0:T(8,128)(2,1)}, u32[]{:S(2)}, u32[]{:S(2)}) collective-permute-start(bf16[1,128,1024]{2,1,0:T(8,128)(2,1)} %collective-permute-done.14.refs_1_), channel_id=1, source_target_pairs={{0,16},{1,3},{2,18},{3,1},{4,20},{5,7},{6,22},{7,5},{8,24},{9,11},... | collective-permute-start | bytes 786440 | tf_op jit(solution)/shard_map/ppermute | solution.py:359
  59.1 1.0 copy-start.3
  60.0 0.9 copy-start.5
  61.0 0.9 copy-start.7
  70.7 15.1 %collective-permute-start.19 = (bf16[1,128,1024]{2,1,0:T(8,128)(2,1)}, bf16[1,128,1024]{2,1,0:T(8,128)(2,1)S(1)}, u32[]{:S(2)}, u32[]{:S(2)}) collective-permute-start(bf16[1,128,1024]{2,1,0:T(8,128)(2,1)} %bitcast.14.refs_4_), channel_id=1, source_target_pairs={{0,16},{1,3},{2,18},{3,1},{4,20},{5,7},{6,22},{7,5},{8,24},{9,11},... | collective-permute-start | bytes 786440 | tf_op jit(solution)/shard_map/ppermute | solution.py:359
  71.8 14.0 %collective-permute-start.20 = (bf16[1,128,1024]{2,1,0:T(8,128)(2,1)}, bf16[1,128,1024]{2,1,0:T(8,128)(2,1)S(1)}, u32[]{:S(2)}, u32[]{:S(2)}) collective-permute-start(bf16[1,128,1024]{2,1,0:T(8,128)(2,1)} %collective-permute-done.18.refs_5_), channel_id=1, source_target_pairs={{0,16},{1,3},{2,18},{3,1},{4,20},{5,7},{6,22},{7,5},{8,24},{9,11},... | collective-permute-start | bytes 786440 | tf_op jit(solution)/shard_map/ppermute | solution.py:359
  78.1 16.6 %collective-permute-start.29 = (bf16[2,128,1024]{2,1,0:T(8,128)(2,1)}, bf16[2,128,1024]{2,1,0:T(8,128)(2,1)S(1)}, u32[]{:S(2)}, u32[]{:S(2)}) collective-permute-start(bf16[2,128,1024]{2,1,0:T(8,128)(2,1)} %pad_maximum_fusion.1.refs_0_), channel_id=1, source_target_pairs={{0,12},{1,13},{2,14},{3,15},{4,0},{5,1},{6,2},{7,3},{8,4},{9,5},{1... | collective-permute-start | bytes 1572872 | tf_op jit(solution)/shard_map/ppermute | solution.py:359
  80.4 22.2 %collective-permute-start.32 = (bf16[2,128,1024]{2,1,0:T(8,128)(2,1)}, bf16[2,128,1024]{2,1,0:T(8,128)(2,1)S(1)}, u32[]{:S(2)}, u32[]{:S(2)}) collective-permute-start(bf16[2,128,1024]{2,1,0:T(8,128)(2,1)} %collective-permute-done.31.refs_2_), channel_id=1, source_target_pairs={{0,12},{1,13},{2,14},{3,15},{4,0},{5,1},{6,2},{7,3},{8,4},{9,5},{1... | collective-permute-start | bytes 1572872 | tf_op jit(solution)/shard_map/ppermute | solution.py:359
  81.7 20.9 %collective-permute-start.30 = (bf16[2,128,1024]{2,1,0:T(8,128)(2,1)}, bf16[2,128,1024]{2,1,0:T(8,128)(2,1)S(1)}, u32[]{:S(2)}, u32[]{:S(2)}) collective-permute-start(bf16[2,128,1024]{2,1,0:T(8,128)(2,1)} %collective-permute-done.28.refs_0_), channel_id=1, source_target_pairs={{0,16},{1,3},{2,18},{3,1},{4,20},{5,7},{6,22},{7,5},{8,24},{9,11},... | collective-permute-start | bytes 1572872 | tf_op jit(solution)/shard_map/ppermute | solution.py:359
  110.3 56.1 %collective-permute-start.34 = (bf16[2048,768]{1,0:T(8,128)(2,1)S(1)}, bf16[2048,768]{1,0:T(8,128)(2,1)S(1)}, u32[]{:S(2)}, u32[]{:S(2)}) collective-permute-start(bf16[2048,768]{1,0:T(8,128)(2,1)S(1)} %shard_map.117), channel_id=1, source_target_pairs={{0,1},{1,0},{2,3},{3,2},{4,5},{5,4},{6,7},{7,6},{8,9},{9,8},{10,11... | collective-permute-start | bytes 9437192 | tf_op jit(solution)/shard_map/ppermute | solution.py:359
  110.3 9.2 %collective-permute-start.21 = (bf16[2,128,1024]{2,1,0:T(8,128)(2,1)S(1)}, bf16[2,128,1024]{2,1,0:T(8,128)(2,1)S(1)}, u32[]{:S(2)}, u32[]{:S(2)}) collective-permute-start(bf16[2,128,1024]{2,1,0:T(8,128)(2,1)S(1)} %get-tuple-element.30), channel_id=1, source_target_pairs={{0,16},{1,3},{2,18},{3,1},{4,20},{5,7},{6,22},{7,5},{8,24},{9,11},... | collective-permute-start | bytes 1572872 | tf_op jit(solution)/shard_map/ppermute | solution.py:359
  111.0 17.3 %collective-permute-start.9 = (bf16[2,128,1024]{2,1,0:T(8,128)(2,1)S(1)}, bf16[2,128,1024]{2,1,0:T(8,128)(2,1)S(1)}, u32[]{:S(2)}, u32[]{:S(2)}) collective-permute-start(bf16[2,128,1024]{2,1,0:T(8,128)(2,1)S(1)} %get-tuple-element.26), channel_id=1, source_target_pairs={{0,16},{1,3},{2,18},{3,1},{4,20},{5,7},{6,22},{7,5},{8,24},{9,11},... | collective-permute-start | bytes 1572872 | tf_op jit(solution)/shard_map/ppermute | solution.py:359
  112.4 27.2 %collective-permute-start.23 = (bf16[2,128,1024]{2,1,0:T(8,128)(2,1)S(1)}, bf16[2,128,1024]{2,1,0:T(8,128)(2,1)S(1)}, u32[]{:S(2)}, u32[]{:S(2)}) collective-permute-start(bf16[2,128,1024]{2,1,0:T(8,128)(2,1)S(1)} %get-tuple-element.31), channel_id=1, source_target_pairs={{0,16},{1,3},{2,18},{3,1},{4,20},{5,7},{6,22},{7,5},{8,24},{9,11},... | collective-permute-start | bytes 1572872 | tf_op jit(solution)/shard_map/ppermute | solution.py:359
  119.8 19.8 %collective-permute-start.22 = (bf16[2,128,1024]{2,1,0:T(8,128)(2,1)S(1)}, bf16[2,128,1024]{2,1,0:T(8,128)(2,1)S(1)}, u32[]{:S(2)}, u32[]{:S(2)}) collective-permute-start(bf16[2,128,1024]{2,1,0:T(8,128)(2,1)S(1)} %add_convert_fusion.1), channel_id=1, source_target_pairs={{0,2},{1,17},{2,0},{3,19},{4,6},{5,21},{6,4},{7,23},{8,10},{9,25},... | collective-permute-start | bytes 1572872 | tf_op jit(solution)/shard_map/ppermute | solution.py:359
  120.6 27.0 %collective-permute-start.11 = (bf16[2,128,1024]{2,1,0:T(8,128)(2,1)S(1)}, bf16[2,128,1024]{2,1,0:T(8,128)(2,1)S(1)}, u32[]{:S(2)}, u32[]{:S(2)}) collective-permute-start(bf16[2,128,1024]{2,1,0:T(8,128)(2,1)S(1)} %get-tuple-element.27), channel_id=1, source_target_pairs={{0,16},{1,3},{2,18},{3,1},{4,20},{5,7},{6,22},{7,5},{8,24},{9,11},... | collective-permute-start | bytes 1572872 | tf_op jit(solution)/shard_map/ppermute | solution.py:359
  128.6 20.1 %collective-permute-start.10 = (bf16[2,128,1024]{2,1,0:T(8,128)(2,1)S(1)}, bf16[2,128,1024]{2,1,0:T(8,128)(2,1)S(1)}, u32[]{:S(2)}, u32[]{:S(2)}) collective-permute-start(bf16[2,128,1024]{2,1,0:T(8,128)(2,1)S(1)} %add_convert_fusion.2), channel_id=1, source_target_pairs={{0,2},{1,17},{2,0},{3,19},{4,6},{5,21},{6,4},{7,23},{8,10},{9,25},... | collective-permute-start | bytes 1572872 | tf_op jit(solution)/shard_map/ppermute | solution.py:359
  139.6 23.7 %collective-permute-start.35 = (bf16[384,2048]{1,0:T(8,128)(2,1)S(1)}, bf16[384,2048]{1,0:T(8,128)(2,1)S(1)}, u32[]{:S(2)}, u32[]{:S(2)}) collective-permute-start(bf16[384,2048]{1,0:T(8,128)(2,1)S(1)} %shard_map.121), channel_id=1, source_target_pairs={{0,1},{1,0},{2,3},{3,2},{4,5},{5,4},{6,7},{7,6},{8,9},{9,8},{10,11... | collective-permute-start | bytes 4718600 | tf_op jit(solution)/shard_map/ppermute | solution.py:359
  139.9 16.0 %collective-permute-start.25 = (bf16[128,1024]{1,0:T(8,128)(2,1)S(1)}, bf16[128,1024]{1,0:T(8,128)(2,1)S(1)}, u32[]{:S(2)}, u32[]{:S(2)}) collective-permute-start(bf16[128,1024]{1,0:T(8,128)(2,1)S(1)} %get-tuple-element.45), channel_id=1, source_target_pairs={{0,4},{1,5},{2,6},{3,7},{4,8},{5,9},{6,10},{7,11},{8,12},{9,13},{1... | collective-permute-start | bytes 786440 | tf_op jit(solution)/shard_map/ppermute | solution.py:359
  147.7 14.7 %collective-permute-start.24 = (bf16[128,1024]{1,0:T(8,128)(2,1)S(1)}, bf16[128,1024]{1,0:T(8,128)(2,1)S(1)}, u32[]{:S(2)}, u32[]{:S(2)}) collective-permute-start(bf16[128,1024]{1,0:T(8,128)(2,1)S(1)} %get-tuple-element.44), channel_id=1, source_target_pairs={{0,8},{1,9},{2,10},{3,11},{4,12},{5,13},{6,14},{7,15},{8,0},{9,1},... | collective-permute-start | bytes 786440 | tf_op jit(solution)/shard_map/ppermute | solution.py:359
  149.0 13.4 %collective-permute-start.12 = (bf16[128,1024]{1,0:T(8,128)(2,1)S(1)}, bf16[128,1024]{1,0:T(8,128)(2,1)S(1)}, u32[]{:S(2)}, u32[]{:S(2)}) collective-permute-start(bf16[128,1024]{1,0:T(8,128)(2,1)S(1)} %fusion.4), channel_id=1, source_target_pairs={{0,12},{1,13},{2,14},{3,15},{4,0},{5,1},{6,2},{7,3},{8,4},{9,5},{1... | collective-permute-start | bytes 786440 | tf_op jit(solution)/shard_map/ppermute | solution.py:359

commit v4 on v3

--- a/solution.py
+++ b/solution.py
@@ -12,7 +12,7 @@
 CORES = 2
 SIDE = 2
 GROUP = 2
-ALONG = {3: -1}
+ALONG = {3: (0, -1), 2: (1, 1)}
 TILE = 512
 F32 = jnp.float32
 BF16 = jnp.bfloat16
@@ -351,6 +351,61 @@
     )(hid, cot, *add)
 
 
+def joint_grads_kernel(slots, added, splits, rows_ref, cot_ref, *refs):
+    given = 2 + 2 * added
+    outs = refs[given * slots :]
+    for slot in range(slots):
+        both_ref, hid_ref, *adds = refs[given * slot : given * (slot + 1)]
+        results = outs[(splits + 1) * slot : (splits + 1) * (slot + 1)]
+        grads = dot_rows(rows_ref[...], both_ref[0])
+        for ref in adds[:added]:
+            grads += ref[...].astype(F32)
+        columns = results[0].shape[1]
+        for number, ref in enumerate(results[:splits]):
+            ref[...] = grads[:, number * columns : (number + 1) * columns].astype(ref.dtype)
+        grads = dot_rows(hid_ref[0], cot_ref[...])
+        for ref in adds[added:]:
+            grads += ref[...].astype(F32)
+        results[splits][...] = grads.astype(results[splits].dtype)
+
+
+def joint_grads(slots, rows_ref, both, cot, hid, in_adds, down_adds, splits, kind):
+    total, features = rows_ref.shape
+    units, width = hid.shape[2], both.shape[2]
+    tile = min(TILE // 2, features)
+    added = len(in_adds[0])
+    columns = width // splits
+
+    def tall(columns):
+        return pl.BlockSpec((tile, columns), lambda i: (i, 0))
+
+    def whole(slot, columns):
+        return pl.BlockSpec((1, total, columns), lambda i: (slot, 0, 0))
+
+    flat = pl.BlockSpec((units, tile), lambda i: (0, i))
+    some = pl.BlockSpec((total, tile), lambda i: (0, i))
+    operands, in_specs, out_shape, out_specs = [rows_ref, cot], [some, some], [], []
+    for number, slot in enumerate(slots):
+        operands += [both, hid, *in_adds[number], *down_adds[number]]
+        in_specs += [whole(slot, width), whole(slot, units)] + [tall(width)] * added + [flat] * added
+        out_shape += [jax.ShapeDtypeStruct((features, columns), kind)] * splits
+        out_shape += [jax.ShapeDtypeStruct((units, features), kind)]
+        out_specs += [tall(columns)] * splits + [flat]
+    return pl.pallas_call(
+        functools.partial(joint_grads_kernel, len(slots), added, splits),
+        grid=(features // tile,),
+        out_shape=tuple(out_shape),
+        in_specs=in_specs,
+        out_specs=tuple(out_specs),
+        compiler_params=pltpu.CompilerParams(vmem_limit_bytes=16 << 20),
+        cost_estimate=pl.CostEstimate(
+            flops=2 * total * features * (width + units) * len(slots),
+            bytes_accessed=4 * features * (total + (width + units) * len(slots)),
+            transcendentals=0,
+        ),
+    )(*operands)
+
+
 def gather_plan(tokens, cotangent, routes, gate_probs, matching, gate_weight, up_weight, down_weight):
     expert_count = lax.axis_size("expert")
     depth, shift, swap, first, second = moves(expert_count)
@@ -391,7 +446,8 @@
     fars = []
     for back, pair in enumerate(pairs):
         if back in ALONG:
-            fars.append(send(fars[0], shift[ALONG[back]]))
+            source, by = ALONG[back]
+            fars.append(send(fars[source], shift[by]))
         else:
             fars.append(send(pair, second))
 
@@ -429,9 +485,8 @@
         )
         if number == len(groups) - 1:
             break
-        for slot in (1, 0):
-            in_sums[slot] = in_grads(slot, kept_rows[number], both, in_sums[slot], (F32,))
-            down_sums[slot] = down_grads(slot, cot, hid, down_sums[slot], F32)
+        sums = joint_grads((0, 1), kept_rows[number], both, cot, hid, in_sums, down_sums, 1, F32)
+        in_sums, down_sums = [[sums[0]], [sums[2]]], [[sums[1]], [sums[3]]]
     (in_got,) = in_grads(1, kept_rows[-1], both, in_sums[1], (BF16,))
     in_got = send(in_got, swap)
     (down_got,) = down_grads(1, cot, hid, down_sums[1], BF16)

time: 173 us -> 189 us (1.092); the launches traced: 170 us -> 189 us
  waiting for transfers between devices: 56.8 us -> 77.2 us
  Pallas kernels: 49 us -> 47.1 us
    ppermute x36, waiting for transfers between devices: 56.5 us -> 76.8 us  [send(): return lax.ppermute(value, AXES, pairs)]
    pallas_call x0 -> x1, Pallas kernels: none -> 7.82 us  [joint_grads(): pl.pallas_call(functools.partial(joint_grads_kernel, len(slots), added, s...]
    pallas_call x4 -> x2, Pallas kernels: 11.9 us -> 6.48 us  [in_grads(): pl.pallas_call(functools.partial(grads_kernel, len(add)), grid=(features...]
    pallas_call x4 -> x2, Pallas kernels: 9.19 us -> 5.18 us  [down_grads(): pl.pallas_call(functools.partial(grads_kernel, len(add)), grid=(features...]
    unnamed x22 -> x30, local copies, waits for them, and re-layouts: 4.98 us -> 5 us
  transfers between devices with their start and end apart: 37 -> 37, of which waited for: 15 -> 16; matrix products, arithmetic and copies ran while one was open for 3% -> 3% of each run, Pallas kernels for 22% -> 19%
where the time goes in v4:
time: 189 us
  waiting for transfers between devices  77.2 us (41%)
  starting transfers between devices  49.9 us (26%)
  Pallas kernels  47.1 us (25%)
  other arithmetic  8.48 us (4%)
  local copies, waits for them, and re-layouts  5.15 us (3%)
    ppermute x36, waiting for transfers between devices, send(): return lax.ppermute(value, AXES, pairs)  76.8 us
    ppermute x36, starting transfers between devices, send(): return lax.ppermute(value, AXES, pairs)  45.7 us
    pallas_call x2, Pallas kernels, forward(): pl.pallas_call(functools.partial(forward_kernel, backs, depth, len(sets))...  17.8 us
    pallas_call x2, Pallas kernels, backward(): pl.pallas_call(functools.partial(backward_kernel, backs, depth), out_shap...  9.83 us
    pallas_call x1, Pallas kernels, joint_grads(): pl.pallas_call(functools.partial(joint_grads_kernel, len(slots), added, s...  7.82 us
    pallas_call x2, Pallas kernels, in_grads(): pl.pallas_call(functools.partial(grads_kernel, len(add)), grid=(features...  6.48 us
    pallas_call x2, Pallas kernels, down_grads(): pl.pallas_call(functools.partial(grads_kernel, len(add)), grid=(features...  5.18 us
    unnamed x30, local copies, waits for them, and re-layouts  5 us
  transfers between devices with their start and end apart: 37, of which 16 were waited for; matrix products, arithmetic and copies ran while one was open for 3% of the time, Pallas kernels for 19%

profile of v4, /device:TPU:0, one launch (start us, length us, event | category | flops | bytes accessed | tf_op | source)
XLA Modules:
  0.0 188.8 jit_solution(3549567073958208994)
XLA Ops:
  0.7 3.9 %pad_maximum_fusion.refs_9_ = bf16[2048,768]{1,0:T(8,128)(2,1)} fusion(bf16[2048,384]{1,0:T(8,128)(2,1)} %bitcast.47, bf16[2048,384]{1,0:T(8,128)(2,1)} %bitcast.48), kind=kLoop, calls=%fused_computation | loop fusion | flops 6291456 | bytes 6291456 | tf_op jit(solution)/shard_map/concatenate | solution.py:422
  5.1 3.0 %collective-permute-start.1 = (bf16[1,128,1024]{2,1,0:T(8,128)(2,1)S(1)}, bf16[1,128,1024]{2,1,0:T(8,128)(2,1)S(1)}, u32[]{:S(2)}, u32[]{:S(2)}) collective-permute-start(bf16[1,128,1024]{2,1,0:T(8,128)(2,1)S(1)} %bitcast.43), channel_id=1, source_target_pairs={{0,16},{1,3},{2,18},{3,1},{4,20},{5,7},{6,22},{7,5},{8,24},{9,11},... | collective-permute-start | bytes 786440 | tf_op jit(solution)/shard_map/ppermute | solution.py:414
  8.1 1.5 collective-permute-start
  9.6 1.6 collective-permute-start.3
  11.1 3.3 %collective-permute-done.1.refs_2_ = bf16[1,128,1024]{2,1,0:T(8,128)(2,1)S(1)} collective-permute-done((bf16[1,128,1024]{2,1,0:T(8,128)(2,1)S(1)}, bf16[1,128,1024]{2,1,0:T(8,128)(2,1)S(1)}, u32[]{:S(2)}, u32[]{:S(2)}) %collective-permute-start.1) | collective-permute-done | bytes 262176 | tf_op jit(solution)/shard_map/ppermute | solution.py:414
  15.2 1.9 %collective-permute-start.26 = (bf16[128,1024]{1,0:T(8,128)(2,1)}, bf16[128,1024]{1,0:T(8,128)(2,1)}, u32[]{:S(2)}, u32[]{:S(2)}) collective-permute-start(bf16[128,1024]{1,0:T(8,128)(2,1)} %param.9), channel_id=1, source_target_pairs={{0,2},{1,17},{2,0},{3,19},{4,6},{5,21},{6,4},{7,23},{8,10},{9,25},... | collective-permute-start | bytes 786440 | tf_op jit(solution)/shard_map/ppermute | solution.py:414
  17.1 1.7 collective-permute-start.2
  19.8 4.9 %collective-permute-done.26 = bf16[128,1024]{1,0:T(8,128)(2,1)} collective-permute-done((bf16[128,1024]{1,0:T(8,128)(2,1)}, bf16[128,1024]{1,0:T(8,128)(2,1)}, u32[]{:S(2)}, u32[]{:S(2)}) %collective-permute-start.26) | collective-permute-done | bytes 262176 | tf_op jit(solution)/shard_map/ppermute | solution.py:414
  24.7 2.2 %collective-permute-start.5 = (bf16[1,128,1024]{2,1,0:T(8,128)(2,1)}, bf16[1,128,1024]{2,1,0:T(8,128)(2,1)S(1)}, u32[]{:S(2)}, u32[]{:S(2)}) collective-permute-start(bf16[1,128,1024]{2,1,0:T(8,128)(2,1)} %bitcast.5.refs_4_), channel_id=1, source_target_pairs={{0,16},{1,3},{2,18},{3,1},{4,20},{5,7},{6,22},{7,5},{8,24},{9,11},... | collective-permute-start | bytes 786440 | tf_op jit(solution)/shard_map/ppermute | solution.py:414
  26.9 1.8 collective-permute-start.13
  28.7 1.6 collective-permute-done.4.refs_5_
  30.3 2.2 %collective-permute-start.6 = (bf16[1,128,1024]{2,1,0:T(8,128)(2,1)}, bf16[1,128,1024]{2,1,0:T(8,128)(2,1)S(1)}, u32[]{:S(2)}, u32[]{:S(2)}) collective-permute-start(bf16[1,128,1024]{2,1,0:T(8,128)(2,1)} %collective-permute-done.4.refs_5_), channel_id=1, source_target_pairs={{0,16},{1,3},{2,18},{3,1},{4,20},{5,7},{6,22},{7,5},{8,24},{9,11},... | collective-permute-start | bytes 786440 | tf_op jit(solution)/shard_map/ppermute | solution.py:414
  32.5 1.9 pad_maximum_fusion.1.refs_0_
  35.1 1.8 collective-permute-start.27
  36.9 2.3 %collective-permute-done.6.refs_7_ = bf16[1,128,1024]{2,1,0:T(8,128)(2,1)S(1)} collective-permute-done((bf16[1,128,1024]{2,1,0:T(8,128)(2,1)}, bf16[1,128,1024]{2,1,0:T(8,128)(2,1)S(1)}, u32[]{:S(2)}, u32[]{:S(2)}) %collective-permute-start.6) | collective-permute-done | bytes 262176 | tf_op jit(solution)/shard_map/ppermute | solution.py:414
  40.0 1.7 collective-permute-start.32
  41.8 3.4 %collective-permute-done.14.refs_1_ = bf16[1,128,1024]{2,1,0:T(8,128)(2,1)} collective-permute-done((bf16[1,128,1024]{2,1,0:T(8,128)(2,1)}, bf16[1,128,1024]{2,1,0:T(8,128)(2,1)}, u32[]{:S(2)}, u32[]{:S(2)}) %collective-permute-start.14) | collective-permute-done | bytes 262176 | tf_op jit(solution)/shard_map/ppermute | solution.py:414
  45.2 1.4 collective-permute-start.17
  47.5 4.2 %all-to-all-start = ((f32[16,2,128]{2,1,0:T(2,128)}), f32[16,2,128]{2,1,0:T(2,128)S(1)}, u32[]{:S(2)}, u32[]{:S(2)}) async-start(f32[16,2,128]{2,1,0:T(2,128)} %bitcast.6), calls=%async_computation | async-start | bytes 32768 | tf_op jit(solution)/shard_map/all_to_all | solution.py:460
  53.7 1.4 collective-permute-start.15
  55.7 1.1 collective-permute-start.18
  56.8 1.1 collective-permute-start.16
  61.1 8.8 %shard_map.111 = (bf16[2,128,1024]{2,1,0:T(8,128)(2,1)S(1)}, bf16[2,128,1024]{2,1,0:T(8,128)(2,1)S(1)}, bf16[2,128,1024]{2,1,0:T(8,128)(2,1)S(1)}, bf16[2,128,10...) custom-call(s32[4]{0:T(128)S(1)} %pad_add_fusion.where_ref, ...), custom_call_target="tpu_custom_call" | custom-call | flops 4831838208 | bytes 6291456 | tf_op jit(solution)/shard_map/pallas_call | solution.py:213
  70.0 2.9 %collective-permute-start.29 = (bf16[2,128,1024]{2,1,0:T(8,128)(2,1)}, bf16[2,128,1024]{2,1,0:T(8,128)(2,1)S(1)}, u32[]{:S(2)}, u32[]{:S(2)}) collective-permute-start(bf16[2,128,1024]{2,1,0:T(8,128)(2,1)} %pad_maximum_fusion.1.refs_0_), channel_id=1, source_target_pairs={{0,12},{1,13},{2,14},{3,15},{4,0},{5,1},{6,2},{7,3},{8,4},{9,5},{1... | collective-permute-start | bytes 1572872 | tf_op jit(solution)/shard_map/ppermute | solution.py:414
  72.9 5.4 %shard_map.114 = (bf16[512,2048]{1,0:T(8,128)(2,1)S(1)}, bf16[2,512,384]{2,1,0:T(8,128)(2,1)S(1)}, bf16[2,512,768]{2,1,0:T(8,128)(2,1)S(1)}) custom-call(s32[4]{0:T(128)S(1)} %pad_add_fusion.where_ref, bf16[2,128,1024]{2,1,0:T(8,128)(2,1)} %pad_maximum_fusion.1.refs_0_, bf16[2,128,1024]{2,1,0:T(8,128)(2,1)} %collective-permute-done.27.refs_1_, ...), custom_call_target="tpu_custom_call" | custom-call | flops 1610612736 | bytes 10485760 | tf_op jit(solution)/shard_map/pallas_call | solution.py:272
  78.9 1.5 collective-permute-start.28
  81.4 7.8 %shard_map.115 = (f32[2048,768]{1,0:T(8,128)S(1)}, f32[384,2048]{1,0:T(8,128)S(1)}, f32[2048,768]{1,0:T(8,128)S(1)}, f32[384,2048]{1,0:T(8,128)S(1)}) custom-call(bf16[512,2048]{1,0:T(8,128)(2,1)S(1)} %get-tuple-element.39.rows_ref, bf16[512,2048]{1,0:T(8,128)(2,1)S(1)} %get-tuple-element.41.cot_ref, ...), custom_call_target="tpu_custom_call" | custom-call | flops 4831838208 | bytes 23068672 | tf_op jit(solution)/shard_map/pallas_call | solution.py:394
  89.3 9.0 %shard_map.112 = (bf16[2,128,1024]{2,1,0:T(8,128)(2,1)S(1)}, bf16[2,128,1024]{2,1,0:T(8,128)(2,1)S(1)}, bf16[2,128,1024]{2,1,0:T(8,128)(2,1)S(1)}, bf16[2,128,10...) custom-call(s32[4]{0:T(128)S(1)} %pad_add_fusion.where_ref, ...), custom_call_target="tpu_custom_call" | custom-call | flops 4831838208 | bytes 6291456 | tf_op jit(solution)/shard_map/pallas_call | solution.py:213
  98.3 10.6 %collective-permute-done.28.refs_0_ = bf16[2,128,1024]{2,1,0:T(8,128)(2,1)S(1)} collective-permute-done((bf16[2,128,1024]{2,1,0:T(8,128)(2,1)}, bf16[2,128,1024]{2,1,0:T(8,128)(2,1)S(1)}, u32[]{:S(2)}, u32[]{:S(2)}) %collective-permute-start.28) | collective-permute-done | bytes 524320 | tf_op jit(solution)/shard_map/ppermute | solution.py:414
  108.9 8.8 %collective-permute-done.31.refs_2_ = bf16[2,128,1024]{2,1,0:T(8,128)(2,1)S(1)} collective-permute-done((bf16[2,128,1024]{2,1,0:T(8,128)(2,1)}, bf16[2,128,1024]{2,1,0:T(8,128)(2,1)S(1)}, u32[]{:S(2)}, u32[]{:S(2)}) %collective-permute-start.31) | collective-permute-done | bytes 524320 | tf_op jit(solution)/shard_map/ppermute | solution.py:414
  117.7 4.4 %shard_map.113 = (bf16[512,2048]{1,0:T(8,128)(2,1)S(1)}, bf16[2,512,384]{2,1,0:T(8,128)(2,1)S(1)}, bf16[2,512,768]{2,1,0:T(8,128)(2,1)S(1)}) custom-call(s32[4]{0:T(128)S(1)} %pad_add_fusion.where_ref, bf16[2,128,1024]{2,1,0:T(8,128)(2,1)S(1)} %collective-permute-done.28.refs_0_, bf16[2,128,1024]{2,1,0:T(8,128)(2,1)S(1)} %collective-permute-done.29.refs_1_, ...), custom_call_target="tpu_custom_call" | custom-call | flops 1610612736 | bytes 10485760 | tf_op jit(solution)/shard_map/pallas_call | solution.py:272
  122.2 2.7 %shard_map.116 = bf16[2048,768]{1,0:T(8,128)(2,1)S(1)} custom-call(bf16[512,2048]{1,0:T(8,128)(2,1)S(1)} %get-tuple-element.36.left_ref, bf16[2,512,768]{2,1,0:T(8,128)(2,1)S(1)} %get-tuple-element.38.right_ref, f32[2048,768]{1,0:T(8,128)S(1)} %get-tuple-element.45.refs_0_), custom_call_target="tpu_custom_call" | custom-call | flops 1610612736 | bytes 5242880 | tf_op jit(solution)/shard_map/pallas_call | solution.py:315
  126.0 1.1 collective-permute-start.9
  128.0 6.2 %collective-permute-done.21 = bf16[2,128,1024]{2,1,0:T(8,128)(2,1)S(1)} collective-permute-done((bf16[2,128,1024]{2,1,0:T(8,128)(2,1)S(1)}, bf16[2,128,1024]{2,1,0:T(8,128)(2,1)S(1)}, u32[]{:S(2)}, u32[]{:S(2)}) %collective-permute-start.21) | collective-permute-done | bytes 524320 | tf_op jit(solution)/shard_map/ppermute | solution.py:414
  134.4 1.2 collective-permute-start.22
  135.6 1.1 collective-permute-start.11
  136.7 6.4 %collective-permute-done.9 = bf16[2,128,1024]{2,1,0:T(8,128)(2,1)S(1)} collective-permute-done((bf16[2,128,1024]{2,1,0:T(8,128)(2,1)S(1)}, bf16[2,128,1024]{2,1,0:T(8,128)(2,1)S(1)}, u32[]{:S(2)}, u32[]{:S(2)}) %collective-permute-start.9) | collective-permute-done | bytes 524320 | tf_op jit(solution)/shard_map/ppermute | solution.py:414
  143.2 1.2 collective-permute-start.10
  144.4 2.1 %shard_map.118 = bf16[384,2048]{1,0:T(8,128)(2,1)S(1)} custom-call(bf16[2,512,384]{2,1,0:T(8,128)(2,1)S(1)} %get-tuple-element.48.left_ref, bf16[512,2048]{1,0:T(8,128)(2,1)S(1)} %get-tuple-element.49.right_ref, f32[384,2048]{1,0:T(8,128)S(1)} %get-tuple-element.51.refs_0_), custom_call_target="tpu_custom_call" | custom-call | flops 805306368 | bytes 3670016 | tf_op jit(solution)/shard_map/pallas_call | solution.py:337
  146.5 7.8 %collective-permute-done.23 = bf16[2,128,1024]{2,1,0:T(8,128)(2,1)S(1)} collective-permute-done((bf16[2,128,1024]{2,1,0:T(8,128)(2,1)S(1)}, bf16[2,128,1024]{2,1,0:T(8,128)(2,1)S(1)}, u32[]{:S(2)}, u32[]{:S(2)}) %collective-permute-start.23) | collective-permute-done | bytes 524320 | tf_op jit(solution)/shard_map/ppermute | solution.py:414
  154.6 2.1 %collective-permute-start.24 = (bf16[128,1024]{1,0:T(8,128)(2,1)S(1)}, bf16[128,1024]{1,0:T(8,128)(2,1)S(1)}, u32[]{:S(2)}, u32[]{:S(2)}) collective-permute-start(bf16[128,1024]{1,0:T(8,128)(2,1)S(1)} %get-tuple-element.52), channel_id=1, source_target_pairs={{0,8},{1,9},{2,10},{3,11},{4,12},{5,13},{6,14},{7,15},{8,0},{9,1},... | collective-permute-start | bytes 786440 | tf_op jit(solution)/shard_map/ppermute | solution.py:414
  156.6 5.7 %collective-permute-done.11 = bf16[2,128,1024]{2,1,0:T(8,128)(2,1)S(1)} collective-permute-done((bf16[2,128,1024]{2,1,0:T(8,128)(2,1)S(1)}, bf16[2,128,1024]{2,1,0:T(8,128)(2,1)S(1)}, u32[]{:S(2)}, u32[]{:S(2)}) %collective-permute-start.11) | collective-permute-done | bytes 524320 | tf_op jit(solution)/shard_map/ppermute | solution.py:414
  162.3 1.1 collective-permute-start.25
  163.8 2.7 %collective-permute-start.12 = (bf16[128,1024]{1,0:T(8,128)(2,1)S(1)}, bf16[128,1024]{1,0:T(8,128)(2,1)S(1)}, u32[]{:S(2)}, u32[]{:S(2)}) collective-permute-start(bf16[128,1024]{1,0:T(8,128)(2,1)S(1)} %fusion.4), channel_id=1, source_target_pairs={{0,12},{1,13},{2,14},{3,15},{4,0},{5,1},{6,2},{7,3},{8,4},{9,5},{1... | collective-permute-start | bytes 786440 | tf_op jit(solution)/shard_map/ppermute | solution.py:414
  166.5 9.5 %collective-permute-done.24 = bf16[128,1024]{1,0:T(8,128)(2,1)S(1)} collective-permute-done((bf16[128,1024]{1,0:T(8,128)(2,1)S(1)}, bf16[128,1024]{1,0:T(8,128)(2,1)S(1)}, u32[]{:S(2)}, u32[]{:S(2)}) %collective-permute-start.24) | collective-permute-done | bytes 262176 | tf_op jit(solution)/shard_map/ppermute | solution.py:414
  176.0 5.1 %collective-permute-done.12 = bf16[128,1024]{1,0:T(8,128)(2,1)S(1)} collective-permute-done((bf16[128,1024]{1,0:T(8,128)(2,1)S(1)}, bf16[128,1024]{1,0:T(8,128)(2,1)S(1)}, u32[]{:S(2)}, u32[]{:S(2)}) %collective-permute-start.12) | collective-permute-done | bytes 262176 | tf_op jit(solution)/shard_map/ppermute | solution.py:414
  182.0 3.1 %shard_map.119 = bf16[384,2048]{1,0:T(8,128)(2,1)} custom-call(bf16[2,512,384]{2,1,0:T(8,128)(2,1)S(1)} %get-tuple-element.48.left_ref, bf16[512,2048]{1,0:T(8,128)(2,1)S(1)} %get-tuple-element.49.right_ref, f32[384,2048]{1,0:T(8,128)S(1)} %get-tuple-element.50.refs_0_, bf16[384,2048]{1,0:T(8,128)(2,1)S(1)} %collective-permute-done.35.refs_1_), custom_call_target="tpu_custom_call" | custom-call | flops 805306368 | bytes 3670016 | tf_op jit(solution)/shard_map/pallas_call | solution.py:337
  185.1 3.8 %shard_map.117 = (bf16[2048,384]{1,0:T(8,128)(2,1)}, bf16[2048,384]{1,0:T(8,128)(2,1)}) custom-call(bf16[512,2048]{1,0:T(8,128)(2,1)S(1)} %get-tuple-element.36.left_ref, bf16[2,512,768]{2,1,0:T(8,128)(2,1)S(1)} %get-tuple-element.38.right_ref, f32[2048,768]{1,0:T(8,128)S(1)} %get-tuple-element.44.refs_0_, bf16[2048,768]{1,0:T(8,128)(2,1)S(1)} %collective-permute-done.34.refs_1_), custom_call_target="tpu_custom_call" | custom-call | flops 1610612736 | bytes 5242880 | tf_op jit(solution)/shard_map/pallas_call | solution.py:315
  (82 shorter events, 16.0 us)
Async XLA Ops:
  0.6 4.4 %copy-start = (bf16[1,384,2048]{2,1,0:T(8,128)(2,1)S(1)}, bf16[1,384,2048]{2,1,0:T(8,128)(2,1)}, u32[]{:S(2)}) copy-start(bf16[1,384,2048]{2,1,0:T(8,128)(2,1)} %param.15) | copy-start | bytes 4718596
  0.6 4.4 %copy-start.5 = (bf16[128,1024]{1,0:T(8,128)(2,1)S(1)}, bf16[128,1024]{1,0:T(8,128)(2,1)}, u32[]{:S(2)}) copy-start(bf16[128,1024]{1,0:T(8,128)(2,1)} %param.8) | copy-start | bytes 786436
  0.7 19.1 %copy-start.12 = (f32[128,8]{0,1:T(8,128)S(1)}, f32[128,8]{0,1:T(8,128)}, u32[]{:S(2)}) copy-start(f32[128,8]{0,1:T(8,128)} %param.11) | copy-start | bytes 12292
  0.7 46.0 %copy-start.13 = (s32[128,8]{0,1:T(8,128)S(1)}, s32[128,8]{0,1:T(8,128)}, u32[]{:S(2)}) copy-start(s32[128,8]{0,1:T(8,128)} %param.10) | copy-start | bytes 12292
  0.7 46.0 %copy-start.14 = (s32[16]{0:T(128)S(1)}, s32[16]{0:T(128)}, u32[]{:S(2)}) copy-start(s32[16]{0:T(128)} %param.12) | copy-start | bytes 196
  4.6 52.3 %collective-permute-start.7 = (bf16[2048,768]{1,0:T(8,128)(2,1)}, bf16[2048,768]{1,0:T(8,128)(2,1)}, u32[]{:S(2)}, u32[]{:S(2)}) collective-permute-start(bf16[2048,768]{1,0:T(8,128)(2,1)} %pad_maximum_fusion.refs_9_), channel_id=1, source_target_pairs={{0,1},{1,0},{2,3},{3,2},{4,5},{5,4},{6,7},{7,6},{8,9},{9,8},{10,11... | collective-permute-start | bytes 9437192 | tf_op jit(solution)/shard_map/ppermute | solution.py:414
  5.1 50.7 %collective-permute-start.8 = (bf16[384,2048]{1,0:T(8,128)(2,1)S(1)}, bf16[384,2048]{1,0:T(8,128)(2,1)S(1)}, u32[]{:S(2)}, u32[]{:S(2)}) collective-permute-start(bf16[384,2048]{1,0:T(8,128)(2,1)S(1)} %bitcast.34), channel_id=1, source_target_pairs={{0,1},{1,0},{2,3},{3,2},{4,5},{5,4},{6,7},{7,6},{8,9},{9,8},{10,11... | collective-permute-start | bytes 4718600 | tf_op jit(solution)/shard_map/ppermute | solution.py:414
  5.1 9.4 %collective-permute-start.1 = (bf16[1,128,1024]{2,1,0:T(8,128)(2,1)S(1)}, bf16[1,128,1024]{2,1,0:T(8,128)(2,1)S(1)}, u32[]{:S(2)}, u32[]{:S(2)}) collective-permute-start(bf16[1,128,1024]{2,1,0:T(8,128)(2,1)S(1)} %bitcast.43), channel_id=1, source_target_pairs={{0,16},{1,3},{2,18},{3,1},{4,20},{5,7},{6,22},{7,5},{8,24},{9,11},... | collective-permute-start | bytes 786440 | tf_op jit(solution)/shard_map/ppermute | solution.py:414
  8.1 9.0 %collective-permute-start = (bf16[1,128,1024]{2,1,0:T(8,128)(2,1)S(1)}, bf16[1,128,1024]{2,1,0:T(8,128)(2,1)}, u32[]{:S(2)}, u32[]{:S(2)}) collective-permute-start(bf16[1,128,1024]{2,1,0:T(8,128)(2,1)S(1)} %bitcast.44), channel_id=1, source_target_pairs={{0,2},{1,17},{2,0},{3,19},{4,6},{5,21},{6,4},{7,23},{8,10},{9,25},... | collective-permute-start | bytes 786440 | tf_op jit(solution)/shard_map/ppermute | solution.py:414
  9.6 9.7 %collective-permute-start.3 = (bf16[128,1024]{1,0:T(8,128)(2,1)S(1)}, bf16[128,1024]{1,0:T(8,128)(2,1)}, u32[]{:S(2)}, u32[]{:S(2)}) collective-permute-start(bf16[128,1024]{1,0:T(8,128)(2,1)S(1)} %copy-done.5), channel_id=1, source_target_pairs={{0,4},{1,5},{2,6},{3,7},{4,8},{5,9},{6,10},{7,11},{8,12},{9,13},{1... | collective-permute-start | bytes 786440 | tf_op jit(solution)/shard_map/ppermute | solution.py:414
  15.2 9.5 %collective-permute-start.26 = (bf16[128,1024]{1,0:T(8,128)(2,1)}, bf16[128,1024]{1,0:T(8,128)(2,1)}, u32[]{:S(2)}, u32[]{:S(2)}) collective-permute-start(bf16[128,1024]{1,0:T(8,128)(2,1)} %param.9), channel_id=1, source_target_pairs={{0,2},{1,17},{2,0},{3,19},{4,6},{5,21},{6,4},{7,23},{8,10},{9,25},... | collective-permute-start | bytes 786440 | tf_op jit(solution)/shard_map/ppermute | solution.py:414
  17.1 9.8 %collective-permute-start.2 = (bf16[1,128,1024]{2,1,0:T(8,128)(2,1)}, bf16[1,128,1024]{2,1,0:T(8,128)(2,1)}, u32[]{:S(2)}, u32[]{:S(2)}) collective-permute-start(bf16[1,128,1024]{2,1,0:T(8,128)(2,1)} %collective-permute-done.refs_1_), channel_id=1, source_target_pairs={{0,16},{1,3},{2,18},{3,1},{4,20},{5,7},{6,22},{7,5},{8,24},{9,11},... | collective-permute-start | bytes 786440 | tf_op jit(solution)/shard_map/ppermute | solution.py:414
  19.3 11.0 %collective-permute-start.4 = (bf16[1,128,1024]{2,1,0:T(8,128)(2,1)}, bf16[1,128,1024]{2,1,0:T(8,128)(2,1)}, u32[]{:S(2)}, u32[]{:S(2)}) collective-permute-start(bf16[1,128,1024]{2,1,0:T(8,128)(2,1)} %bitcast.5.refs_4_), channel_id=1, source_target_pairs={{0,2},{1,17},{2,0},{3,19},{4,6},{5,21},{6,4},{7,23},{8,10},{9,25},... | collective-permute-start | bytes 786440 | tf_op jit(solution)/shard_map/ppermute | solution.py:414
  24.7 9.7 %collective-permute-start.5 = (bf16[1,128,1024]{2,1,0:T(8,128)(2,1)}, bf16[1,128,1024]{2,1,0:T(8,128)(2,1)S(1)}, u32[]{:S(2)}, u32[]{:S(2)}) collective-permute-start(bf16[1,128,1024]{2,1,0:T(8,128)(2,1)} %bitcast.5.refs_4_), channel_id=1, source_target_pairs={{0,16},{1,3},{2,18},{3,1},{4,20},{5,7},{6,22},{7,5},{8,24},{9,11},... | collective-permute-start | bytes 786440 | tf_op jit(solution)/shard_map/ppermute | solution.py:414
  26.9 10.0 %collective-permute-start.13 = (bf16[128,1024]{1,0:T(8,128)(2,1)}, bf16[128,1024]{1,0:T(8,128)(2,1)}, u32[]{:S(2)}, u32[]{:S(2)}) collective-permute-start(bf16[128,1024]{1,0:T(8,128)(2,1)} %collective-permute-done.3), channel_id=1, source_target_pairs={{0,4},{1,5},{2,6},{3,7},{4,8},{5,9},{6,10},{7,11},{8,12},{9,13},{1... | collective-permute-start | bytes 786440 | tf_op jit(solution)/shard_map/ppermute | solution.py:414
  30.3 9.0 %collective-permute-start.6 = (bf16[1,128,1024]{2,1,0:T(8,128)(2,1)}, bf16[1,128,1024]{2,1,0:T(8,128)(2,1)S(1)}, u32[]{:S(2)}, u32[]{:S(2)}) collective-permute-start(bf16[1,128,1024]{2,1,0:T(8,128)(2,1)} %collective-permute-done.4.refs_5_), channel_id=1, source_target_pairs={{0,16},{1,3},{2,18},{3,1},{4,20},{5,7},{6,22},{7,5},{8,24},{9,11},... | collective-permute-start | bytes 786440 | tf_op jit(solution)/shard_map/ppermute | solution.py:414
  35.1 16.7 %collective-permute-start.27 = (bf16[2,128,1024]{2,1,0:T(8,128)(2,1)}, bf16[2,128,1024]{2,1,0:T(8,128)(2,1)}, u32[]{:S(2)}, u32[]{:S(2)}) collective-permute-start(bf16[2,128,1024]{2,1,0:T(8,128)(2,1)} %pad_maximum_fusion.1.refs_0_), channel_id=1, source_target_pairs={{0,4},{1,5},{2,6},{3,7},{4,8},{5,9},{6,10},{7,11},{8,12},{9,13},{1... | collective-permute-start | bytes 1572872 | tf_op jit(solution)/shard_map/ppermute | solution.py:414
  36.9 8.3 %collective-permute-start.14 = (bf16[1,128,1024]{2,1,0:T(8,128)(2,1)}, bf16[1,128,1024]{2,1,0:T(8,128)(2,1)}, u32[]{:S(2)}, u32[]{:S(2)}) collective-permute-start(bf16[1,128,1024]{2,1,0:T(8,128)(2,1)} %bitcast.13.refs_0_), channel_id=1, source_target_pairs={{0,2},{1,17},{2,0},{3,19},{4,6},{5,21},{6,4},{7,23},{8,10},{9,25},... | collective-permute-start | bytes 786440 | tf_op jit(solution)/shard_map/ppermute | solution.py:414
  40.0 15.1 %collective-permute-start.32 = (bf16[2,128,1024]{2,1,0:T(8,128)(2,1)}, bf16[2,128,1024]{2,1,0:T(8,128)(2,1)}, u32[]{:S(2)}, u32[]{:S(2)}) collective-permute-start(bf16[2,128,1024]{2,1,0:T(8,128)(2,1)} %pad_maximum_fusion.1.refs_0_), channel_id=1, source_target_pairs={{0,16},{1,3},{2,18},{3,1},{4,20},{5,7},{6,22},{7,5},{8,24},{9,11},... | collective-permute-start | bytes 1572872 | tf_op jit(solution)/shard_map/ppermute | solution.py:414
  45.2 8.5 %collective-permute-start.17 = (bf16[128,1024]{1,0:T(8,128)(2,1)}, bf16[128,1024]{1,0:T(8,128)(2,1)}, u32[]{:S(2)}, u32[]{:S(2)}) collective-permute-start(bf16[128,1024]{1,0:T(8,128)(2,1)} %collective-permute-done.13), channel_id=1, source_target_pairs={{0,4},{1,5},{2,6},{3,7},{4,8},{5,9},{6,10},{7,11},{8,12},{9,13},{1... | collective-permute-start | bytes 786440 | tf_op jit(solution)/shard_map/ppermute | solution.py:414
  47.5 10.7 %all-to-all-start = ((f32[16,2,128]{2,1,0:T(2,128)}), f32[16,2,128]{2,1,0:T(2,128)S(1)}, u32[]{:S(2)}, u32[]{:S(2)}) async-start(f32[16,2,128]{2,1,0:T(2,128)} %bitcast.6), calls=%async_computation | async-start | bytes 32768 | tf_op jit(solution)/shard_map/all_to_all | solution.py:460
  51.8 18.2 %collective-permute-start.30 = (bf16[2,128,1024]{2,1,0:T(8,128)(2,1)}, bf16[2,128,1024]{2,1,0:T(8,128)(2,1)}, u32[]{:S(2)}, u32[]{:S(2)}) collective-permute-start(bf16[2,128,1024]{2,1,0:T(8,128)(2,1)} %collective-permute-done.27.refs_1_), channel_id=1, source_target_pairs={{0,16},{1,3},{2,18},{3,1},{4,20},{5,7},{6,22},{7,5},{8,24},{9,11},... | collective-permute-start | bytes 1572872 | tf_op jit(solution)/shard_map/ppermute | solution.py:414
  53.7 24.6 %collective-permute-start.15 = (bf16[1,128,1024]{2,1,0:T(8,128)(2,1)}, bf16[1,128,1024]{2,1,0:T(8,128)(2,1)}, u32[]{:S(2)}, u32[]{:S(2)}) collective-permute-start(bf16[1,128,1024]{2,1,0:T(8,128)(2,1)} %bitcast.13.refs_0_), channel_id=1, source_target_pairs={{0,16},{1,3},{2,18},{3,1},{4,20},{5,7},{6,22},{7,5},{8,24},{9,11},... | collective-permute-start | bytes 786440 | tf_op jit(solution)/shard_map/ppermute | solution.py:414
  55.1 26.3 %collective-permute-start.19 = (bf16[1,128,1024]{2,1,0:T(8,128)(2,1)}, bf16[1,128,1024]{2,1,0:T(8,128)(2,1)}, u32[]{:S(2)}, u32[]{:S(2)}) collective-permute-start(bf16[1,128,1024]{2,1,0:T(8,128)(2,1)} %bitcast.14.refs_4_), channel_id=1, source_target_pairs={{0,16},{1,3},{2,18},{3,1},{4,20},{5,7},{6,22},{7,5},{8,24},{9,11},... | collective-permute-start | bytes 786440 | tf_op jit(solution)/shard_map/ppermute | solution.py:414
  55.7 24.7 %collective-permute-start.18 = (bf16[1,128,1024]{2,1,0:T(8,128)(2,1)}, bf16[1,128,1024]{2,1,0:T(8,128)(2,1)}, u32[]{:S(2)}, u32[]{:S(2)}) collective-permute-start(bf16[1,128,1024]{2,1,0:T(8,128)(2,1)} %bitcast.14.refs_4_), channel_id=1, source_target_pairs={{0,2},{1,17},{2,0},{3,19},{4,6},{5,21},{6,4},{7,23},{8,10},{9,25},... | collective-permute-start | bytes 786440 | tf_op jit(solution)/shard_map/ppermute | solution.py:414
  56.8 22.1 %collective-permute-start.16 = (bf16[1,128,1024]{2,1,0:T(8,128)(2,1)}, bf16[1,128,1024]{2,1,0:T(8,128)(2,1)}, u32[]{:S(2)}, u32[]{:S(2)}) collective-permute-start(bf16[1,128,1024]{2,1,0:T(8,128)(2,1)} %collective-permute-done.14.refs_1_), channel_id=1, source_target_pairs={{0,16},{1,3},{2,18},{3,1},{4,20},{5,7},{6,22},{7,5},{8,24},{9,11},... | collective-permute-start | bytes 786440 | tf_op jit(solution)/shard_map/ppermute | solution.py:414
  58.3 1.0 copy-start.7
  59.2 0.9 copy-start.9
  69.9 8.4 %copy-start.1 = (bf16[2,128,1024]{2,1,0:T(8,128)(2,1)}, bf16[2,128,1024]{2,1,0:T(8,128)(2,1)S(1)}, u32[]{:S(2)}) copy-start(bf16[2,128,1024]{2,1,0:T(8,128)(2,1)S(1)} %get-tuple-element.31) | copy-start | bytes 1572868
  69.9 8.4 %copy-start.3 = (bf16[2,128,1024]{2,1,0:T(8,128)(2,1)}, bf16[2,128,1024]{2,1,0:T(8,128)(2,1)S(1)}, u32[]{:S(2)}) copy-start(bf16[2,128,1024]{2,1,0:T(8,128)(2,1)S(1)} %get-tuple-element.30) | copy-start | bytes 1572868
  70.0 28.4 %collective-permute-start.29 = (bf16[2,128,1024]{2,1,0:T(8,128)(2,1)}, bf16[2,128,1024]{2,1,0:T(8,128)(2,1)S(1)}, u32[]{:S(2)}, u32[]{:S(2)}) collective-permute-start(bf16[2,128,1024]{2,1,0:T(8,128)(2,1)} %pad_maximum_fusion.1.refs_0_), channel_id=1, source_target_pairs={{0,12},{1,13},{2,14},{3,15},{4,0},{5,1},{6,2},{7,3},{8,4},{9,5},{1... | collective-permute-start | bytes 1572872 | tf_op jit(solution)/shard_map/ppermute | solution.py:414
  78.3 20.0 %collective-permute-start.33 = (bf16[2,128,1024]{2,1,0:T(8,128)(2,1)}, bf16[2,128,1024]{2,1,0:T(8,128)(2,1)S(1)}, u32[]{:S(2)}, u32[]{:S(2)}) collective-permute-start(bf16[2,128,1024]{2,1,0:T(8,128)(2,1)} %collective-permute-done.32.refs_2_), channel_id=1, source_target_pairs={{0,12},{1,13},{2,14},{3,15},{4,0},{5,1},{6,2},{7,3},{8,4},{9,5},{1... | collective-permute-start | bytes 1572872 | tf_op jit(solution)/shard_map/ppermute | solution.py:414
  78.9 30.0 %collective-permute-start.28 = (bf16[2,128,1024]{2,1,0:T(8,128)(2,1)}, bf16[2,128,1024]{2,1,0:T(8,128)(2,1)S(1)}, u32[]{:S(2)}, u32[]{:S(2)}) collective-permute-start(bf16[2,128,1024]{2,1,0:T(8,128)(2,1)} %collective-permute-done.27.refs_1_), channel_id=1, source_target_pairs={{0,4},{1,5},{2,6},{3,7},{4,8},{5,9},{6,10},{7,11},{8,12},{9,13},{1... | collective-permute-start | bytes 1572872 | tf_op jit(solution)/shard_map/ppermute | solution.py:414
  80.4 8.9 %collective-permute-start.20 = (bf16[1,128,1024]{2,1,0:T(8,128)(2,1)}, bf16[1,128,1024]{2,1,0:T(8,128)(2,1)S(1)}, u32[]{:S(2)}, u32[]{:S(2)}) collective-permute-start(bf16[1,128,1024]{2,1,0:T(8,128)(2,1)} %collective-permute-done.18.refs_5_), channel_id=1, source_target_pairs={{0,16},{1,3},{2,18},{3,1},{4,20},{5,7},{6,22},{7,5},{8,24},{9,11},... | collective-permute-start | bytes 786440 | tf_op jit(solution)/shard_map/ppermute | solution.py:414
  81.4 36.4 %collective-permute-start.31 = (bf16[2,128,1024]{2,1,0:T(8,128)(2,1)}, bf16[2,128,1024]{2,1,0:T(8,128)(2,1)S(1)}, u32[]{:S(2)}, u32[]{:S(2)}) collective-permute-start(bf16[2,128,1024]{2,1,0:T(8,128)(2,1)} %collective-permute-done.30.refs_3_), channel_id=1, source_target_pairs={{0,4},{1,5},{2,6},{3,7},{4,8},{5,9},{6,10},{7,11},{8,12},{9,13},{1... | collective-permute-start | bytes 1572872 | tf_op jit(solution)/shard_map/ppermute | solution.py:414
  122.2 3.8 %copy-start.4 = (bf16[2,128,1024]{2,1,0:T(8,128)(2,1)S(1)}, bf16[2,128,1024]{2,1,0:T(8,128)(2,1)}, u32[]{:S(2)}) copy-start(bf16[2,128,1024]{2,1,0:T(8,128)(2,1)} %copy-done.3) | copy-start | bytes 1572868
  122.2 13.4 %copy-start.2 = (bf16[2,128,1024]{2,1,0:T(8,128)(2,1)S(1)}, bf16[2,128,1024]{2,1,0:T(8,128)(2,1)}, u32[]{:S(2)}) copy-start(bf16[2,128,1024]{2,1,0:T(8,128)(2,1)} %copy-done.1) | copy-start | bytes 1572868
  124.9 60.2 %collective-permute-start.34 = (bf16[2048,768]{1,0:T(8,128)(2,1)S(1)}, bf16[2048,768]{1,0:T(8,128)(2,1)S(1)}, u32[]{:S(2)}, u32[]{:S(2)}) collective-permute-start(bf16[2048,768]{1,0:T(8,128)(2,1)S(1)} %shard_map.116), channel_id=1, source_target_pairs={{0,1},{1,0},{2,3},{3,2},{4,5},{5,4},{6,7},{7,6},{8,9},{9,8},{10,11... | collective-permute-start | bytes 9437192 | tf_op jit(solution)/shard_map/ppermute | solution.py:414
  125.0 9.2 %collective-permute-start.21 = (bf16[2,128,1024]{2,1,0:T(8,128)(2,1)S(1)}, bf16[2,128,1024]{2,1,0:T(8,128)(2,1)S(1)}, u32[]{:S(2)}, u32[]{:S(2)}) collective-permute-start(bf16[2,128,1024]{2,1,0:T(8,128)(2,1)S(1)} %get-tuple-element.34), channel_id=1, source_target_pairs={{0,16},{1,3},{2,18},{3,1},{4,20},{5,7},{6,22},{7,5},{8,24},{9,11},... | collective-permute-start | bytes 1572872 | tf_op jit(solution)/shard_map/ppermute | solution.py:414
  126.0 17.0 %collective-permute-start.9 = (bf16[2,128,1024]{2,1,0:T(8,128)(2,1)S(1)}, bf16[2,128,1024]{2,1,0:T(8,128)(2,1)S(1)}, u32[]{:S(2)}, u32[]{:S(2)}) collective-permute-start(bf16[2,128,1024]{2,1,0:T(8,128)(2,1)S(1)} %copy-done.4), channel_id=1, source_target_pairs={{0,16},{1,3},{2,18},{3,1},{4,20},{5,7},{6,22},{7,5},{8,24},{9,11},... | collective-permute-start | bytes 1572872 | tf_op jit(solution)/shard_map/ppermute | solution.py:414
  127.1 27.2 %collective-permute-start.23 = (bf16[2,128,1024]{2,1,0:T(8,128)(2,1)S(1)}, bf16[2,128,1024]{2,1,0:T(8,128)(2,1)S(1)}, u32[]{:S(2)}, u32[]{:S(2)}) collective-permute-start(bf16[2,128,1024]{2,1,0:T(8,128)(2,1)S(1)} %get-tuple-element.35), channel_id=1, source_target_pairs={{0,16},{1,3},{2,18},{3,1},{4,20},{5,7},{6,22},{7,5},{8,24},{9,11},... | collective-permute-start | bytes 1572872 | tf_op jit(solution)/shard_map/ppermute | solution.py:414
  134.4 19.8 %collective-permute-start.22 = (bf16[2,128,1024]{2,1,0:T(8,128)(2,1)S(1)}, bf16[2,128,1024]{2,1,0:T(8,128)(2,1)S(1)}, u32[]{:S(2)}, u32[]{:S(2)}) collective-permute-start(bf16[2,128,1024]{2,1,0:T(8,128)(2,1)S(1)} %add_convert_fusion.1), channel_id=1, source_target_pairs={{0,2},{1,17},{2,0},{3,19},{4,6},{5,21},{6,4},{7,23},{8,10},{9,25},... | collective-permute-start | bytes 1572872 | tf_op jit(solution)/shard_map/ppermute | solution.py:414
  135.6 26.7 %collective-permute-start.11 = (bf16[2,128,1024]{2,1,0:T(8,128)(2,1)S(1)}, bf16[2,128,1024]{2,1,0:T(8,128)(2,1)S(1)}, u32[]{:S(2)}, u32[]{:S(2)}) collective-permute-start(bf16[2,128,1024]{2,1,0:T(8,128)(2,1)S(1)} %copy-done.2), channel_id=1, source_target_pairs={{0,16},{1,3},{2,18},{3,1},{4,20},{5,7},{6,22},{7,5},{8,24},{9,11},... | collective-permute-start | bytes 1572872 | tf_op jit(solution)/shard_map/ppermute | solution.py:414
  143.2 20.2 %collective-permute-start.10 = (bf16[2,128,1024]{2,1,0:T(8,128)(2,1)S(1)}, bf16[2,128,1024]{2,1,0:T(8,128)(2,1)S(1)}, u32[]{:S(2)}, u32[]{:S(2)}) collective-permute-start(bf16[2,128,1024]{2,1,0:T(8,128)(2,1)S(1)} %add_convert_fusion.2), channel_id=1, source_target_pairs={{0,2},{1,17},{2,0},{3,19},{4,6},{5,21},{6,4},{7,23},{8,10},{9,25},... | collective-permute-start | bytes 1572872 | tf_op jit(solution)/shard_map/ppermute | solution.py:414
  154.3 27.7 %collective-permute-start.35 = (bf16[384,2048]{1,0:T(8,128)(2,1)S(1)}, bf16[384,2048]{1,0:T(8,128)(2,1)S(1)}, u32[]{:S(2)}, u32[]{:S(2)}) collective-permute-start(bf16[384,2048]{1,0:T(8,128)(2,1)S(1)} %shard_map.118), channel_id=1, source_target_pairs={{0,1},{1,0},{2,3},{3,2},{4,5},{5,4},{6,7},{7,6},{8,9},{9,8},{10,11... | collective-permute-start | bytes 4718600 | tf_op jit(solution)/shard_map/ppermute | solution.py:414
  154.6 21.4 %collective-permute-start.24 = (bf16[128,1024]{1,0:T(8,128)(2,1)S(1)}, bf16[128,1024]{1,0:T(8,128)(2,1)S(1)}, u32[]{:S(2)}, u32[]{:S(2)}) collective-permute-start(bf16[128,1024]{1,0:T(8,128)(2,1)S(1)} %get-tuple-element.52), channel_id=1, source_target_pairs={{0,8},{1,9},{2,10},{3,11},{4,12},{5,13},{6,14},{7,15},{8,0},{9,1},... | collective-permute-start | bytes 786440 | tf_op jit(solution)/shard_map/ppermute | solution.py:414
  162.3 13.7 %collective-permute-start.25 = (bf16[128,1024]{1,0:T(8,128)(2,1)S(1)}, bf16[128,1024]{1,0:T(8,128)(2,1)S(1)}, u32[]{:S(2)}, u32[]{:S(2)}) collective-permute-start(bf16[128,1024]{1,0:T(8,128)(2,1)S(1)} %get-tuple-element.53), channel_id=1, source_target_pairs={{0,4},{1,5},{2,6},{3,7},{4,8},{5,9},{6,10},{7,11},{8,12},{9,13},{1... | collective-permute-start | bytes 786440 | tf_op jit(solution)/shard_map/ppermute | solution.py:414
  163.8 17.4 %collective-permute-start.12 = (bf16[128,1024]{1,0:T(8,128)(2,1)S(1)}, bf16[128,1024]{1,0:T(8,128)(2,1)S(1)}, u32[]{:S(2)}, u32[]{:S(2)}) collective-permute-start(bf16[128,1024]{1,0:T(8,128)(2,1)S(1)} %fusion.4), channel_id=1, source_target_pairs={{0,12},{1,13},{2,14},{3,15},{4,0},{5,1},{6,2},{7,3},{8,4},{9,5},{1... | collective-permute-start | bytes 786440 | tf_op jit(solution)/shard_map/ppermute | solution.py:414
  (4 other events, 3.1 us)

commit v5 on v4

--- a/solution.py
+++ b/solution.py
@@ -245,9 +245,10 @@
     copies[0].start()
     width = pre_ref.shape[1] // 2
     units = width // 2
+    products = dot_columns(c_buf[...], jnp.concatenate([downs[0][...], downs[1][...]], axis=0))
     for slot in range(CORES):
         weights = row_weights(mix_ref, where_ref, backs, depth, slot)
-        hidden_cot = weights * dot_columns(c_buf[...], downs[slot][...])
+        hidden_cot = weights * products[:, slot * units : (slot + 1) * units]
         gate = pre_ref[:, slot * width : slot * width + units]
         up = pre_ref[:, slot * width + units : (slot + 1) * width]
         sigma = jax.nn.sigmoid(gate)
@@ -332,7 +333,7 @@
 def down_grads(slot, cot, hid, add, kind):
     total, features = cot.shape
     units = hid.shape[2]
-    tile = min(TILE, features)
+    tile = min(2 * TILE, features)
     flat = pl.BlockSpec((units, tile), lambda i: (0, i))
     return pl.pallas_call(
         functools.partial(grads_kernel, len(add)),

time: 189 us -> 188 us (level)
  Pallas kernels: 47.1 us -> 45.2 us
where the time goes in v5:
time: 188 us
  waiting for transfers between devices  78.1 us (42%)
  starting transfers between devices  49.9 us (27%)
  Pallas kernels  45.2 us (24%)
  other arithmetic  8.48 us (5%)
  local copies, waits for them, and re-layouts  5.15 us (3%)
    ppermute x36, waiting for transfers between devices, send(): return lax.ppermute(value, AXES, pairs)  77.7 us
    ppermute x36, starting transfers between devices, send(): return lax.ppermute(value, AXES, pairs)  45.7 us
    pallas_call x2, Pallas kernels, forward(): pl.pallas_call(functools.partial(forward_kernel, backs, depth, len(sets))...  17.8 us
    pallas_call x2, Pallas kernels, backward(): pl.pallas_call(functools.partial(backward_kernel, backs, depth), out_shap...  8.89 us
    pallas_call x1, Pallas kernels, joint_grads(): pl.pallas_call(functools.partial(joint_grads_kernel, len(slots), added, s...  7.82 us
    pallas_call x2, Pallas kernels, in_grads(): pl.pallas_call(functools.partial(grads_kernel, len(add)), grid=(features...  6.49 us
    unnamed x30, local copies, waits for them, and re-layouts  5 us
    pallas_call x2, Pallas kernels, down_grads(): pl.pallas_call(functools.partial(grads_kernel, len(add)), grid=(features...  4.26 us
  transfers between devices with their start and end apart: 37, of which 16 were waited for; matrix products, arithmetic and copies ran while one was open for 3% of the time, Pallas kernels for 19%

profile of v5, /device:TPU:0, one launch (start us, length us, event | category | flops | bytes accessed | tf_op | source)
XLA Modules:
  0.0 187.9 jit_solution(12777600486513088387)
XLA Ops:
  0.7 3.9 %pad_maximum_fusion.refs_9_ = bf16[2048,768]{1,0:T(8,128)(2,1)} fusion(bf16[2048,384]{1,0:T(8,128)(2,1)} %bitcast.47, bf16[2048,384]{1,0:T(8,128)(2,1)} %bitcast.48), kind=kLoop, calls=%fused_computation | loop fusion | flops 6291456 | bytes 6291456 | tf_op jit(solution)/shard_map/concatenate | solution.py:423
  5.1 3.0 %collective-permute-start.1 = (bf16[1,128,1024]{2,1,0:T(8,128)(2,1)S(1)}, bf16[1,128,1024]{2,1,0:T(8,128)(2,1)S(1)}, u32[]{:S(2)}, u32[]{:S(2)}) collective-permute-start(bf16[1,128,1024]{2,1,0:T(8,128)(2,1)S(1)} %bitcast.43), channel_id=1, source_target_pairs={{0,16},{1,3},{2,18},{3,1},{4,20},{5,7},{6,22},{7,5},{8,24},{9,11},... | collective-permute-start | bytes 786440 | tf_op jit(solution)/shard_map/ppermute | solution.py:415
  8.1 1.5 collective-permute-start
  9.6 1.6 collective-permute-start.3
  11.1 3.3 %collective-permute-done.1.refs_2_ = bf16[1,128,1024]{2,1,0:T(8,128)(2,1)S(1)} collective-permute-done((bf16[1,128,1024]{2,1,0:T(8,128)(2,1)S(1)}, bf16[1,128,1024]{2,1,0:T(8,128)(2,1)S(1)}, u32[]{:S(2)}, u32[]{:S(2)}) %collective-permute-start.1) | collective-permute-done | bytes 262176 | tf_op jit(solution)/shard_map/ppermute | solution.py:415
  15.2 1.9 %collective-permute-start.26 = (bf16[128,1024]{1,0:T(8,128)(2,1)}, bf16[128,1024]{1,0:T(8,128)(2,1)}, u32[]{:S(2)}, u32[]{:S(2)}) collective-permute-start(bf16[128,1024]{1,0:T(8,128)(2,1)} %param.9), channel_id=1, source_target_pairs={{0,2},{1,17},{2,0},{3,19},{4,6},{5,21},{6,4},{7,23},{8,10},{9,25},... | collective-permute-start | bytes 786440 | tf_op jit(solution)/shard_map/ppermute | solution.py:415
  17.1 1.7 collective-permute-start.2
  19.8 4.9 %collective-permute-done.26 = bf16[128,1024]{1,0:T(8,128)(2,1)} collective-permute-done((bf16[128,1024]{1,0:T(8,128)(2,1)}, bf16[128,1024]{1,0:T(8,128)(2,1)}, u32[]{:S(2)}, u32[]{:S(2)}) %collective-permute-start.26) | collective-permute-done | bytes 262176 | tf_op jit(solution)/shard_map/ppermute | solution.py:415
  24.7 2.2 %collective-permute-start.5 = (bf16[1,128,1024]{2,1,0:T(8,128)(2,1)}, bf16[1,128,1024]{2,1,0:T(8,128)(2,1)S(1)}, u32[]{:S(2)}, u32[]{:S(2)}) collective-permute-start(bf16[1,128,1024]{2,1,0:T(8,128)(2,1)} %bitcast.5.refs_4_), channel_id=1, source_target_pairs={{0,16},{1,3},{2,18},{3,1},{4,20},{5,7},{6,22},{7,5},{8,24},{9,11},... | collective-permute-start | bytes 786440 | tf_op jit(solution)/shard_map/ppermute | solution.py:415
  26.9 1.8 collective-permute-start.13
  28.7 1.6 collective-permute-done.4.refs_5_
  30.3 2.2 %collective-permute-start.6 = (bf16[1,128,1024]{2,1,0:T(8,128)(2,1)}, bf16[1,128,1024]{2,1,0:T(8,128)(2,1)S(1)}, u32[]{:S(2)}, u32[]{:S(2)}) collective-permute-start(bf16[1,128,1024]{2,1,0:T(8,128)(2,1)} %collective-permute-done.4.refs_5_), channel_id=1, source_target_pairs={{0,16},{1,3},{2,18},{3,1},{4,20},{5,7},{6,22},{7,5},{8,24},{9,11},... | collective-permute-start | bytes 786440 | tf_op jit(solution)/shard_map/ppermute | solution.py:415
  32.5 1.9 pad_maximum_fusion.1.refs_0_
  35.1 1.8 collective-permute-start.27
  36.9 2.3 %collective-permute-done.6.refs_7_ = bf16[1,128,1024]{2,1,0:T(8,128)(2,1)S(1)} collective-permute-done((bf16[1,128,1024]{2,1,0:T(8,128)(2,1)}, bf16[1,128,1024]{2,1,0:T(8,128)(2,1)S(1)}, u32[]{:S(2)}, u32[]{:S(2)}) %collective-permute-start.6) | collective-permute-done | bytes 262176 | tf_op jit(solution)/shard_map/ppermute | solution.py:415
  40.0 1.7 collective-permute-start.32
  41.8 3.4 %collective-permute-done.14.refs_1_ = bf16[1,128,1024]{2,1,0:T(8,128)(2,1)} collective-permute-done((bf16[1,128,1024]{2,1,0:T(8,128)(2,1)}, bf16[1,128,1024]{2,1,0:T(8,128)(2,1)}, u32[]{:S(2)}, u32[]{:S(2)}) %collective-permute-start.14) | collective-permute-done | bytes 262176 | tf_op jit(solution)/shard_map/ppermute | solution.py:415
  45.2 1.4 collective-permute-start.17
  47.5 4.2 %all-to-all-start = ((f32[16,2,128]{2,1,0:T(2,128)}), f32[16,2,128]{2,1,0:T(2,128)S(1)}, u32[]{:S(2)}, u32[]{:S(2)}) async-start(f32[16,2,128]{2,1,0:T(2,128)} %bitcast.6), calls=%async_computation | async-start | bytes 32768 | tf_op jit(solution)/shard_map/all_to_all | solution.py:461
  53.7 1.4 collective-permute-start.15
  55.7 1.1 collective-permute-start.18
  56.8 1.1 collective-permute-start.16
  61.1 8.8 %shard_map.111 = (bf16[2,128,1024]{2,1,0:T(8,128)(2,1)S(1)}, bf16[2,128,1024]{2,1,0:T(8,128)(2,1)S(1)}, bf16[2,128,1024]{2,1,0:T(8,128)(2,1)S(1)}, bf16[2,128,10...) custom-call(s32[4]{0:T(128)S(1)} %pad_add_fusion.where_ref, ...), custom_call_target="tpu_custom_call" | custom-call | flops 4831838208 | bytes 6291456 | tf_op jit(solution)/shard_map/pallas_call | solution.py:213
  70.0 2.9 %collective-permute-start.29 = (bf16[2,128,1024]{2,1,0:T(8,128)(2,1)}, bf16[2,128,1024]{2,1,0:T(8,128)(2,1)S(1)}, u32[]{:S(2)}, u32[]{:S(2)}) collective-permute-start(bf16[2,128,1024]{2,1,0:T(8,128)(2,1)} %pad_maximum_fusion.1.refs_0_), channel_id=1, source_target_pairs={{0,12},{1,13},{2,14},{3,15},{4,0},{5,1},{6,2},{7,3},{8,4},{9,5},{1... | collective-permute-start | bytes 1572872 | tf_op jit(solution)/shard_map/ppermute | solution.py:415
  72.9 4.9 %shard_map.114 = (bf16[512,2048]{1,0:T(8,128)(2,1)S(1)}, bf16[2,512,384]{2,1,0:T(8,128)(2,1)S(1)}, bf16[2,512,768]{2,1,0:T(8,128)(2,1)S(1)}) custom-call(s32[4]{0:T(128)S(1)} %pad_add_fusion.where_ref, bf16[2,128,1024]{2,1,0:T(8,128)(2,1)} %pad_maximum_fusion.1.refs_0_, bf16[2,128,1024]{2,1,0:T(8,128)(2,1)} %collective-permute-done.27.refs_1_, ...), custom_call_target="tpu_custom_call" | custom-call | flops 1610612736 | bytes 10485760 | tf_op jit(solution)/shard_map/pallas_call | solution.py:273
  78.5 1.5 collective-permute-start.28
  81.0 7.8 %shard_map.115 = (f32[2048,768]{1,0:T(8,128)S(1)}, f32[384,2048]{1,0:T(8,128)S(1)}, f32[2048,768]{1,0:T(8,128)S(1)}, f32[384,2048]{1,0:T(8,128)S(1)}) custom-call(bf16[512,2048]{1,0:T(8,128)(2,1)S(1)} %get-tuple-element.39.rows_ref, bf16[512,2048]{1,0:T(8,128)(2,1)S(1)} %get-tuple-element.41.cot_ref, ...), custom_call_target="tpu_custom_call" | custom-call | flops 4831838208 | bytes 23068672 | tf_op jit(solution)/shard_map/pallas_call | solution.py:395
  88.8 9.0 %shard_map.112 = (bf16[2,128,1024]{2,1,0:T(8,128)(2,1)S(1)}, bf16[2,128,1024]{2,1,0:T(8,128)(2,1)S(1)}, bf16[2,128,1024]{2,1,0:T(8,128)(2,1)S(1)}, bf16[2,128,10...) custom-call(s32[4]{0:T(128)S(1)} %pad_add_fusion.where_ref, ...), custom_call_target="tpu_custom_call" | custom-call | flops 4831838208 | bytes 6291456 | tf_op jit(solution)/shard_map/pallas_call | solution.py:213
  97.9 11.0 %collective-permute-done.28.refs_0_ = bf16[2,128,1024]{2,1,0:T(8,128)(2,1)S(1)} collective-permute-done((bf16[2,128,1024]{2,1,0:T(8,128)(2,1)}, bf16[2,128,1024]{2,1,0:T(8,128)(2,1)S(1)}, u32[]{:S(2)}, u32[]{:S(2)}) %collective-permute-start.28) | collective-permute-done | bytes 524320 | tf_op jit(solution)/shard_map/ppermute | solution.py:415
  108.9 8.8 %collective-permute-done.31.refs_2_ = bf16[2,128,1024]{2,1,0:T(8,128)(2,1)S(1)} collective-permute-done((bf16[2,128,1024]{2,1,0:T(8,128)(2,1)}, bf16[2,128,1024]{2,1,0:T(8,128)(2,1)S(1)}, u32[]{:S(2)}, u32[]{:S(2)}) %collective-permute-start.31) | collective-permute-done | bytes 524320 | tf_op jit(solution)/shard_map/ppermute | solution.py:415
  117.7 3.9 %shard_map.113 = (bf16[512,2048]{1,0:T(8,128)(2,1)S(1)}, bf16[2,512,384]{2,1,0:T(8,128)(2,1)S(1)}, bf16[2,512,768]{2,1,0:T(8,128)(2,1)S(1)}) custom-call(s32[4]{0:T(128)S(1)} %pad_add_fusion.where_ref, bf16[2,128,1024]{2,1,0:T(8,128)(2,1)S(1)} %collective-permute-done.28.refs_0_, bf16[2,128,1024]{2,1,0:T(8,128)(2,1)S(1)} %collective-permute-done.29.refs_1_, ...), custom_call_target="tpu_custom_call" | custom-call | flops 1610612736 | bytes 10485760 | tf_op jit(solution)/shard_map/pallas_call | solution.py:273
  121.7 2.7 %shard_map.116 = bf16[2048,768]{1,0:T(8,128)(2,1)S(1)} custom-call(bf16[512,2048]{1,0:T(8,128)(2,1)S(1)} %get-tuple-element.36.left_ref, bf16[2,512,768]{2,1,0:T(8,128)(2,1)S(1)} %get-tuple-element.38.right_ref, f32[2048,768]{1,0:T(8,128)S(1)} %get-tuple-element.45.refs_0_), custom_call_target="tpu_custom_call" | custom-call | flops 1610612736 | bytes 5242880 | tf_op jit(solution)/shard_map/pallas_call | solution.py:316
  125.5 1.1 collective-permute-start.9
  127.6 6.2 %collective-permute-done.21 = bf16[2,128,1024]{2,1,0:T(8,128)(2,1)S(1)} collective-permute-done((bf16[2,128,1024]{2,1,0:T(8,128)(2,1)S(1)}, bf16[2,128,1024]{2,1,0:T(8,128)(2,1)S(1)}, u32[]{:S(2)}, u32[]{:S(2)}) %collective-permute-start.21) | collective-permute-done | bytes 524320 | tf_op jit(solution)/shard_map/ppermute | solution.py:415
  134.0 1.2 collective-permute-start.22
  135.1 1.1 collective-permute-start.11
  136.2 6.4 %collective-permute-done.9 = bf16[2,128,1024]{2,1,0:T(8,128)(2,1)S(1)} collective-permute-done((bf16[2,128,1024]{2,1,0:T(8,128)(2,1)S(1)}, bf16[2,128,1024]{2,1,0:T(8,128)(2,1)S(1)}, u32[]{:S(2)}, u32[]{:S(2)}) %collective-permute-start.9) | collective-permute-done | bytes 524320 | tf_op jit(solution)/shard_map/ppermute | solution.py:415
  142.8 1.2 collective-permute-start.10
  143.9 1.7 shard_map.118
  145.6 8.2 %collective-permute-done.23 = bf16[2,128,1024]{2,1,0:T(8,128)(2,1)S(1)} collective-permute-done((bf16[2,128,1024]{2,1,0:T(8,128)(2,1)S(1)}, bf16[2,128,1024]{2,1,0:T(8,128)(2,1)S(1)}, u32[]{:S(2)}, u32[]{:S(2)}) %collective-permute-start.23) | collective-permute-done | bytes 524320 | tf_op jit(solution)/shard_map/ppermute | solution.py:415
  154.1 2.1 %collective-permute-start.24 = (bf16[128,1024]{1,0:T(8,128)(2,1)S(1)}, bf16[128,1024]{1,0:T(8,128)(2,1)S(1)}, u32[]{:S(2)}, u32[]{:S(2)}) collective-permute-start(bf16[128,1024]{1,0:T(8,128)(2,1)S(1)} %get-tuple-element.52), channel_id=1, source_target_pairs={{0,8},{1,9},{2,10},{3,11},{4,12},{5,13},{6,14},{7,15},{8,0},{9,1},... | collective-permute-start | bytes 786440 | tf_op jit(solution)/shard_map/ppermute | solution.py:415
  156.2 5.7 %collective-permute-done.11 = bf16[2,128,1024]{2,1,0:T(8,128)(2,1)S(1)} collective-permute-done((bf16[2,128,1024]{2,1,0:T(8,128)(2,1)S(1)}, bf16[2,128,1024]{2,1,0:T(8,128)(2,1)S(1)}, u32[]{:S(2)}, u32[]{:S(2)}) %collective-permute-start.11) | collective-permute-done | bytes 524320 | tf_op jit(solution)/shard_map/ppermute | solution.py:415
  161.8 1.1 collective-permute-start.25
  163.3 2.7 %collective-permute-start.12 = (bf16[128,1024]{1,0:T(8,128)(2,1)S(1)}, bf16[128,1024]{1,0:T(8,128)(2,1)S(1)}, u32[]{:S(2)}, u32[]{:S(2)}) collective-permute-start(bf16[128,1024]{1,0:T(8,128)(2,1)S(1)} %fusion.4), channel_id=1, source_target_pairs={{0,12},{1,13},{2,14},{3,15},{4,0},{5,1},{6,2},{7,3},{8,4},{9,5},{1... | collective-permute-start | bytes 786440 | tf_op jit(solution)/shard_map/ppermute | solution.py:415
  166.0 9.5 %collective-permute-done.24 = bf16[128,1024]{1,0:T(8,128)(2,1)S(1)} collective-permute-done((bf16[128,1024]{1,0:T(8,128)(2,1)S(1)}, bf16[128,1024]{1,0:T(8,128)(2,1)S(1)}, u32[]{:S(2)}, u32[]{:S(2)}) %collective-permute-start.24) | collective-permute-done | bytes 262176 | tf_op jit(solution)/shard_map/ppermute | solution.py:415
  175.5 5.1 %collective-permute-done.12 = bf16[128,1024]{1,0:T(8,128)(2,1)S(1)} collective-permute-done((bf16[128,1024]{1,0:T(8,128)(2,1)S(1)}, bf16[128,1024]{1,0:T(8,128)(2,1)S(1)}, u32[]{:S(2)}, u32[]{:S(2)}) %collective-permute-start.12) | collective-permute-done | bytes 262176 | tf_op jit(solution)/shard_map/ppermute | solution.py:415
  181.5 2.6 %shard_map.119 = bf16[384,2048]{1,0:T(8,128)(2,1)} custom-call(bf16[2,512,384]{2,1,0:T(8,128)(2,1)S(1)} %get-tuple-element.48.left_ref, bf16[512,2048]{1,0:T(8,128)(2,1)S(1)} %get-tuple-element.49.right_ref, f32[384,2048]{1,0:T(8,128)S(1)} %get-tuple-element.50.refs_0_, bf16[384,2048]{1,0:T(8,128)(2,1)S(1)} %collective-permute-done.35.refs_1_), custom_call_target="tpu_custom_call" | custom-call | flops 805306368 | bytes 3670016 | tf_op jit(solution)/shard_map/pallas_call | solution.py:338
  184.1 3.8 %shard_map.117 = (bf16[2048,384]{1,0:T(8,128)(2,1)}, bf16[2048,384]{1,0:T(8,128)(2,1)}) custom-call(bf16[512,2048]{1,0:T(8,128)(2,1)S(1)} %get-tuple-element.36.left_ref, bf16[2,512,768]{2,1,0:T(8,128)(2,1)S(1)} %get-tuple-element.38.right_ref, f32[2048,768]{1,0:T(8,128)S(1)} %get-tuple-element.44.refs_0_, bf16[2048,768]{1,0:T(8,128)(2,1)S(1)} %collective-permute-done.34.refs_1_), custom_call_target="tpu_custom_call" | custom-call | flops 1610612736 | bytes 5242880 | tf_op jit(solution)/shard_map/pallas_call | solution.py:316
  (82 shorter events, 16.0 us)
Async XLA Ops:
  0.6 4.4 %copy-start = (bf16[1,384,2048]{2,1,0:T(8,128)(2,1)S(1)}, bf16[1,384,2048]{2,1,0:T(8,128)(2,1)}, u32[]{:S(2)}) copy-start(bf16[1,384,2048]{2,1,0:T(8,128)(2,1)} %param.15) | copy-start | bytes 4718596
  0.6 4.4 %copy-start.5 = (bf16[128,1024]{1,0:T(8,128)(2,1)S(1)}, bf16[128,1024]{1,0:T(8,128)(2,1)}, u32[]{:S(2)}) copy-start(bf16[128,1024]{1,0:T(8,128)(2,1)} %param.8) | copy-start | bytes 786436
  0.7 19.1 %copy-start.12 = (f32[128,8]{0,1:T(8,128)S(1)}, f32[128,8]{0,1:T(8,128)}, u32[]{:S(2)}) copy-start(f32[128,8]{0,1:T(8,128)} %param.11) | copy-start | bytes 12292
  0.7 46.0 %copy-start.13 = (s32[128,8]{0,1:T(8,128)S(1)}, s32[128,8]{0,1:T(8,128)}, u32[]{:S(2)}) copy-start(s32[128,8]{0,1:T(8,128)} %param.10) | copy-start | bytes 12292
  0.7 46.0 %copy-start.14 = (s32[16]{0:T(128)S(1)}, s32[16]{0:T(128)}, u32[]{:S(2)}) copy-start(s32[16]{0:T(128)} %param.12) | copy-start | bytes 196
  4.6 52.3 %collective-permute-start.7 = (bf16[2048,768]{1,0:T(8,128)(2,1)}, bf16[2048,768]{1,0:T(8,128)(2,1)}, u32[]{:S(2)}, u32[]{:S(2)}) collective-permute-start(bf16[2048,768]{1,0:T(8,128)(2,1)} %pad_maximum_fusion.refs_9_), channel_id=1, source_target_pairs={{0,1},{1,0},{2,3},{3,2},{4,5},{5,4},{6,7},{7,6},{8,9},{9,8},{10,11... | collective-permute-start | bytes 9437192 | tf_op jit(solution)/shard_map/ppermute | solution.py:415
  5.1 50.7 %collective-permute-start.8 = (bf16[384,2048]{1,0:T(8,128)(2,1)S(1)}, bf16[384,2048]{1,0:T(8,128)(2,1)S(1)}, u32[]{:S(2)}, u32[]{:S(2)}) collective-permute-start(bf16[384,2048]{1,0:T(8,128)(2,1)S(1)} %bitcast.34), channel_id=1, source_target_pairs={{0,1},{1,0},{2,3},{3,2},{4,5},{5,4},{6,7},{7,6},{8,9},{9,8},{10,11... | collective-permute-start | bytes 4718600 | tf_op jit(solution)/shard_map/ppermute | solution.py:415
  5.1 9.4 %collective-permute-start.1 = (bf16[1,128,1024]{2,1,0:T(8,128)(2,1)S(1)}, bf16[1,128,1024]{2,1,0:T(8,128)(2,1)S(1)}, u32[]{:S(2)}, u32[]{:S(2)}) collective-permute-start(bf16[1,128,1024]{2,1,0:T(8,128)(2,1)S(1)} %bitcast.43), channel_id=1, source_target_pairs={{0,16},{1,3},{2,18},{3,1},{4,20},{5,7},{6,22},{7,5},{8,24},{9,11},... | collective-permute-start | bytes 786440 | tf_op jit(solution)/shard_map/ppermute | solution.py:415
  8.1 9.0 %collective-permute-start = (bf16[1,128,1024]{2,1,0:T(8,128)(2,1)S(1)}, bf16[1,128,1024]{2,1,0:T(8,128)(2,1)}, u32[]{:S(2)}, u32[]{:S(2)}) collective-permute-start(bf16[1,128,1024]{2,1,0:T(8,128)(2,1)S(1)} %bitcast.44), channel_id=1, source_target_pairs={{0,2},{1,17},{2,0},{3,19},{4,6},{5,21},{6,4},{7,23},{8,10},{9,25},... | collective-permute-start | bytes 786440 | tf_op jit(solution)/shard_map/ppermute | solution.py:415
  9.6 9.7 %collective-permute-start.3 = (bf16[128,1024]{1,0:T(8,128)(2,1)S(1)}, bf16[128,1024]{1,0:T(8,128)(2,1)}, u32[]{:S(2)}, u32[]{:S(2)}) collective-permute-start(bf16[128,1024]{1,0:T(8,128)(2,1)S(1)} %copy-done.5), channel_id=1, source_target_pairs={{0,4},{1,5},{2,6},{3,7},{4,8},{5,9},{6,10},{7,11},{8,12},{9,13},{1... | collective-permute-start | bytes 786440 | tf_op jit(solution)/shard_map/ppermute | solution.py:415
  15.2 9.5 %collective-permute-start.26 = (bf16[128,1024]{1,0:T(8,128)(2,1)}, bf16[128,1024]{1,0:T(8,128)(2,1)}, u32[]{:S(2)}, u32[]{:S(2)}) collective-permute-start(bf16[128,1024]{1,0:T(8,128)(2,1)} %param.9), channel_id=1, source_target_pairs={{0,2},{1,17},{2,0},{3,19},{4,6},{5,21},{6,4},{7,23},{8,10},{9,25},... | collective-permute-start | bytes 786440 | tf_op jit(solution)/shard_map/ppermute | solution.py:415
  17.1 9.8 %collective-permute-start.2 = (bf16[1,128,1024]{2,1,0:T(8,128)(2,1)}, bf16[1,128,1024]{2,1,0:T(8,128)(2,1)}, u32[]{:S(2)}, u32[]{:S(2)}) collective-permute-start(bf16[1,128,1024]{2,1,0:T(8,128)(2,1)} %collective-permute-done.refs_1_), channel_id=1, source_target_pairs={{0,16},{1,3},{2,18},{3,1},{4,20},{5,7},{6,22},{7,5},{8,24},{9,11},... | collective-permute-start | bytes 786440 | tf_op jit(solution)/shard_map/ppermute | solution.py:415
  19.3 11.0 %collective-permute-start.4 = (bf16[1,128,1024]{2,1,0:T(8,128)(2,1)}, bf16[1,128,1024]{2,1,0:T(8,128)(2,1)}, u32[]{:S(2)}, u32[]{:S(2)}) collective-permute-start(bf16[1,128,1024]{2,1,0:T(8,128)(2,1)} %bitcast.5.refs_4_), channel_id=1, source_target_pairs={{0,2},{1,17},{2,0},{3,19},{4,6},{5,21},{6,4},{7,23},{8,10},{9,25},... | collective-permute-start | bytes 786440 | tf_op jit(solution)/shard_map/ppermute | solution.py:415
  24.7 9.7 %collective-permute-start.5 = (bf16[1,128,1024]{2,1,0:T(8,128)(2,1)}, bf16[1,128,1024]{2,1,0:T(8,128)(2,1)S(1)}, u32[]{:S(2)}, u32[]{:S(2)}) collective-permute-start(bf16[1,128,1024]{2,1,0:T(8,128)(2,1)} %bitcast.5.refs_4_), channel_id=1, source_target_pairs={{0,16},{1,3},{2,18},{3,1},{4,20},{5,7},{6,22},{7,5},{8,24},{9,11},... | collective-permute-start | bytes 786440 | tf_op jit(solution)/shard_map/ppermute | solution.py:415
  26.9 10.0 %collective-permute-start.13 = (bf16[128,1024]{1,0:T(8,128)(2,1)}, bf16[128,1024]{1,0:T(8,128)(2,1)}, u32[]{:S(2)}, u32[]{:S(2)}) collective-permute-start(bf16[128,1024]{1,0:T(8,128)(2,1)} %collective-permute-done.3), channel_id=1, source_target_pairs={{0,4},{1,5},{2,6},{3,7},{4,8},{5,9},{6,10},{7,11},{8,12},{9,13},{1... | collective-permute-start | bytes 786440 | tf_op jit(solution)/shard_map/ppermute | solution.py:415
  30.3 9.0 %collective-permute-start.6 = (bf16[1,128,1024]{2,1,0:T(8,128)(2,1)}, bf16[1,128,1024]{2,1,0:T(8,128)(2,1)S(1)}, u32[]{:S(2)}, u32[]{:S(2)}) collective-permute-start(bf16[1,128,1024]{2,1,0:T(8,128)(2,1)} %collective-permute-done.4.refs_5_), channel_id=1, source_target_pairs={{0,16},{1,3},{2,18},{3,1},{4,20},{5,7},{6,22},{7,5},{8,24},{9,11},... | collective-permute-start | bytes 786440 | tf_op jit(solution)/shard_map/ppermute | solution.py:415
  35.1 16.7 %collective-permute-start.27 = (bf16[2,128,1024]{2,1,0:T(8,128)(2,1)}, bf16[2,128,1024]{2,1,0:T(8,128)(2,1)}, u32[]{:S(2)}, u32[]{:S(2)}) collective-permute-start(bf16[2,128,1024]{2,1,0:T(8,128)(2,1)} %pad_maximum_fusion.1.refs_0_), channel_id=1, source_target_pairs={{0,4},{1,5},{2,6},{3,7},{4,8},{5,9},{6,10},{7,11},{8,12},{9,13},{1... | collective-permute-start | bytes 1572872 | tf_op jit(solution)/shard_map/ppermute | solution.py:415
  36.9 8.3 %collective-permute-start.14 = (bf16[1,128,1024]{2,1,0:T(8,128)(2,1)}, bf16[1,128,1024]{2,1,0:T(8,128)(2,1)}, u32[]{:S(2)}, u32[]{:S(2)}) collective-permute-start(bf16[1,128,1024]{2,1,0:T(8,128)(2,1)} %bitcast.13.refs_0_), channel_id=1, source_target_pairs={{0,2},{1,17},{2,0},{3,19},{4,6},{5,21},{6,4},{7,23},{8,10},{9,25},... | collective-permute-start | bytes 786440 | tf_op jit(solution)/shard_map/ppermute | solution.py:415
  40.0 15.1 %collective-permute-start.32 = (bf16[2,128,1024]{2,1,0:T(8,128)(2,1)}, bf16[2,128,1024]{2,1,0:T(8,128)(2,1)}, u32[]{:S(2)}, u32[]{:S(2)}) collective-permute-start(bf16[2,128,1024]{2,1,0:T(8,128)(2,1)} %pad_maximum_fusion.1.refs_0_), channel_id=1, source_target_pairs={{0,16},{1,3},{2,18},{3,1},{4,20},{5,7},{6,22},{7,5},{8,24},{9,11},... | collective-permute-start | bytes 1572872 | tf_op jit(solution)/shard_map/ppermute | solution.py:415
  45.2 8.5 %collective-permute-start.17 = (bf16[128,1024]{1,0:T(8,128)(2,1)}, bf16[128,1024]{1,0:T(8,128)(2,1)}, u32[]{:S(2)}, u32[]{:S(2)}) collective-permute-start(bf16[128,1024]{1,0:T(8,128)(2,1)} %collective-permute-done.13), channel_id=1, source_target_pairs={{0,4},{1,5},{2,6},{3,7},{4,8},{5,9},{6,10},{7,11},{8,12},{9,13},{1... | collective-permute-start | bytes 786440 | tf_op jit(solution)/shard_map/ppermute | solution.py:415
  47.5 10.7 %all-to-all-start = ((f32[16,2,128]{2,1,0:T(2,128)}), f32[16,2,128]{2,1,0:T(2,128)S(1)}, u32[]{:S(2)}, u32[]{:S(2)}) async-start(f32[16,2,128]{2,1,0:T(2,128)} %bitcast.6), calls=%async_computation | async-start | bytes 32768 | tf_op jit(solution)/shard_map/all_to_all | solution.py:461
  51.8 18.2 %collective-permute-start.30 = (bf16[2,128,1024]{2,1,0:T(8,128)(2,1)}, bf16[2,128,1024]{2,1,0:T(8,128)(2,1)}, u32[]{:S(2)}, u32[]{:S(2)}) collective-permute-start(bf16[2,128,1024]{2,1,0:T(8,128)(2,1)} %collective-permute-done.27.refs_1_), channel_id=1, source_target_pairs={{0,16},{1,3},{2,18},{3,1},{4,20},{5,7},{6,22},{7,5},{8,24},{9,11},... | collective-permute-start | bytes 1572872 | tf_op jit(solution)/shard_map/ppermute | solution.py:415
  53.7 24.2 %collective-permute-start.15 = (bf16[1,128,1024]{2,1,0:T(8,128)(2,1)}, bf16[1,128,1024]{2,1,0:T(8,128)(2,1)}, u32[]{:S(2)}, u32[]{:S(2)}) collective-permute-start(bf16[1,128,1024]{2,1,0:T(8,128)(2,1)} %bitcast.13.refs_0_), channel_id=1, source_target_pairs={{0,16},{1,3},{2,18},{3,1},{4,20},{5,7},{6,22},{7,5},{8,24},{9,11},... | collective-permute-start | bytes 786440 | tf_op jit(solution)/shard_map/ppermute | solution.py:415
  55.1 25.8 %collective-permute-start.19 = (bf16[1,128,1024]{2,1,0:T(8,128)(2,1)}, bf16[1,128,1024]{2,1,0:T(8,128)(2,1)}, u32[]{:S(2)}, u32[]{:S(2)}) collective-permute-start(bf16[1,128,1024]{2,1,0:T(8,128)(2,1)} %bitcast.14.refs_4_), channel_id=1, source_target_pairs={{0,16},{1,3},{2,18},{3,1},{4,20},{5,7},{6,22},{7,5},{8,24},{9,11},... | collective-permute-start | bytes 786440 | tf_op jit(solution)/shard_map/ppermute | solution.py:415
  55.7 24.2 %collective-permute-start.18 = (bf16[1,128,1024]{2,1,0:T(8,128)(2,1)}, bf16[1,128,1024]{2,1,0:T(8,128)(2,1)}, u32[]{:S(2)}, u32[]{:S(2)}) collective-permute-start(bf16[1,128,1024]{2,1,0:T(8,128)(2,1)} %bitcast.14.refs_4_), channel_id=1, source_target_pairs={{0,2},{1,17},{2,0},{3,19},{4,6},{5,21},{6,4},{7,23},{8,10},{9,25},... | collective-permute-start | bytes 786440 | tf_op jit(solution)/shard_map/ppermute | solution.py:415
  56.8 21.7 %collective-permute-start.16 = (bf16[1,128,1024]{2,1,0:T(8,128)(2,1)}, bf16[1,128,1024]{2,1,0:T(8,128)(2,1)}, u32[]{:S(2)}, u32[]{:S(2)}) collective-permute-start(bf16[1,128,1024]{2,1,0:T(8,128)(2,1)} %collective-permute-done.14.refs_1_), channel_id=1, source_target_pairs={{0,16},{1,3},{2,18},{3,1},{4,20},{5,7},{6,22},{7,5},{8,24},{9,11},... | collective-permute-start | bytes 786440 | tf_op jit(solution)/shard_map/ppermute | solution.py:415
  58.3 1.0 copy-start.7
  59.2 0.9 copy-start.9
  69.9 7.9 %copy-start.1 = (bf16[2,128,1024]{2,1,0:T(8,128)(2,1)}, bf16[2,128,1024]{2,1,0:T(8,128)(2,1)S(1)}, u32[]{:S(2)}) copy-start(bf16[2,128,1024]{2,1,0:T(8,128)(2,1)S(1)} %get-tuple-element.31) | copy-start | bytes 1572868
  69.9 7.9 %copy-start.3 = (bf16[2,128,1024]{2,1,0:T(8,128)(2,1)}, bf16[2,128,1024]{2,1,0:T(8,128)(2,1)S(1)}, u32[]{:S(2)}) copy-start(bf16[2,128,1024]{2,1,0:T(8,128)(2,1)S(1)} %get-tuple-element.30) | copy-start | bytes 1572868
  70.0 27.9 %collective-permute-start.29 = (bf16[2,128,1024]{2,1,0:T(8,128)(2,1)}, bf16[2,128,1024]{2,1,0:T(8,128)(2,1)S(1)}, u32[]{:S(2)}, u32[]{:S(2)}) collective-permute-start(bf16[2,128,1024]{2,1,0:T(8,128)(2,1)} %pad_maximum_fusion.1.refs_0_), channel_id=1, source_target_pairs={{0,12},{1,13},{2,14},{3,15},{4,0},{5,1},{6,2},{7,3},{8,4},{9,5},{1... | collective-permute-start | bytes 1572872 | tf_op jit(solution)/shard_map/ppermute | solution.py:415
  77.9 20.0 %collective-permute-start.33 = (bf16[2,128,1024]{2,1,0:T(8,128)(2,1)}, bf16[2,128,1024]{2,1,0:T(8,128)(2,1)S(1)}, u32[]{:S(2)}, u32[]{:S(2)}) collective-permute-start(bf16[2,128,1024]{2,1,0:T(8,128)(2,1)} %collective-permute-done.32.refs_2_), channel_id=1, source_target_pairs={{0,12},{1,13},{2,14},{3,15},{4,0},{5,1},{6,2},{7,3},{8,4},{9,5},{1... | collective-permute-start | bytes 1572872 | tf_op jit(solution)/shard_map/ppermute | solution.py:415
  78.5 30.4 %collective-permute-start.28 = (bf16[2,128,1024]{2,1,0:T(8,128)(2,1)}, bf16[2,128,1024]{2,1,0:T(8,128)(2,1)S(1)}, u32[]{:S(2)}, u32[]{:S(2)}) collective-permute-start(bf16[2,128,1024]{2,1,0:T(8,128)(2,1)} %collective-permute-done.27.refs_1_), channel_id=1, source_target_pairs={{0,4},{1,5},{2,6},{3,7},{4,8},{5,9},{6,10},{7,11},{8,12},{9,13},{1... | collective-permute-start | bytes 1572872 | tf_op jit(solution)/shard_map/ppermute | solution.py:415
  79.9 8.9 %collective-permute-start.20 = (bf16[1,128,1024]{2,1,0:T(8,128)(2,1)}, bf16[1,128,1024]{2,1,0:T(8,128)(2,1)S(1)}, u32[]{:S(2)}, u32[]{:S(2)}) collective-permute-start(bf16[1,128,1024]{2,1,0:T(8,128)(2,1)} %collective-permute-done.18.refs_5_), channel_id=1, source_target_pairs={{0,16},{1,3},{2,18},{3,1},{4,20},{5,7},{6,22},{7,5},{8,24},{9,11},... | collective-permute-start | bytes 786440 | tf_op jit(solution)/shard_map/ppermute | solution.py:415
  80.9 36.8 %collective-permute-start.31 = (bf16[2,128,1024]{2,1,0:T(8,128)(2,1)}, bf16[2,128,1024]{2,1,0:T(8,128)(2,1)S(1)}, u32[]{:S(2)}, u32[]{:S(2)}) collective-permute-start(bf16[2,128,1024]{2,1,0:T(8,128)(2,1)} %collective-permute-done.30.refs_3_), channel_id=1, source_target_pairs={{0,4},{1,5},{2,6},{3,7},{4,8},{5,9},{6,10},{7,11},{8,12},{9,13},{1... | collective-permute-start | bytes 1572872 | tf_op jit(solution)/shard_map/ppermute | solution.py:415
  121.7 3.9 %copy-start.4 = (bf16[2,128,1024]{2,1,0:T(8,128)(2,1)S(1)}, bf16[2,128,1024]{2,1,0:T(8,128)(2,1)}, u32[]{:S(2)}) copy-start(bf16[2,128,1024]{2,1,0:T(8,128)(2,1)} %copy-done.3) | copy-start | bytes 1572868
  121.7 13.4 %copy-start.2 = (bf16[2,128,1024]{2,1,0:T(8,128)(2,1)S(1)}, bf16[2,128,1024]{2,1,0:T(8,128)(2,1)}, u32[]{:S(2)}) copy-start(bf16[2,128,1024]{2,1,0:T(8,128)(2,1)} %copy-done.1) | copy-start | bytes 1572868
  124.4 59.6 %collective-permute-start.34 = (bf16[2048,768]{1,0:T(8,128)(2,1)S(1)}, bf16[2048,768]{1,0:T(8,128)(2,1)S(1)}, u32[]{:S(2)}, u32[]{:S(2)}) collective-permute-start(bf16[2048,768]{1,0:T(8,128)(2,1)S(1)} %shard_map.116), channel_id=1, source_target_pairs={{0,1},{1,0},{2,3},{3,2},{4,5},{5,4},{6,7},{7,6},{8,9},{9,8},{10,11... | collective-permute-start | bytes 9437192 | tf_op jit(solution)/shard_map/ppermute | solution.py:415
  124.5 9.2 %collective-permute-start.21 = (bf16[2,128,1024]{2,1,0:T(8,128)(2,1)S(1)}, bf16[2,128,1024]{2,1,0:T(8,128)(2,1)S(1)}, u32[]{:S(2)}, u32[]{:S(2)}) collective-permute-start(bf16[2,128,1024]{2,1,0:T(8,128)(2,1)S(1)} %get-tuple-element.34), channel_id=1, source_target_pairs={{0,16},{1,3},{2,18},{3,1},{4,20},{5,7},{6,22},{7,5},{8,24},{9,11},... | collective-permute-start | bytes 1572872 | tf_op jit(solution)/shard_map/ppermute | solution.py:415
  125.5 17.0 %collective-permute-start.9 = (bf16[2,128,1024]{2,1,0:T(8,128)(2,1)S(1)}, bf16[2,128,1024]{2,1,0:T(8,128)(2,1)S(1)}, u32[]{:S(2)}, u32[]{:S(2)}) collective-permute-start(bf16[2,128,1024]{2,1,0:T(8,128)(2,1)S(1)} %copy-done.4), channel_id=1, source_target_pairs={{0,16},{1,3},{2,18},{3,1},{4,20},{5,7},{6,22},{7,5},{8,24},{9,11},... | collective-permute-start | bytes 1572872 | tf_op jit(solution)/shard_map/ppermute | solution.py:415
  126.6 27.2 %collective-permute-start.23 = (bf16[2,128,1024]{2,1,0:T(8,128)(2,1)S(1)}, bf16[2,128,1024]{2,1,0:T(8,128)(2,1)S(1)}, u32[]{:S(2)}, u32[]{:S(2)}) collective-permute-start(bf16[2,128,1024]{2,1,0:T(8,128)(2,1)S(1)} %get-tuple-element.35), channel_id=1, source_target_pairs={{0,16},{1,3},{2,18},{3,1},{4,20},{5,7},{6,22},{7,5},{8,24},{9,11},... | collective-permute-start | bytes 1572872 | tf_op jit(solution)/shard_map/ppermute | solution.py:415
  134.0 19.8 %collective-permute-start.22 = (bf16[2,128,1024]{2,1,0:T(8,128)(2,1)S(1)}, bf16[2,128,1024]{2,1,0:T(8,128)(2,1)S(1)}, u32[]{:S(2)}, u32[]{:S(2)}) collective-permute-start(bf16[2,128,1024]{2,1,0:T(8,128)(2,1)S(1)} %add_convert_fusion.1), channel_id=1, source_target_pairs={{0,2},{1,17},{2,0},{3,19},{4,6},{5,21},{6,4},{7,23},{8,10},{9,25},... | collective-permute-start | bytes 1572872 | tf_op jit(solution)/shard_map/ppermute | solution.py:415
  135.1 26.7 %collective-permute-start.11 = (bf16[2,128,1024]{2,1,0:T(8,128)(2,1)S(1)}, bf16[2,128,1024]{2,1,0:T(8,128)(2,1)S(1)}, u32[]{:S(2)}, u32[]{:S(2)}) collective-permute-start(bf16[2,128,1024]{2,1,0:T(8,128)(2,1)S(1)} %copy-done.2), channel_id=1, source_target_pairs={{0,16},{1,3},{2,18},{3,1},{4,20},{5,7},{6,22},{7,5},{8,24},{9,11},... | collective-permute-start | bytes 1572872 | tf_op jit(solution)/shard_map/ppermute | solution.py:415
  142.8 20.2 %collective-permute-start.10 = (bf16[2,128,1024]{2,1,0:T(8,128)(2,1)S(1)}, bf16[2,128,1024]{2,1,0:T(8,128)(2,1)S(1)}, u32[]{:S(2)}, u32[]{:S(2)}) collective-permute-start(bf16[2,128,1024]{2,1,0:T(8,128)(2,1)S(1)} %add_convert_fusion.2), channel_id=1, source_target_pairs={{0,2},{1,17},{2,0},{3,19},{4,6},{5,21},{6,4},{7,23},{8,10},{9,25},... | collective-permute-start | bytes 1572872 | tf_op jit(solution)/shard_map/ppermute | solution.py:415
  153.8 27.7 %collective-permute-start.35 = (bf16[384,2048]{1,0:T(8,128)(2,1)S(1)}, bf16[384,2048]{1,0:T(8,128)(2,1)S(1)}, u32[]{:S(2)}, u32[]{:S(2)}) collective-permute-start(bf16[384,2048]{1,0:T(8,128)(2,1)S(1)} %shard_map.118), channel_id=1, source_target_pairs={{0,1},{1,0},{2,3},{3,2},{4,5},{5,4},{6,7},{7,6},{8,9},{9,8},{10,11... | collective-permute-start | bytes 4718600 | tf_op jit(solution)/shard_map/ppermute | solution.py:415
  154.1 21.4 %collective-permute-start.24 = (bf16[128,1024]{1,0:T(8,128)(2,1)S(1)}, bf16[128,1024]{1,0:T(8,128)(2,1)S(1)}, u32[]{:S(2)}, u32[]{:S(2)}) collective-permute-start(bf16[128,1024]{1,0:T(8,128)(2,1)S(1)} %get-tuple-element.52), channel_id=1, source_target_pairs={{0,8},{1,9},{2,10},{3,11},{4,12},{5,13},{6,14},{7,15},{8,0},{9,1},... | collective-permute-start | bytes 786440 | tf_op jit(solution)/shard_map/ppermute | solution.py:415
  161.8 13.7 %collective-permute-start.25 = (bf16[128,1024]{1,0:T(8,128)(2,1)S(1)}, bf16[128,1024]{1,0:T(8,128)(2,1)S(1)}, u32[]{:S(2)}, u32[]{:S(2)}) collective-permute-start(bf16[128,1024]{1,0:T(8,128)(2,1)S(1)} %get-tuple-element.53), channel_id=1, source_target_pairs={{0,4},{1,5},{2,6},{3,7},{4,8},{5,9},{6,10},{7,11},{8,12},{9,13},{1... | collective-permute-start | bytes 786440 | tf_op jit(solution)/shard_map/ppermute | solution.py:415
  163.3 17.4 %collective-permute-start.12 = (bf16[128,1024]{1,0:T(8,128)(2,1)S(1)}, bf16[128,1024]{1,0:T(8,128)(2,1)S(1)}, u32[]{:S(2)}, u32[]{:S(2)}) collective-permute-start(bf16[128,1024]{1,0:T(8,128)(2,1)S(1)} %fusion.4), channel_id=1, source_target_pairs={{0,12},{1,13},{2,14},{3,15},{4,0},{5,1},{6,2},{7,3},{8,4},{9,5},{1... | collective-permute-start | bytes 786440 | tf_op jit(solution)/shard_map/ppermute | solution.py:415
  (4 other events, 3.1 us)
